TPU v7x, 512 devices: a whole 4x4x16 slice. The times are simulated.
512 devices in a mesh: dp: 64 (over z, x_lo, core), lon: 8 (over y, x_hi).
Axes of the slice: x: 4 (x_hi: 2, x_lo: 2; x = x_hi * 2 + x_lo), y: 4, z: 16, core: 2. Of those that a mesh axis runs over, the one named last changes fastest.
Arguments:
- features: bfloat16 [64, 72, 48, 1152], P('dp', 'lon'), may hold values from -6 to 6
- depth_w: bfloat16 [2, 3, 3, 1152], replicated, may hold values from -2 to 2
- point_w: bfloat16 [2, 1152, 256], replicated, may hold values from -0.1875 to 0.1875
- point_bias: float32 [2, 256], replicated, may hold values from -3 to 3
- cotangent: bfloat16 [64, 72, 48, 512], P('dp', 'lon'), may hold values from -6 to 6
Outputs:
- feature_grad: bfloat16 [64, 72, 48, 1152], P('dp', 'lon')
- depth_grad: bfloat16 [2, 3, 3, 1152], replicated
- point_grad: bfloat16 [2, 1152, 256], replicated
- bias_grad: float32 [2, 256], replicated
All inputs are finite; a program needn't handle non-finite values.
Results may differ from a plain program's by a relative error of at most 0.0075.
Values may be sent and summed in bfloat16 or wider, within the bound.
No kernel may reach another device: no remote copies, remote signals or barrier semaphores. Data moves between devices by JAX's collectives and lax.ppermute only.
A program may use at most 128 MiB of HBM per device.

v0:
```python
import jax
import jax.numpy as jnp
from jax import lax
from jax.sharding import PartitionSpec as P

RATE_A = 24
RATE_B = 36


def from_behind(block, axis, distance):
    devices = range(lax.axis_size(axis))
    route = [((i - distance) % len(devices), i) for i in devices]
    return lax.ppermute(block, axis, route)


def lat_shift(grid_field, offset, axis_pos):
    height = grid_field.shape[axis_pos]
    if offset == 0:
        return grid_field
    widths = [(0, 0)] * grid_field.ndim
    if offset > 0:
        kept_rows = lax.slice_in_dim(grid_field, offset, height, axis=axis_pos)
        widths[axis_pos] = (0, offset)
    else:
        kept_rows = lax.slice_in_dim(grid_field, 0, height + offset, axis=axis_pos)
        widths[axis_pos] = (-offset, 0)
    return jnp.pad(kept_rows, widths)


def gate_slope(pre_act):
    sigmoid_val = jax.nn.sigmoid(pre_act)
    return sigmoid_val * (1.0 + pre_act * (1.0 - sigmoid_val))


def column_plan(dilation, direction, columns, group_size):
    run_list = []
    for column in range(columns):
        target = column + direction * dilation
        offset = target // columns
        local_col = target % columns
        if run_list and run_list[-1][0] == offset:
            run_list[-1][2] = local_col + 1
        else:
            run_list.append([offset, local_col, local_col + 1])
    return [(-entry[0] % group_size, entry[1], entry[2]) for entry in run_list]


def join_pieces(piece_list):
    if len(piece_list) == 1:
        return piece_list[0]
    return jnp.concatenate(piece_list, axis=1)


def fetch_each(grid_field, offset_pairs, group_size, send_fn):
    result = {}
    for offset_pair in offset_pairs:
        piece_list = []
        for shift_by, first_col, finish in column_plan(
            offset_pair[0], offset_pair[1], grid_field.shape[1], group_size
        ):
            column_piece = grid_field[:, first_col:finish]
            column_piece = send_fn(column_piece, shift_by)
            piece_list.append(column_piece)
        result[offset_pair] = join_pieces(piece_list)
    return result


def send_features(column_piece, shift_by):
    return from_behind(column_piece, "lon", shift_by)


def send_grads(column_piece, shift_by):
    return from_behind(column_piece, "lon", shift_by)


def per_device(features, depth_w, point_w, point_bias, cotangent):
    group_size = lax.axis_size("lon")
    channels = features.shape[3]
    outputs = point_w.shape[2]
    dilations = (RATE_A, RATE_B)
    offset_pairs = [(dilation, direction) for dilation in dilations for direction in (-1, 1)]
    moved_in = fetch_each(features, offset_pairs, group_size, send_features)
    depth_outs = []
    for branch, dilation in enumerate(dilations):
        depth_acc = jnp.zeros(features.shape, jnp.float32)
        for lon_step in (-1, 0, 1):
            source = features if lon_step == 0 else moved_in[dilation, lon_step]
            for lat_step in (-1, 0, 1):
                tapped = lat_shift(source, lat_step * dilation, 2).astype(jnp.float32)
                depth_acc = (
                    depth_acc
                    + depth_w[branch, lat_step + 1, lon_step + 1].astype(jnp.float32) * tapped
                )
        depth_outs.append(depth_acc.astype(jnp.bfloat16))
    point_terms = []
    bias_terms = []
    dgrad_list = []
    for branch, dilation in enumerate(dilations):
        flat_depth = depth_outs[branch].reshape(-1, channels)
        point_act = (
            jnp.dot(flat_depth, point_w[branch], preferred_element_type=jnp.float32)
            + point_bias[branch]
        )
        upstream_part = (
            cotangent[..., branch * outputs : (branch + 1) * outputs]
            .reshape(-1, outputs)
            .astype(jnp.float32)
        )
        pgrad = (upstream_part * gate_slope(point_act)).astype(jnp.bfloat16)
        bias_terms.append(jnp.sum(pgrad.astype(jnp.float32), axis=0))
        point_terms.append(
            lax.dot_general(
                flat_depth, pgrad, (((0,), (0,)), ((), ())), preferred_element_type=jnp.float32
            )
        )
        dgrad = lax.dot_general(
            pgrad, point_w[branch], (((1,), (1,)), ((), ())), preferred_element_type=jnp.float32
        )
        dgrad_list.append(dgrad.astype(jnp.bfloat16).reshape(features.shape))
    point_local = jnp.stack(point_terms)
    bias_local = jnp.stack(bias_terms)
    grad_field = jnp.zeros(features.shape, jnp.float32)
    depth_terms = []
    for branch, dilation in enumerate(dilations):
        branch_pairs = [(dilation, -1), (dilation, 1)]
        moved_back = fetch_each(dgrad_list[branch], branch_pairs, group_size, send_grads)
        dgrad_wide = dgrad_list[branch].astype(jnp.float32)
        tap_rows = []
        for lat_step in (-1, 0, 1):
            tap_cols = []
            for lon_step in (-1, 0, 1):
                source = features if lon_step == 0 else moved_in[dilation, lon_step]
                tapped = lat_shift(source, lat_step * dilation, 2).astype(jnp.float32)
                tap_cols.append(jnp.sum(tapped * dgrad_wide, axis=(0, 1, 2)))
                behind = dgrad_list[branch] if lon_step == 0 else moved_back[dilation, -lon_step]
                behind = lat_shift(behind, -lat_step * dilation, 2).astype(jnp.float32)
                grad_field = (
                    grad_field
                    + depth_w[branch, lat_step + 1, lon_step + 1].astype(jnp.float32) * behind
                )
            tap_rows.append(jnp.stack(tap_cols))
        depth_terms.append(jnp.stack(tap_rows))
    depth_local = jnp.stack(depth_terms)
    feature_grad = grad_field.astype(jnp.bfloat16)
    point_sum, depth_sum, bias_sum = lax.psum((point_local, depth_local, bias_local), ("dp", "lon"))
    images = lax.axis_size("dp") * features.shape[0]
    depth_grad = (depth_sum / images).astype(jnp.bfloat16)
    point_grad = (point_sum / images).astype(jnp.bfloat16)
    bias_grad = bias_sum / images
    return (feature_grad, depth_grad, point_grad, bias_grad)


def solution(mesh):
    placed = (P("dp", "lon", None, None), P(), P(), P(), P("dp", "lon", None, None))
    return jax.shard_map(
        per_device,
        mesh=mesh,
        in_specs=placed,
        out_specs=(P("dp", "lon", None, None), P(), P(), P()),
        check_vma=False,
    )
```

profile of v0, /device:TPU:1, one launch (start us, length us, event | category | flops | bytes accessed | tf_op | source)
XLA Modules:
  0.0 733.2 jit_solution(12406998658973591604)
XLA Ops:
  7.2 0.0 all-reduce.23.cloned.1.call-start
  7.2 5.8 collective-permute-start.8
  13.0 1.4 fusion.71
  14.4 4.8 collective-permute-start
  19.2 0.1 fusion.70
  19.3 0.0 copy-start.29
  19.3 0.0 copy-start.5
  19.3 0.0 copy-start.3
  19.3 2.1 collective-permute-start.1
  21.3 5.4 collective-permute-start.3
  26.8 3.0 collective-permute-start.2
  29.8 0.1 fusion.72
  29.8 0.1 fusion.75
  30.0 0.2 convert_reduce_fusion.19
  30.3 0.0 copy-start.7
  30.3 42.3 %collective-permute-done.2 = bf16[1,3,48,1152]{3,2,1,0:T(8,128)(2,1)S(1)} collective-permute-done((bf16[1,3,48,1152]{3,2,1,0:T(8,128)(2,1)S(1)}, bf16[1,3,48,1152]{3,2,1,0:T(8,128)(2,1)S(1)}, u32[]{:S(2)}, u32[]{:S(2)}) %collective-permute-start.2) | collective-permute-done | bytes 331808 | tf_op jit(solution)/shard_map/ppermute | solution.py:13
  72.6 0.0 collective-permute-done
  72.6 0.1 constant_dynamic-update-slice_fusion.1
  72.7 0.0 collective-permute-done.1
  72.8 0.1 fusion.69
  72.8 0.0 collective-permute-done.3
  72.9 0.1 constant_dynamic-update-slice_fusion.2
  72.9 0.1 fusion.73
  73.1 0.0 copy-start.4
  73.1 1.5 fusion.8
  74.6 0.6 convert_reduce_fusion.1
  75.2 0.7 fusion.26
  75.9 1.2 fusion.67
  77.0 0.8 fusion.68
  77.9 3.3 collective-permute-start.4
  81.2 0.9 fusion.63
  82.1 0.6 stack.122
  82.7 0.6 stack.124
  83.3 4.4 collective-permute-start.5
  87.7 3.3 collective-permute-start.6
  91.0 2.0 collective-permute-start.7
  93.0 1.5 convolution_bitcast_fusion.1
  94.5 0.0 collective-permute-done.4
  94.5 0.8 constant_dynamic-update-slice_fusion.5
  95.3 0.1 fusion.74
  95.4 1.4 fusion.15
  96.7 0.6 convert_reduce_fusion
  97.3 1.6 convolution_bitcast_fusion
  98.9 0.5 convolution_convert_fusion
  99.3 4.3 collective-permute-start.9
  103.6 2.3 fusion.41
  106.1 139.6 %psum.23 = f32[2,256]{1,0:T(2,128)S(1)} all-reduce(f32[2,256]{1,0:T(2,128)S(1)} %pad_maximum_fusion.2), channel_id=1, replica_groups=mesh['dp'=64,'lon'=8] {'dp','lon'}, use_global_device_ids=true, to_apply=%region_19.20 | all-reduce | flops 512 | bytes 4096 | tf_op jit(solution)/shard_map/psum | solution.py:145
  245.7 3.2 pad_maximum_fusion
  249.1 0.7 pad_maximum_fusion.1
  249.8 0.0 all-reduce.23.cloned.1.call-update
  249.8 0.6 broadcast_multiply_fusion
  250.4 0.1 fusion.66
  250.5 1.1 constant_dynamic-update-slice_fusion.7
  251.6 0.0 collective-permute-done.5
  251.6 1.2 constant_dynamic-update-slice_fusion.4
  252.8 1.0 constant_dynamic-update-slice_fusion.6
  253.8 0.1 fusion.62
  253.9 0.0 copy-start.8
  254.0 0.1 fusion.64
  254.1 1.2 fusion.65
  255.5 5.0 fusion.25
  260.5 462.3 %all-reduce.23.cloned.1.call-done = (f32[2,3,3,1152]{3,2,1,0:T(4,128)}, f32[2,1152,256]{2,1,0:T(8,128)}) async-done(((f32[2,3,3,1152]{3,2,1,0:T(4,128)}, f32[2,1152,256]{2,1,0:T(8,128)}), (f32[2,3,3,1152]{3,2,1,0:T(4,128)}, f32[2,1152,256]{2,1,0:T(8,128)})) %all-reduce.23.cloned.1.call-update) | async-done | bytes 2442256 | tf_op jit(solution)/shard_map/psum | solution.py:145
  722.7 2.9 multiply_convert_fusion
  725.7 0.7 copy.9
  (83 shorter events, 0.5 us)
Async XLA Ops:
  7.2 12.0 %copy-start = (bf16[1,9,48,1152]{3,2,1,0:T(8,128)(2,1)S(1)}, bf16[1,9,48,1152]{3,2,1,0:T(8,128)(2,1)}, u32[]{:S(2)}) copy-start(bf16[1,9,48,1152]{3,2,1,0:T(8,128)(2,1)} %param.5) | copy-start | bytes 2985988
  7.2 715.6 %all-reduce.23.cloned.1.call-start = ((), (), s32[]{:S(2)}) async-start(), calls=%async_computation | async-start | bytes 4939776 | tf_op jit(solution)/shard_map/psum | solution.py:145
  7.2 88.0 %collective-permute-start.8 = (bf16[1,9,48,1152]{3,2,1,0:T(8,128)(2,1)}, bf16[1,9,48,1152]{3,2,1,0:T(8,128)(2,1)S(1)}, u32[]{:S(2)}, u32[]{:S(2)}) collective-permute-start(bf16[1,9,48,1152]{3,2,1,0:T(8,128)(2,1)} %param.5), channel_id=1, source_target_pairs={{4,0},{5,1},{6,2},{7,3},{0,4},{1,5},{2,6},{3,7},{12,8},{13,9},{14,... | collective-permute-start | bytes 2985992 | tf_op jit(solution)/shard_map/ppermute | solution.py:13
  14.4 58.2 %collective-permute-start = (bf16[1,6,48,1152]{3,2,1,0:T(8,128)(2,1)S(1)}, bf16[1,6,48,1152]{3,2,1,0:T(8,128)(2,1)S(1)}, u32[]{:S(2)}, u32[]{:S(2)}) collective-permute-start(bf16[1,6,48,1152]{3,2,1,0:T(8,128)(2,1)S(1)} %get-tuple-element.61), channel_id=1, source_target_pairs={{5,0},{6,1},{7,2},{0,3},{1,4},{2,5},{3,6},{4,7},{13,8},{14,9},{15,... | collective-permute-start | bytes 1990664 | tf_op jit(solution)/shard_map/ppermute | solution.py:13
  19.3 10.7 %copy-start.29 = (f32[2,256]{1,0:T(2,128)S(1)}, f32[2,256]{1,0:T(2,128)}, u32[]{:S(2)}) copy-start(f32[2,256]{1,0:T(2,128)} %param.8) | copy-start | bytes 6148
  19.3 10.7 %copy-start.5 = (bf16[2,3,3,1152]{3,0,2,1:T(2,128)(2,1)S(1)}, bf16[2,3,3,1152]{3,0,2,1:T(2,128)(2,1)}, u32[]{:S(2)}) copy-start(bf16[2,3,3,1152]{3,0,2,1:T(2,128)(2,1)} %param.6) | copy-start | bytes 124420
  19.3 10.9 %copy-start.3 = (bf16[1,9,48,512]{3,2,1,0:T(8,128)(2,1)S(1)}, bf16[1,9,48,512]{3,2,1,0:T(8,128)(2,1)}, u32[]{:S(2)}) copy-start(bf16[1,9,48,512]{3,2,1,0:T(8,128)(2,1)} %param.9) | copy-start | bytes 1327108
  19.3 53.4 %collective-permute-start.1 = (bf16[1,3,48,1152]{3,2,1,0:T(8,128)(2,1)S(1)}, bf16[1,3,48,1152]{3,2,1,0:T(8,128)(2,1)S(1)}, u32[]{:S(2)}, u32[]{:S(2)}) collective-permute-start(bf16[1,3,48,1152]{3,2,1,0:T(8,128)(2,1)S(1)} %get-tuple-element.59), channel_id=1, source_target_pairs={{6,0},{7,1},{0,2},{1,3},{2,4},{3,5},{4,6},{5,7},{14,8},{15,9},{8,1... | collective-permute-start | bytes 995336 | tf_op jit(solution)/shard_map/ppermute | solution.py:13
  21.3 51.5 %collective-permute-start.3 = (bf16[1,6,48,1152]{3,2,1,0:T(8,128)(2,1)S(1)}, bf16[1,6,48,1152]{3,2,1,0:T(8,128)(2,1)S(1)}, u32[]{:S(2)}, u32[]{:S(2)}) collective-permute-start(bf16[1,6,48,1152]{3,2,1,0:T(8,128)(2,1)S(1)} %get-tuple-element.62), channel_id=1, source_target_pairs={{3,0},{4,1},{5,2},{6,3},{7,4},{0,5},{1,6},{2,7},{11,8},{12,9},{13,... | collective-permute-start | bytes 1990664 | tf_op jit(solution)/shard_map/ppermute | solution.py:13
  26.8 45.8 %collective-permute-start.2 = (bf16[1,3,48,1152]{3,2,1,0:T(8,128)(2,1)S(1)}, bf16[1,3,48,1152]{3,2,1,0:T(8,128)(2,1)S(1)}, u32[]{:S(2)}, u32[]{:S(2)}) collective-permute-start(bf16[1,3,48,1152]{3,2,1,0:T(8,128)(2,1)S(1)} %get-tuple-element.60), channel_id=1, source_target_pairs={{2,0},{3,1},{4,2},{5,3},{6,4},{7,5},{0,6},{1,7},{10,8},{11,9},{12,... | collective-permute-start | bytes 995336 | tf_op jit(solution)/shard_map/ppermute | solution.py:13
  30.2 42.8 %copy-start.9 = (f32[1152]{0:T(1024)}, f32[1152]{0:T(1024)S(1)}, u32[]{:S(2)}) copy-start(f32[1152]{0:T(1024)S(1)} %get-tuple-element.23) | copy-start | bytes 13828
  30.2 42.8 %copy-start.11 = (f32[1152]{0:T(1024)}, f32[1152]{0:T(1024)S(1)}, u32[]{:S(2)}) copy-start(f32[1152]{0:T(1024)S(1)} %get-tuple-element.31) | copy-start | bytes 13828
  30.2 42.8 %copy-start.13 = (f32[1152]{0:T(1024)}, f32[1152]{0:T(1024)S(1)}, u32[]{:S(2)}) copy-start(f32[1152]{0:T(1024)S(1)} %get-tuple-element.32) | copy-start | bytes 13828
  30.2 42.8 %copy-start.15 = (f32[1152]{0:T(1024)}, f32[1152]{0:T(1024)S(1)}, u32[]{:S(2)}) copy-start(f32[1152]{0:T(1024)S(1)} %get-tuple-element.33) | copy-start | bytes 13828
  30.2 42.8 %copy-start.17 = (f32[1152]{0:T(1024)}, f32[1152]{0:T(1024)S(1)}, u32[]{:S(2)}) copy-start(f32[1152]{0:T(1024)S(1)} %get-tuple-element.34) | copy-start | bytes 13828
  30.3 42.8 %copy-start.19 = (f32[1152]{0:T(1024)}, f32[1152]{0:T(1024)S(1)}, u32[]{:S(2)}) copy-start(f32[1152]{0:T(1024)S(1)} %get-tuple-element.35) | copy-start | bytes 13828
  30.3 42.8 %copy-start.21 = (f32[1152]{0:T(1024)}, f32[1152]{0:T(1024)S(1)}, u32[]{:S(2)}) copy-start(f32[1152]{0:T(1024)S(1)} %get-tuple-element.36) | copy-start | bytes 13828
  30.3 42.8 %copy-start.23 = (f32[1152]{0:T(1024)}, f32[1152]{0:T(1024)S(1)}, u32[]{:S(2)}) copy-start(f32[1152]{0:T(1024)S(1)} %get-tuple-element.37) | copy-start | bytes 13828
  30.3 42.8 %copy-start.25 = (f32[1152]{0:T(1024)}, f32[1152]{0:T(1024)S(1)}, u32[]{:S(2)}) copy-start(f32[1152]{0:T(1024)S(1)} %get-tuple-element.38) | copy-start | bytes 13828
  30.3 65.1 %copy-start.7 = (f32[1152]{0:T(1024)}, f32[1152]{0:T(1024)S(1)}, u32[]{:S(2)}) copy-start(f32[1152]{0:T(1024)S(1)} %get-tuple-element.40) | copy-start | bytes 13828
  73.1 1.5 copy-start.4
  77.9 16.6 %collective-permute-start.4 = (bf16[1,3,48,1152]{3,2,1,0:T(8,128)(2,1)S(1)}, bf16[1,3,48,1152]{3,2,1,0:T(8,128)(2,1)S(1)}, u32[]{:S(2)}, u32[]{:S(2)}) collective-permute-start(bf16[1,3,48,1152]{3,2,1,0:T(8,128)(2,1)S(1)} %get-tuple-element.55), channel_id=1, source_target_pairs={{2,0},{3,1},{4,2},{5,3},{6,4},{7,5},{0,6},{1,7},{10,8},{11,9},{12,... | collective-permute-start | bytes 995336 | tf_op jit(solution)/shard_map/ppermute | solution.py:13
  83.3 168.3 %collective-permute-start.5 = (bf16[1,6,48,1152]{3,2,1,0:T(8,128)(2,1)}, bf16[1,6,48,1152]{3,2,1,0:T(8,128)(2,1)}, u32[]{:S(2)}, u32[]{:S(2)}) collective-permute-start(bf16[1,6,48,1152]{3,2,1,0:T(8,128)(2,1)} %get-tuple-element.53), channel_id=1, source_target_pairs={{3,0},{4,1},{5,2},{6,3},{7,4},{0,5},{1,6},{2,7},{11,8},{12,9},{13,... | collective-permute-start | bytes 1990664 | tf_op jit(solution)/shard_map/ppermute | solution.py:13
  87.7 162.7 %collective-permute-start.6 = (bf16[1,6,48,1152]{3,2,1,0:T(8,128)(2,1)}, bf16[1,6,48,1152]{3,2,1,0:T(8,128)(2,1)}, u32[]{:S(2)}, u32[]{:S(2)}) collective-permute-start(bf16[1,6,48,1152]{3,2,1,0:T(8,128)(2,1)} %get-tuple-element.54), channel_id=1, source_target_pairs={{5,0},{6,1},{7,2},{0,3},{1,4},{2,5},{3,6},{4,7},{13,8},{14,9},{15,... | collective-permute-start | bytes 1990664 | tf_op jit(solution)/shard_map/ppermute | solution.py:13
  91.0 161.8 %collective-permute-start.7 = (bf16[1,3,48,1152]{3,2,1,0:T(8,128)(2,1)}, bf16[1,3,48,1152]{3,2,1,0:T(8,128)(2,1)}, u32[]{:S(2)}, u32[]{:S(2)}) collective-permute-start(bf16[1,3,48,1152]{3,2,1,0:T(8,128)(2,1)} %get-tuple-element.56), channel_id=1, source_target_pairs={{6,0},{7,1},{0,2},{1,3},{2,4},{3,5},{4,6},{5,7},{14,8},{15,9},{8,1... | collective-permute-start | bytes 995336 | tf_op jit(solution)/shard_map/ppermute | solution.py:13
  99.3 154.8 %collective-permute-start.9 = (bf16[1,9,48,1152]{3,2,1,0:T(8,128)(2,1)S(1)}, bf16[1,9,48,1152]{3,2,1,0:T(8,128)(2,1)}, u32[]{:S(2)}, u32[]{:S(2)}) collective-permute-start(bf16[1,9,48,1152]{3,2,1,0:T(8,128)(2,1)S(1)} %bitcast.69), channel_id=1, source_target_pairs={{4,0},{5,1},{6,2},{7,3},{0,4},{1,5},{2,6},{3,7},{12,8},{13,9},{14,... | collective-permute-start | bytes 2985992 | tf_op jit(solution)/shard_map/ppermute | solution.py:13
  245.7 3.3 copy-start.27
  245.7 3.3 copy-start.28
  249.8 1.9 copy-start.1
  253.9 1.4 copy-start.2
  253.9 1.4 copy-start.8
  254.0 1.4 copy-start.10
  254.0 1.4 copy-start.12
  254.0 1.4 copy-start.14
  254.0 1.4 copy-start.16
  254.0 1.4 copy-start.18
  254.0 1.4 copy-start.20
  254.0 1.4 copy-start.22
  254.0 1.4 copy-start.24
  254.0 1.4 copy-start.26
  722.7 2.9 copy-start.6
Sparse Core Ops, SparseCore 0:
  249.9 472.7 all-reduce.22
where the time goes:
time: 734 us; the launch traced here: 733 us
  waiting for transfers between devices  505 us (69%)
  blocking collectives  140 us (19%)
  starting transfers between devices  38.2 us (5%)
  other arithmetic  17.9 us (2%)
  between operations  14.9 us (2%)
  local copies, waits for them, and re-layouts  12.6 us (2%)
    psum x1, waiting for transfers between devices, per_device(): lax.psum((point_local, depth_local, bias_local), ('dp', 'lon'))  462 us
    psum x1, blocking collectives, per_device(): lax.psum((point_local, depth_local, bias_local), ('dp', 'lon'))  140 us
    ppermute x10, waiting for transfers between devices, from_behind(): return lax.ppermute(block, axis, route)  42.3 us
    ppermute x10, starting transfers between devices, from_behind(): return lax.ppermute(block, axis, route)  38.2 us
  transfers between devices with their start and end apart: 11, of which 2 were waited for; matrix products, arithmetic and copies ran while one was open for 4% of the time, Pallas kernels for 0%

commit v1 on v0

--- a/solution.py
+++ b/solution.py
@@ -1,6 +1,7 @@
 import jax
 import jax.numpy as jnp
 from jax import lax
+from jax.sharding import Mesh
 from jax.sharding import PartitionSpec as P
 
 RATE_A = 24
@@ -66,15 +67,68 @@
 
 
 def send_features(column_piece, shift_by):
-    return from_behind(column_piece, "lon", shift_by)
+    return from_behind(column_piece, LON, shift_by)
 
 
 def send_grads(column_piece, shift_by):
-    return from_behind(column_piece, "lon", shift_by)
+    return from_behind(column_piece, LON, shift_by)
+
+
+DP = ("z", "xl", "core")
+LON = ("y", "xh")
+PLANE = ("xl", "y", "xh")
+LANES = 128
+
+
+def swap_cores(block):
+    return lax.ppermute(block, "core", [(0, 1), (1, 0)])
+
+
+def exchange(blocks, axes):
+    return lax.all_to_all(blocks, axes, 0, 0, tiled=True)
+
+
+def gather_copies(block, axes):
+    peers = lax.axis_size(axes)
+    return exchange(jnp.broadcast_to(block[None], (peers,) + block.shape), axes)
+
+
+def sum_over_mesh(point_local, depth_local, bias_local, images):
+    branches, channels, outputs = point_local.shape
+    plane = lax.axis_size(PLANE)
+    depth = lax.axis_size("z")
+    main = point_local.reshape(branches, channels, 2, outputs // 2)
+    main = main.transpose(2, 0, 1, 3).reshape(2, plane, -1, LANES)
+    small = jnp.concatenate([depth_local.reshape(-1), bias_local.reshape(-1)])
+    unit = 2 * plane * LANES
+    main_rows = main.shape[2]
+    small_rows = -(-small.size // unit)
+    rows = -(-(main_rows + small_rows) // depth) * depth
+    small_rows = rows - main_rows
+    small = jnp.pad(small, (0, small_rows * unit - small.size)).reshape(2, plane, -1, LANES)
+    terms = jnp.concatenate([main, small], axis=2)
+    core = lax.axis_index("core")
+    kept = lax.dynamic_index_in_dim(terms, core, 0, keepdims=False)
+    sent = lax.dynamic_index_in_dim(terms, 1 - core, 0, keepdims=False)
+    terms = kept + swap_cores(sent.astype(jnp.bfloat16)).astype(jnp.float32)
+    terms = exchange(terms.astype(jnp.bfloat16), PLANE)
+    terms = jnp.sum(terms.astype(jnp.float32), axis=0)
+    terms = exchange(terms.reshape(depth, rows // depth, LANES), "z")
+    total = (jnp.sum(terms, axis=0) / images).astype(jnp.bfloat16)
+    total = gather_copies(total, "z").reshape(rows, LANES)
+    total = gather_copies(total, PLANE)
+    other = swap_cores(total)
+    total = jnp.where(core == 0, jnp.stack([total, other]), jnp.stack([other, total]))
+    point = total[:, :, :main_rows].reshape(2, branches, channels, outputs // 2)
+    point = point.transpose(1, 2, 0, 3).reshape(point_local.shape)
+    small = total[:, :, main_rows:].reshape(-1)
+    depth_grad = small[: depth_local.size].reshape(depth_local.shape)
+    bias = small[depth_local.size : depth_local.size + bias_local.size].reshape(bias_local.shape)
+    return point, depth_grad, bias.astype(jnp.float32)
 
 
 def per_device(features, depth_w, point_w, point_bias, cotangent):
-    group_size = lax.axis_size("lon")
+    group_size = lax.axis_size(LON)
     channels = features.shape[3]
     outputs = point_w.shape[2]
     dilations = (RATE_A, RATE_B)
@@ -142,20 +196,18 @@
         depth_terms.append(jnp.stack(tap_rows))
     depth_local = jnp.stack(depth_terms)
     feature_grad = grad_field.astype(jnp.bfloat16)
-    point_sum, depth_sum, bias_sum = lax.psum((point_local, depth_local, bias_local), ("dp", "lon"))
-    images = lax.axis_size("dp") * features.shape[0]
-    depth_grad = (depth_sum / images).astype(jnp.bfloat16)
-    point_grad = (point_sum / images).astype(jnp.bfloat16)
-    bias_grad = bias_sum / images
+    images = lax.axis_size(DP) * features.shape[0]
+    point_grad, depth_grad, bias_grad = sum_over_mesh(point_local, depth_local, bias_local, images)
     return (feature_grad, depth_grad, point_grad, bias_grad)
 
 
 def solution(mesh):
-    placed = (P("dp", "lon", None, None), P(), P(), P(), P("dp", "lon", None, None))
+    fine = Mesh(mesh.devices.reshape(16, 2, 2, 4, 2), DP + LON)
+    placed = (P(DP, LON, None, None), P(), P(), P(), P(DP, LON, None, None))
     return jax.shard_map(
         per_device,
-        mesh=mesh,
+        mesh=fine,
         in_specs=placed,
-        out_specs=(P("dp", "lon", None, None), P(), P(), P()),
+        out_specs=(P(DP, LON, None, None), P(), P(), P()),
         check_vma=False,
     )

time: 734 us -> 248 us (0.34)
  waiting for transfers between devices: 505 us -> 101 us
  blocking collectives: 140 us -> 0 us
  starting transfers between devices: 38.2 us -> 77.8 us
  local copies, waits for them, and re-layouts: 12.6 us -> 41 us
  between operations: 14.9 us -> 1.74 us
    psum x1 -> x0, waiting for transfers between devices: 462 us -> none  [per_device(): lax.psum((point_local, depth_local, bias_local), ('dp', 'lon'))]
    psum x1 -> x0, blocking collectives: 140 us -> none  [per_device(): lax.psum((point_local, depth_local, bias_local), ('dp', 'lon'))]
    all_to_all x0 -> x4, waiting for transfers between devices: none -> 50.3 us  [exchange(): return lax.all_to_all(blocks, axes, 0, 0, tiled=True)]
    all_to_all x0 -> x4, starting transfers between devices: none -> 29.3 us  [exchange(): return lax.all_to_all(blocks, axes, 0, 0, tiled=True)]
    reshape x0 -> x5, local copies, waits for them, and re-layouts: none -> 14.5 us  [the longest x1 11.3 us: sum_over_mesh(): point = total[:, :, :main_rows].reshape(2, branches, channels, outputs // 2)]
    ppermute x0 -> x2, starting transfers between devices: none -> 10.7 us  [swap_cores(): return lax.ppermute(block, 'core', [(0, 1), (1, 0)])]
    ppermute x10, waiting for transfers between devices: 42.3 us -> 50.8 us  [from_behind(): return lax.ppermute(block, axis, route)]
  transfers between devices with their start and end apart: 11 -> 16, of which waited for: 2 -> 6; matrix products, arithmetic and copies ran while one was open for 4% -> 20% of each run, Pallas kernels for 0% -> 0%
where the time goes in v1:
time: 248 us; the launch traced here: 247 us
  waiting for transfers between devices  101 us (41%)
  starting transfers between devices  77.8 us (31%)
  local copies, waits for them, and re-layouts  41 us (17%)
  other arithmetic  19.3 us (8%)
  matrix products  5.62 us (2%)
    ppermute x10, waiting for transfers between devices, from_behind(): return lax.ppermute(block, axis, route)  50.8 us
    all_to_all x4, waiting for transfers between devices, exchange(): return lax.all_to_all(blocks, axes, 0, 0, tiled=True)  50.3 us
    ppermute x10, starting transfers between devices, from_behind(): return lax.ppermute(block, axis, route)  37.8 us
    all_to_all x4, starting transfers between devices, exchange(): return lax.all_to_all(blocks, axes, 0, 0, tiled=True)  29.3 us
    reshape x1, local copies, waits for them, and re-layouts, sum_over_mesh(): point = total[:, :, :main_rows].reshape(2, branches, channels, outputs // 2)  11.3 us
    ppermute x2, starting transfers between devices, swap_cores(): return lax.ppermute(block, 'core', [(0, 1), (1, 0)])  10.7 us
    convert_element_type x1, other arithmetic, per_device(): feature_grad = grad_field.astype(jnp.bfloat16)  6.45 us
    unnamed x86, local copies, waits for them, and re-layouts  6.01 us
  transfers between devices with their start and end apart: 16, of which 6 were waited for; matrix products, arithmetic and copies ran while one was open for 20% of the time, Pallas kernels for 0%

profile of v1, /device:TPU:1, one launch (start us, length us, event | category | flops | bytes accessed | tf_op | source)
XLA Modules:
  0.0 246.7 jit_solution(8986146383047011700)
XLA Ops:
  0.6 5.8 %collective-permute-start.8 = (bf16[1,9,48,1152]{3,2,1,0:T(8,128)(2,1)}, bf16[1,9,48,1152]{3,2,1,0:T(8,128)(2,1)S(1)}, u32[]{:S(2)}, u32[]{:S(2)}) collective-permute-start(bf16[1,9,48,1152]{3,2,1,0:T(8,128)(2,1)} %param.5), channel_id=1, source_target_pairs={{4,0},{5,1},{6,2},{7,3},{0,4},{1,5},{2,6},{3,7},{12,8},{13,9},{14,... | collective-permute-start | bytes 2985992 | tf_op jit(solution)/shard_map/ppermute | solution.py:14
  6.4 2.5 fusion.82
  8.9 4.8 %collective-permute-start = (bf16[1,6,48,1152]{3,2,1,0:T(8,128)(2,1)}, bf16[1,6,48,1152]{3,2,1,0:T(8,128)(2,1)}, u32[]{:S(2)}, u32[]{:S(2)}) collective-permute-start(bf16[1,6,48,1152]{3,2,1,0:T(8,128)(2,1)} %get-tuple-element.59), channel_id=1, source_target_pairs={{5,0},{6,1},{7,2},{0,3},{1,4},{2,5},{3,6},{4,7},{13,8},{14,9},{15,... | collective-permute-start | bytes 1990664 | tf_op jit(solution)/shard_map/ppermute | solution.py:14
  13.7 0.9 fusion.81
  14.6 2.0 collective-permute-start.1
  16.6 5.4 %collective-permute-start.3 = (bf16[1,6,48,1152]{3,2,1,0:T(8,128)(2,1)}, bf16[1,6,48,1152]{3,2,1,0:T(8,128)(2,1)}, u32[]{:S(2)}, u32[]{:S(2)}) collective-permute-start(bf16[1,6,48,1152]{3,2,1,0:T(8,128)(2,1)} %get-tuple-element.60), channel_id=1, source_target_pairs={{3,0},{4,1},{5,2},{6,3},{7,4},{0,5},{1,6},{2,7},{11,8},{12,9},{13,... | collective-permute-start | bytes 1990664 | tf_op jit(solution)/shard_map/ppermute | solution.py:14
  22.1 3.0 %collective-permute-start.2 = (bf16[1,3,48,1152]{3,2,1,0:T(8,128)(2,1)}, bf16[1,3,48,1152]{3,2,1,0:T(8,128)(2,1)}, u32[]{:S(2)}, u32[]{:S(2)}) collective-permute-start(bf16[1,3,48,1152]{3,2,1,0:T(8,128)(2,1)} %get-tuple-element.58), channel_id=1, source_target_pairs={{2,0},{3,1},{4,2},{5,3},{6,4},{7,5},{0,6},{1,7},{10,8},{11,9},{12,... | collective-permute-start | bytes 995336 | tf_op jit(solution)/shard_map/ppermute | solution.py:14
  25.2 1.0 fusion.86
  26.6 38.9 %collective-permute-done.2 = bf16[1,3,48,1152]{3,2,1,0:T(8,128)(2,1)} collective-permute-done((bf16[1,3,48,1152]{3,2,1,0:T(8,128)(2,1)}, bf16[1,3,48,1152]{3,2,1,0:T(8,128)(2,1)}, u32[]{:S(2)}, u32[]{:S(2)}) %collective-permute-start.2) | collective-permute-done | bytes 331808 | tf_op jit(solution)/shard_map/ppermute | solution.py:14
  65.6 1.0 constant_dynamic-update-slice_fusion.3
  66.6 1.1 constant_dynamic-update-slice_fusion.1
  67.7 1.0 constant_dynamic-update-slice_fusion
  68.8 1.2 constant_dynamic-update-slice_fusion.2
  70.2 1.5 fusion.8
  71.7 0.6 convert_reduce_fusion.2
  72.3 0.7 fusion.26
  73.0 1.2 fusion.78
  74.1 4.3 %collective-permute-start.5 = (bf16[1,6,48,1152]{3,2,1,0:T(8,128)(2,1)}, bf16[1,6,48,1152]{3,2,1,0:T(8,128)(2,1)}, u32[]{:S(2)}, u32[]{:S(2)}) collective-permute-start(bf16[1,6,48,1152]{3,2,1,0:T(8,128)(2,1)} %get-tuple-element.51), channel_id=1, source_target_pairs={{3,0},{4,1},{5,2},{6,3},{7,4},{0,5},{1,6},{2,7},{11,8},{12,9},{13,... | collective-permute-start | bytes 1990664 | tf_op jit(solution)/shard_map/ppermute | solution.py:14
  78.5 1.0 fusion.79
  79.4 2.3 collective-permute-start.4
  81.7 5.1 %collective-permute-start.6 = (bf16[1,6,48,1152]{3,2,1,0:T(8,128)(2,1)}, bf16[1,6,48,1152]{3,2,1,0:T(8,128)(2,1)}, u32[]{:S(2)}, u32[]{:S(2)}) collective-permute-start(bf16[1,6,48,1152]{3,2,1,0:T(8,128)(2,1)} %get-tuple-element.52), channel_id=1, source_target_pairs={{5,0},{6,1},{7,2},{0,3},{1,4},{2,5},{3,6},{4,7},{13,8},{14,9},{15,... | collective-permute-start | bytes 1990664 | tf_op jit(solution)/shard_map/ppermute | solution.py:14
  86.8 1.9 collective-permute-start.7
  88.7 1.5 convolution_bitcast_fusion.1
  90.5 1.4 fusion.15
  91.9 0.6 convert_reduce_fusion.1
  92.5 0.7 copy-done.9
  93.1 0.5 convolution_convert_fusion
  93.9 2.2 fusion.41
  96.6 1.8 convolution_bitcast_fusion
  98.4 1.4 maximum_bitcast_fusion
  100.1 4.1 %collective-permute-start.10 = (bf16[16,160,128]{2,1,0:T(8,128)(2,1)S(1)}, bf16[16,160,128]{2,1,0:T(8,128)(2,1)S(1)}, u32[]{:S(2)}, u32[]{:S(2)}) collective-permute-start(bf16[16,160,128]{2,1,0:T(8,128)(2,1)S(1)} %fusion.54), channel_id=1, source_target_pairs={{0,8},{8,0},{1,9},{9,1},{2,10},{10,2},{3,11},{11,3},{4,12},{12,4},... | collective-permute-start | bytes 1966088 | tf_op jit(solution)/shard_map/ppermute | solution.py:84
  104.1 0.9 fusion.74
  105.0 11.9 %collective-permute-done.4 = bf16[1,3,48,1152]{3,2,1,0:T(8,128)(2,1)} collective-permute-done((bf16[1,3,48,1152]{3,2,1,0:T(8,128)(2,1)}, bf16[1,3,48,1152]{3,2,1,0:T(8,128)(2,1)}, u32[]{:S(2)}, u32[]{:S(2)}) %collective-permute-start.4) | collective-permute-done | bytes 331808 | tf_op jit(solution)/shard_map/ppermute | solution.py:14
  116.9 1.0 constant_dynamic-update-slice_fusion.5
  117.9 3.2 %collective-permute-start.9 = (bf16[1,9,48,1152]{3,2,1,0:T(8,128)(2,1)S(1)}, bf16[1,9,48,1152]{3,2,1,0:T(8,128)(2,1)}, u32[]{:S(2)}, u32[]{:S(2)}) collective-permute-start(bf16[1,9,48,1152]{3,2,1,0:T(8,128)(2,1)S(1)} %bitcast.114), channel_id=1, source_target_pairs={{4,0},{5,1},{6,2},{7,3},{0,4},{1,5},{2,6},{3,7},{12,8},{13,9},{14,... | collective-permute-start | bytes 2985992 | tf_op jit(solution)/shard_map/ppermute | solution.py:14
  121.1 1.0 fusion.53
  122.1 4.8 %all-to-all-start = ((bf16[16,160,128]{2,1,0:T(8,128)(2,1)}), bf16[16,160,128]{2,1,0:T(8,128)(2,1)}, u32[]{:S(2)}, u32[]{:S(2)}) async-start(bf16[16,160,128]{2,1,0:T(8,128)(2,1)} %fusion.53), calls=%async_computation | async-start | bytes 1310720 | tf_op jit(solution)/shard_map/all_to_all | solution.py:88
  126.9 0.9 fusion.77
  127.9 1.2 constant_dynamic-update-slice_fusion.4
  129.1 23.7 %all-to-all-done = bf16[16,160,128]{2,1,0:T(8,128)(2,1)} async-done(((bf16[16,160,128]{2,1,0:T(8,128)(2,1)}), bf16[16,160,128]{2,1,0:T(8,128)(2,1)}, u32[]{:S(2)}, u32[]{:S(2)}) %all-to-all-start) | async-done | bytes 655392 | tf_op jit(solution)/shard_map/all_to_all | solution.py:88
  152.8 1.8 convert_reduce_fusion
  154.6 1.5 reshape.325
  156.2 15.0 %all-to-all-start.1 = ((f32[16,10,128]{2,1,0:T(8,128)}), f32[16,10,128]{2,1,0:T(8,128)}, u32[]{:S(2)}, u32[]{:S(2)}) async-start(f32[16,10,128]{2,1,0:T(8,128)} %reshape.325), calls=%async_computation.1 | async-start | bytes 262144 | tf_op jit(solution)/shard_map/all_to_all | solution.py:88
  171.1 1.0 fusion.73
  172.2 1.1 constant_dynamic-update-slice_fusion.7
  173.3 9.9 %all-to-all-done.1 = f32[16,10,128]{2,1,0:T(8,128)} async-done(((f32[16,10,128]{2,1,0:T(8,128)}), f32[16,10,128]{2,1,0:T(8,128)}, u32[]{:S(2)}, u32[]{:S(2)}) %all-to-all-start.1) | async-done | bytes 81952 | tf_op jit(solution)/shard_map/all_to_all | solution.py:88
  183.3 0.9 reduce_sum.201
  184.2 0.6 broadcast_in_dim.6
  184.8 5.1 %all-to-all-start.2 = ((bf16[16,10,128]{2,1,0:T(8,128)(2,1)}), bf16[16,10,128]{2,1,0:T(8,128)(2,1)S(1)}, u32[]{:S(2)}, u32[]{:S(2)}) async-start(bf16[16,10,128]{2,1,0:T(8,128)(2,1)} %broadcast_in_dim.6), calls=%async_computation.2 | async-start | bytes 131072 | tf_op jit(solution)/shard_map/all_to_all | solution.py:88
  189.9 1.0 constant_dynamic-update-slice_fusion.6
  191.0 10.5 %all-to-all-done.2 = bf16[16,10,128]{2,1,0:T(8,128)(2,1)S(1)} async-done(((bf16[16,10,128]{2,1,0:T(8,128)(2,1)}), bf16[16,10,128]{2,1,0:T(8,128)(2,1)S(1)}, u32[]{:S(2)}, u32[]{:S(2)}) %all-to-all-start.2) | async-done | bytes 40992 | tf_op jit(solution)/shard_map/all_to_all | solution.py:88
  201.5 0.6 broadcast_in_dim.7
  202.1 1.7 broadcast_in_dim.8
  203.8 4.4 %all-to-all-start.3 = ((bf16[16,160,128]{2,1,0:T(8,128)(2,1)}), bf16[16,160,128]{2,1,0:T(8,128)(2,1)}, u32[]{:S(2)}, u32[]{:S(2)}) async-start(bf16[16,160,128]{2,1,0:T(8,128)(2,1)} %broadcast_in_dim.8), calls=%async_computation.3 | async-start | bytes 1310720 | tf_op jit(solution)/shard_map/all_to_all | solution.py:88
  208.4 1.0 fusion.75
  209.4 2.0 fusion.76
  211.4 6.1 %all-to-all-done.3 = bf16[16,160,128]{2,1,0:T(8,128)(2,1)} async-done(((bf16[16,160,128]{2,1,0:T(8,128)(2,1)}), bf16[16,160,128]{2,1,0:T(8,128)(2,1)}, u32[]{:S(2)}, u32[]{:S(2)}) %all-to-all-start.3) | async-done | bytes 655392 | tf_op jit(solution)/shard_map/all_to_all | solution.py:88
  217.5 6.7 %collective-permute-start.11 = (bf16[16,160,128]{2,1,0:T(8,128)(2,1)}, bf16[16,160,128]{2,1,0:T(8,128)(2,1)S(1)}, u32[]{:S(2)}, u32[]{:S(2)}) collective-permute-start(bf16[16,160,128]{2,1,0:T(8,128)(2,1)} %all-to-all-done.3), channel_id=1, source_target_pairs={{0,8},{8,0},{1,9},{9,1},{2,10},{10,2},{3,11},{11,3},{4,12},{12,4},... | collective-permute-start | bytes 1966088 | tf_op jit(solution)/shard_map/ppermute | solution.py:84
  224.3 6.4 %fusion.25 = bf16[1,9,48,1152]{3,2,1,0:T(8,128)(2,1)} fusion(bf16[1,9,48,1152]{3,2,1,0:T(8,128)(2,1)} %collective-permute-done.9, bf16[1,9,48,1152]{3,2,1,0:T(8,128)(2,1)S(1)} %bitcast.116, bf16[1,9,48,1152]{3,2,1,0:T(8,128)(2,1)S(1)} %bitcast.110, bf16[1,9,48,1152]{3,2,1,0:T(8,128)(2,1)S(1)} %constant_dynamic-update-slice_fusion.6, ...), kind=kLoop, calls=%fused_computation.73 | loop fusion | flops 25380864 | bytes 10036224 | tf_op jit(solution)/shard_map/convert_element_type | solution.py:198
  230.7 1.5 maximum_select_fusion
  232.4 11.3 %copy.29 = bf16[2,2,1152,128]{3,0,2,1:T(2,128)(2,1)S(1)} copy(bf16[2,2,1152,128]{3,2,1,0:T(8,128)(2,1)S(1)} %bitcast.117) | data formatting | bytes 2359296 | tf_op jit(solution)/shard_map/reshape | solution.py:122
  243.7 1.6 reshape.329
  245.4 0.7 copy.16
  246.1 0.6 slice_convert_fusion
  (130 shorter events, 1.7 us)
Async XLA Ops:
  0.6 13.0 %copy-start = (bf16[1,9,48,1152]{3,2,1,0:T(8,128)(2,1)S(1)}, bf16[1,9,48,1152]{3,2,1,0:T(8,128)(2,1)}, u32[]{:S(2)}) copy-start(bf16[1,9,48,1152]{3,2,1,0:T(8,128)(2,1)} %param.5) | copy-start | bytes 2985988
  0.6 89.6 %collective-permute-start.8 = (bf16[1,9,48,1152]{3,2,1,0:T(8,128)(2,1)}, bf16[1,9,48,1152]{3,2,1,0:T(8,128)(2,1)S(1)}, u32[]{:S(2)}, u32[]{:S(2)}) collective-permute-start(bf16[1,9,48,1152]{3,2,1,0:T(8,128)(2,1)} %param.5), channel_id=1, source_target_pairs={{4,0},{5,1},{6,2},{7,3},{0,4},{1,5},{2,6},{3,7},{12,8},{13,9},{14,... | collective-permute-start | bytes 2985992 | tf_op jit(solution)/shard_map/ppermute | solution.py:14
  8.9 57.7 %collective-permute-start = (bf16[1,6,48,1152]{3,2,1,0:T(8,128)(2,1)}, bf16[1,6,48,1152]{3,2,1,0:T(8,128)(2,1)}, u32[]{:S(2)}, u32[]{:S(2)}) collective-permute-start(bf16[1,6,48,1152]{3,2,1,0:T(8,128)(2,1)} %get-tuple-element.59), channel_id=1, source_target_pairs={{5,0},{6,1},{7,2},{0,3},{1,4},{2,5},{3,6},{4,7},{13,8},{14,9},{15,... | collective-permute-start | bytes 1990664 | tf_op jit(solution)/shard_map/ppermute | solution.py:14
  14.6 11.6 %copy-start.39 = (f32[2,256]{1,0:T(2,128)S(1)}, f32[2,256]{1,0:T(2,128)}, u32[]{:S(2)}) copy-start(f32[2,256]{1,0:T(2,128)} %param.8) | copy-start | bytes 6148
  14.6 11.6 %copy-start.12 = (bf16[2,3,3,1152]{3,0,2,1:T(2,128)(2,1)S(1)}, bf16[2,3,3,1152]{3,0,2,1:T(2,128)(2,1)}, u32[]{:S(2)}) copy-start(bf16[2,3,3,1152]{3,0,2,1:T(2,128)(2,1)} %param.6) | copy-start | bytes 124420
  14.6 11.8 %copy-start.10 = (bf16[1,9,48,512]{3,2,1,0:T(8,128)(2,1)S(1)}, bf16[1,9,48,512]{3,2,1,0:T(8,128)(2,1)}, u32[]{:S(2)}) copy-start(bf16[1,9,48,512]{3,2,1,0:T(8,128)(2,1)} %param.9) | copy-start | bytes 1327108
  14.6 53.1 %collective-permute-start.1 = (bf16[1,3,48,1152]{3,2,1,0:T(8,128)(2,1)}, bf16[1,3,48,1152]{3,2,1,0:T(8,128)(2,1)}, u32[]{:S(2)}, u32[]{:S(2)}) collective-permute-start(bf16[1,3,48,1152]{3,2,1,0:T(8,128)(2,1)} %get-tuple-element.57), channel_id=1, source_target_pairs={{6,0},{7,1},{0,2},{1,3},{2,4},{3,5},{4,6},{5,7},{14,8},{15,9},{8,1... | collective-permute-start | bytes 995336 | tf_op jit(solution)/shard_map/ppermute | solution.py:14
  16.6 52.2 %collective-permute-start.3 = (bf16[1,6,48,1152]{3,2,1,0:T(8,128)(2,1)}, bf16[1,6,48,1152]{3,2,1,0:T(8,128)(2,1)}, u32[]{:S(2)}, u32[]{:S(2)}) collective-permute-start(bf16[1,6,48,1152]{3,2,1,0:T(8,128)(2,1)} %get-tuple-element.60), channel_id=1, source_target_pairs={{3,0},{4,1},{5,2},{6,3},{7,4},{0,5},{1,6},{2,7},{11,8},{12,9},{13,... | collective-permute-start | bytes 1990664 | tf_op jit(solution)/shard_map/ppermute | solution.py:14
  22.1 43.5 %collective-permute-start.2 = (bf16[1,3,48,1152]{3,2,1,0:T(8,128)(2,1)}, bf16[1,3,48,1152]{3,2,1,0:T(8,128)(2,1)}, u32[]{:S(2)}, u32[]{:S(2)}) collective-permute-start(bf16[1,3,48,1152]{3,2,1,0:T(8,128)(2,1)} %get-tuple-element.58), channel_id=1, source_target_pairs={{2,0},{3,1},{4,2},{5,3},{6,4},{7,5},{0,6},{1,7},{10,8},{11,9},{12,... | collective-permute-start | bytes 995336 | tf_op jit(solution)/shard_map/ppermute | solution.py:14
  25.1 45.0 %copy-start.4 = (bf16[1,9,24,1152]{3,2,1,0:T(8,128)(2,1)}, bf16[1,9,24,1152]{3,2,1,0:T(8,128)(2,1)S(1)}, u32[]{:S(2)}) copy-start(bf16[1,9,24,1152]{3,2,1,0:T(8,128)(2,1)S(1)} %get-tuple-element.62) | copy-start | bytes 1492996
  26.4 43.7 %copy-start.30 = (f32[1152]{0:T(1024)}, f32[1152]{0:T(1024)S(1)}, u32[]{:S(2)}) copy-start(f32[1152]{0:T(1024)S(1)} %get-tuple-element.23) | copy-start | bytes 13828
  26.4 43.7 %copy-start.31 = (f32[1152]{0:T(1024)}, f32[1152]{0:T(1024)S(1)}, u32[]{:S(2)}) copy-start(f32[1152]{0:T(1024)S(1)} %get-tuple-element.31) | copy-start | bytes 13828
  26.4 43.7 %copy-start.32 = (f32[1152]{0:T(1024)}, f32[1152]{0:T(1024)S(1)}, u32[]{:S(2)}) copy-start(f32[1152]{0:T(1024)S(1)} %get-tuple-element.32) | copy-start | bytes 13828
  26.4 43.7 %copy-start.33 = (f32[1152]{0:T(1024)}, f32[1152]{0:T(1024)S(1)}, u32[]{:S(2)}) copy-start(f32[1152]{0:T(1024)S(1)} %get-tuple-element.33) | copy-start | bytes 13828
  26.4 43.7 %copy-start.34 = (f32[1152]{0:T(1024)}, f32[1152]{0:T(1024)S(1)}, u32[]{:S(2)}) copy-start(f32[1152]{0:T(1024)S(1)} %get-tuple-element.34) | copy-start | bytes 13828
  26.5 43.7 %copy-start.35 = (f32[1152]{0:T(1024)}, f32[1152]{0:T(1024)S(1)}, u32[]{:S(2)}) copy-start(f32[1152]{0:T(1024)S(1)} %get-tuple-element.35) | copy-start | bytes 13828
  26.5 43.7 %copy-start.36 = (f32[1152]{0:T(1024)}, f32[1152]{0:T(1024)S(1)}, u32[]{:S(2)}) copy-start(f32[1152]{0:T(1024)S(1)} %get-tuple-element.36) | copy-start | bytes 13828
  26.5 43.7 %copy-start.37 = (f32[1152]{0:T(1024)}, f32[1152]{0:T(1024)S(1)}, u32[]{:S(2)}) copy-start(f32[1152]{0:T(1024)S(1)} %get-tuple-element.37) | copy-start | bytes 13828
  26.5 43.7 %copy-start.38 = (f32[1152]{0:T(1024)}, f32[1152]{0:T(1024)S(1)}, u32[]{:S(2)}) copy-start(f32[1152]{0:T(1024)S(1)} %get-tuple-element.38) | copy-start | bytes 13828
  26.5 63.9 %copy-start.13 = (f32[1152]{0:T(1024)}, f32[1152]{0:T(1024)S(1)}, u32[]{:S(2)}) copy-start(f32[1152]{0:T(1024)S(1)} %get-tuple-element.24) | copy-start | bytes 13828
  26.5 63.9 %copy-start.15 = (f32[1152]{0:T(1024)}, f32[1152]{0:T(1024)S(1)}, u32[]{:S(2)}) copy-start(f32[1152]{0:T(1024)S(1)} %get-tuple-element.25) | copy-start | bytes 13828
  26.5 63.9 %copy-start.17 = (f32[1152]{0:T(1024)}, f32[1152]{0:T(1024)S(1)}, u32[]{:S(2)}) copy-start(f32[1152]{0:T(1024)S(1)} %get-tuple-element.26) | copy-start | bytes 13828
  26.5 63.9 %copy-start.19 = (f32[1152]{0:T(1024)}, f32[1152]{0:T(1024)S(1)}, u32[]{:S(2)}) copy-start(f32[1152]{0:T(1024)S(1)} %get-tuple-element.27) | copy-start | bytes 13828
  26.5 63.9 %copy-start.21 = (f32[1152]{0:T(1024)}, f32[1152]{0:T(1024)S(1)}, u32[]{:S(2)}) copy-start(f32[1152]{0:T(1024)S(1)} %get-tuple-element.28) | copy-start | bytes 13828
  26.5 63.9 %copy-start.23 = (f32[1152]{0:T(1024)}, f32[1152]{0:T(1024)S(1)}, u32[]{:S(2)}) copy-start(f32[1152]{0:T(1024)S(1)} %get-tuple-element.29) | copy-start | bytes 13828
  26.6 63.9 %copy-start.25 = (f32[1152]{0:T(1024)}, f32[1152]{0:T(1024)S(1)}, u32[]{:S(2)}) copy-start(f32[1152]{0:T(1024)S(1)} %get-tuple-element.30) | copy-start | bytes 13828
  26.6 63.9 %copy-start.27 = (f32[1152]{0:T(1024)}, f32[1152]{0:T(1024)S(1)}, u32[]{:S(2)}) copy-start(f32[1152]{0:T(1024)S(1)} %get-tuple-element.39) | copy-start | bytes 13828
  26.6 63.9 %copy-start.29 = (f32[1152]{0:T(1024)}, f32[1152]{0:T(1024)S(1)}, u32[]{:S(2)}) copy-start(f32[1152]{0:T(1024)S(1)} %get-tuple-element.40) | copy-start | bytes 13828
  70.2 1.5 copy-start.11
  74.1 53.7 %collective-permute-start.5 = (bf16[1,6,48,1152]{3,2,1,0:T(8,128)(2,1)}, bf16[1,6,48,1152]{3,2,1,0:T(8,128)(2,1)}, u32[]{:S(2)}, u32[]{:S(2)}) collective-permute-start(bf16[1,6,48,1152]{3,2,1,0:T(8,128)(2,1)} %get-tuple-element.51), channel_id=1, source_target_pairs={{3,0},{4,1},{5,2},{6,3},{7,4},{0,5},{1,6},{2,7},{11,8},{12,9},{13,... | collective-permute-start | bytes 1990664 | tf_op jit(solution)/shard_map/ppermute | solution.py:14
  79.4 11.0 %copy-start.7 = (bf16[1,9,12,1152]{3,2,1,0:T(8,128)(2,1)S(1)}, bf16[1,9,12,1152]{3,2,1,0:T(8,128)(2,1)}, u32[]{:S(2)}) copy-start(bf16[1,9,12,1152]{3,2,1,0:T(8,128)(2,1)} %get-tuple-element.67) | copy-start | bytes 746500
  79.4 11.0 %copy-start.8 = (bf16[1,9,12,1152]{3,2,1,0:T(8,128)(2,1)S(1)}, bf16[1,9,12,1152]{3,2,1,0:T(8,128)(2,1)}, u32[]{:S(2)}) copy-start(bf16[1,9,12,1152]{3,2,1,0:T(8,128)(2,1)} %get-tuple-element.68) | copy-start | bytes 746500
  79.4 37.5 %collective-permute-start.4 = (bf16[1,3,48,1152]{3,2,1,0:T(8,128)(2,1)}, bf16[1,3,48,1152]{3,2,1,0:T(8,128)(2,1)}, u32[]{:S(2)}, u32[]{:S(2)}) collective-permute-start(bf16[1,3,48,1152]{3,2,1,0:T(8,128)(2,1)} %get-tuple-element.53), channel_id=1, source_target_pairs={{2,0},{3,1},{4,2},{5,3},{6,4},{7,5},{0,6},{1,7},{10,8},{11,9},{12,... | collective-permute-start | bytes 995336 | tf_op jit(solution)/shard_map/ppermute | solution.py:14
  81.7 90.5 %collective-permute-start.6 = (bf16[1,6,48,1152]{3,2,1,0:T(8,128)(2,1)}, bf16[1,6,48,1152]{3,2,1,0:T(8,128)(2,1)}, u32[]{:S(2)}, u32[]{:S(2)}) collective-permute-start(bf16[1,6,48,1152]{3,2,1,0:T(8,128)(2,1)} %get-tuple-element.52), channel_id=1, source_target_pairs={{5,0},{6,1},{7,2},{0,3},{1,4},{2,5},{3,6},{4,7},{13,8},{14,9},{15,... | collective-permute-start | bytes 1990664 | tf_op jit(solution)/shard_map/ppermute | solution.py:14
  86.8 103.1 %collective-permute-start.7 = (bf16[1,3,48,1152]{3,2,1,0:T(8,128)(2,1)}, bf16[1,3,48,1152]{3,2,1,0:T(8,128)(2,1)}, u32[]{:S(2)}, u32[]{:S(2)}) collective-permute-start(bf16[1,3,48,1152]{3,2,1,0:T(8,128)(2,1)} %get-tuple-element.54), channel_id=1, source_target_pairs={{6,0},{7,1},{0,2},{1,3},{2,4},{3,5},{4,6},{5,7},{14,8},{15,9},{8,1... | collective-permute-start | bytes 995336 | tf_op jit(solution)/shard_map/ppermute | solution.py:14
  90.3 1.6 copy-start.1
  91.9 4.2 %copy-start.6 = (bf16[1,9,48,1152]{3,2,1,0:T(8,128)(2,1)}, bf16[1,9,48,1152]{3,2,1,0:T(8,128)(2,1)S(1)}, u32[]{:S(2)}) copy-start(bf16[1,9,48,1152]{3,2,1,0:T(8,128)(2,1)S(1)} %fusion.15) | copy-start | bytes 2985988
  92.5 0.7 copy-start.9
  92.5 1.3 copy-start.2
  92.5 1.4 copy-start.5
  100.1 21.0 %collective-permute-start.10 = (bf16[16,160,128]{2,1,0:T(8,128)(2,1)S(1)}, bf16[16,160,128]{2,1,0:T(8,128)(2,1)S(1)}, u32[]{:S(2)}, u32[]{:S(2)}) collective-permute-start(bf16[16,160,128]{2,1,0:T(8,128)(2,1)S(1)} %fusion.54), channel_id=1, source_target_pairs={{0,8},{8,0},{1,9},{9,1},{2,10},{10,2},{3,11},{11,3},{4,12},{12,4},... | collective-permute-start | bytes 1966088 | tf_op jit(solution)/shard_map/ppermute | solution.py:84
  117.9 91.5 %collective-permute-start.9 = (bf16[1,9,48,1152]{3,2,1,0:T(8,128)(2,1)S(1)}, bf16[1,9,48,1152]{3,2,1,0:T(8,128)(2,1)}, u32[]{:S(2)}, u32[]{:S(2)}) collective-permute-start(bf16[1,9,48,1152]{3,2,1,0:T(8,128)(2,1)S(1)} %bitcast.114), channel_id=1, source_target_pairs={{4,0},{5,1},{6,2},{7,3},{0,4},{1,5},{2,6},{3,7},{12,8},{13,9},{14,... | collective-permute-start | bytes 2985992 | tf_op jit(solution)/shard_map/ppermute | solution.py:14
  122.1 30.7 %all-to-all-start = ((bf16[16,160,128]{2,1,0:T(8,128)(2,1)}), bf16[16,160,128]{2,1,0:T(8,128)(2,1)}, u32[]{:S(2)}, u32[]{:S(2)}) async-start(bf16[16,160,128]{2,1,0:T(8,128)(2,1)} %fusion.53), calls=%async_computation | async-start | bytes 1310720 | tf_op jit(solution)/shard_map/all_to_all | solution.py:88
  129.0 43.1 %copy-start.3 = (bf16[1,9,48,1152]{3,2,1,0:T(8,128)(2,1)}, bf16[1,9,48,1152]{3,2,1,0:T(8,128)(2,1)S(1)}, u32[]{:S(2)}) copy-start(bf16[1,9,48,1152]{3,2,1,0:T(8,128)(2,1)S(1)} %constant_dynamic-update-slice_fusion.4) | copy-start | bytes 2985988
  156.2 27.1 %all-to-all-start.1 = ((f32[16,10,128]{2,1,0:T(8,128)}), f32[16,10,128]{2,1,0:T(8,128)}, u32[]{:S(2)}, u32[]{:S(2)}) async-start(f32[16,10,128]{2,1,0:T(8,128)} %reshape.325), calls=%async_computation.1 | async-start | bytes 262144 | tf_op jit(solution)/shard_map/all_to_all | solution.py:88
  184.8 16.6 %all-to-all-start.2 = ((bf16[16,10,128]{2,1,0:T(8,128)(2,1)}), bf16[16,10,128]{2,1,0:T(8,128)(2,1)S(1)}, u32[]{:S(2)}, u32[]{:S(2)}) async-start(bf16[16,10,128]{2,1,0:T(8,128)(2,1)} %broadcast_in_dim.6), calls=%async_computation.2 | async-start | bytes 131072 | tf_op jit(solution)/shard_map/all_to_all | solution.py:88
  203.8 13.7 %all-to-all-start.3 = ((bf16[16,160,128]{2,1,0:T(8,128)(2,1)}), bf16[16,160,128]{2,1,0:T(8,128)(2,1)}, u32[]{:S(2)}, u32[]{:S(2)}) async-start(bf16[16,160,128]{2,1,0:T(8,128)(2,1)} %broadcast_in_dim.8), calls=%async_computation.3 | async-start | bytes 1310720 | tf_op jit(solution)/shard_map/all_to_all | solution.py:88
  208.3 15.9 %copy-start.14 = (f32[1152]{0:T(1024)S(1)}, f32[1152]{0:T(1024)}, u32[]{:S(2)}) copy-start(f32[1152]{0:T(1024)} %copy-done.13) | copy-start | bytes 13828
  208.3 15.9 %copy-start.16 = (f32[1152]{0:T(1024)S(1)}, f32[1152]{0:T(1024)}, u32[]{:S(2)}) copy-start(f32[1152]{0:T(1024)} %copy-done.15) | copy-start | bytes 13828
  208.3 15.9 %copy-start.18 = (f32[1152]{0:T(1024)S(1)}, f32[1152]{0:T(1024)}, u32[]{:S(2)}) copy-start(f32[1152]{0:T(1024)} %copy-done.17) | copy-start | bytes 13828
  208.3 15.9 %copy-start.20 = (f32[1152]{0:T(1024)S(1)}, f32[1152]{0:T(1024)}, u32[]{:S(2)}) copy-start(f32[1152]{0:T(1024)} %copy-done.19) | copy-start | bytes 13828
  208.3 15.9 %copy-start.22 = (f32[1152]{0:T(1024)S(1)}, f32[1152]{0:T(1024)}, u32[]{:S(2)}) copy-start(f32[1152]{0:T(1024)} %copy-done.21) | copy-start | bytes 13828
  208.3 15.9 %copy-start.24 = (f32[1152]{0:T(1024)S(1)}, f32[1152]{0:T(1024)}, u32[]{:S(2)}) copy-start(f32[1152]{0:T(1024)} %copy-done.23) | copy-start | bytes 13828
  208.3 15.9 %copy-start.26 = (f32[1152]{0:T(1024)S(1)}, f32[1152]{0:T(1024)}, u32[]{:S(2)}) copy-start(f32[1152]{0:T(1024)} %copy-done.25) | copy-start | bytes 13828
  208.4 15.9 %copy-start.28 = (f32[1152]{0:T(1024)S(1)}, f32[1152]{0:T(1024)}, u32[]{:S(2)}) copy-start(f32[1152]{0:T(1024)} %copy-done.27) | copy-start | bytes 13828
  217.5 13.2 %collective-permute-start.11 = (bf16[16,160,128]{2,1,0:T(8,128)(2,1)}, bf16[16,160,128]{2,1,0:T(8,128)(2,1)S(1)}, u32[]{:S(2)}, u32[]{:S(2)}) collective-permute-start(bf16[16,160,128]{2,1,0:T(8,128)(2,1)} %all-to-all-done.3), channel_id=1, source_target_pairs={{0,8},{8,0},{1,9},{9,1},{2,10},{10,2},{3,11},{11,3},{4,12},{12,4},... | collective-permute-start | bytes 1966088 | tf_op jit(solution)/shard_map/ppermute | solution.py:84

commit v2 on v0

v2 whole, which is shorter than its diff:
```python
import jax
import jax.numpy as jnp
from jax import lax
from jax.sharding import Mesh
from jax.sharding import PartitionSpec as P

RATE_A = 24
RATE_B = 36
CLASS = 12
PAIR = 2

DP = ("zh", "zl", "xl", "core")
LON = ("y", "xh")
PLANE = ("xl", "y", "xh")


def swap_cores(block):
    return lax.ppermute(block, "core", [(0, 1), (1, 0)])


def exchange(blocks, axes):
    return lax.all_to_all(blocks, axes, 0, 0, tiled=True)


def gather_copies(block, axes):
    peers = lax.axis_size(axes)
    return exchange(jnp.broadcast_to(block[None], (peers,) + block.shape), axes)


def scatter_sum(terms):
    core = lax.axis_index("core")
    kept = lax.dynamic_index_in_dim(terms, core, 0, keepdims=False)
    sent = lax.dynamic_index_in_dim(terms, 1 - core, 0, keepdims=False)
    terms = kept + swap_cores(sent.astype(jnp.bfloat16)).astype(jnp.float32)
    terms = exchange(terms.astype(jnp.bfloat16), PLANE)
    return jnp.sum(terms.astype(jnp.float32), axis=0)


def sum_over_mesh(point_local, depth_local, bias_local, images):
    branches, channels, outputs = point_local.shape
    plane = lax.axis_size(PLANE)
    main = scatter_sum(point_local.reshape(branches, plane, -1, outputs))
    small = jnp.concatenate([depth_local.reshape(branches, -1), bias_local], axis=1)
    used = small.shape[1]
    unit = plane * 8 * outputs
    room = -(-used // unit) * unit
    small = jnp.pad(small, ((0, 0), (0, room - used))).reshape(branches, plane, -1, outputs)
    small = scatter_sum(small)
    main_rows = main.shape[0]
    terms = jnp.concatenate([main, small], axis=0)
    terms = jnp.sum(gather_copies(terms, "zl"), axis=0)
    terms = jnp.sum(gather_copies(terms.astype(jnp.bfloat16), "zh").astype(jnp.float32), axis=0)
    total = gather_copies((terms / images).astype(jnp.bfloat16), PLANE)
    other = swap_cores(total)
    first = lax.axis_index("core") == 0
    total = jnp.stack([jnp.where(first, total, other), jnp.where(first, other, total)])
    point = total[:, :, :main_rows].reshape(point_local.shape)
    small = total[:, :, main_rows:].reshape(branches, -1)
    depth_grad = small[:, : used - outputs].reshape(depth_local.shape)
    bias = small[:, used - outputs : used].astype(jnp.float32)
    return point, depth_grad, bias


def to_classes(field):
    _, columns, rows, width = field.shape
    peers = lax.axis_size(LON)
    groups = CLASS // PAIR
    chunks = field.reshape(columns, rows // CLASS, groups, PAIR, width).transpose(2, 0, 1, 3, 4)
    chunks = chunks.reshape(groups, columns, rows // groups, width)
    chunks = jnp.pad(chunks, ((0, peers - groups), (0, 0), (0, 0), (0, 0)))
    return exchange(chunks, LON).reshape(peers * columns, rows // groups, width)


def from_classes(field, rows):
    columns, held, width = field.shape
    peers = lax.axis_size(LON)
    groups = CLASS // PAIR
    chunks = exchange(field.reshape(peers, columns // peers, held, width), LON)[:groups]
    chunks = chunks.reshape(groups, columns // peers, rows // CLASS, PAIR, width)
    return chunks.transpose(1, 2, 0, 3, 4).reshape(1, columns // peers, rows, width)


def lat_shift(field, dilation, step):
    if step == 0:
        return field
    height = field.shape[1]
    offset = dilation * PAIR // CLASS
    if step > 0:
        return jnp.pad(field[:, offset:], ((0, 0), (0, offset), (0, 0)))
    return jnp.pad(field[:, : height - offset], ((0, 0), (offset, 0), (0, 0)))


def gate_slope(pre_act):
    sigmoid_val = jax.nn.sigmoid(pre_act)
    return sigmoid_val * (1.0 + pre_act * (1.0 - sigmoid_val))


def per_device(features, depth_w, point_w, point_bias, cotangent):
    rows = features.shape[2]
    outputs = point_w.shape[2]
    dilations = (RATE_A, RATE_B)
    images = lax.axis_size(DP) * features.shape[0]
    taps = depth_w.astype(jnp.float32)
    field = to_classes(features)
    upstream = to_classes(cotangent)
    columns, held, channels = field.shape
    point_terms = []
    bias_terms = []
    dgrad_list = []
    for branch, dilation in enumerate(dilations):
        depth_acc = jnp.zeros(field.shape, jnp.float32)
        for lon_step in (-1, 0, 1):
            source = jnp.roll(field, -lon_step * dilation, axis=0)
            for lat_step in (-1, 0, 1):
                tapped = lat_shift(source, dilation, lat_step).astype(jnp.float32)
                depth_acc = depth_acc + taps[branch, lat_step + 1, lon_step + 1] * tapped
        flat_depth = depth_acc.astype(jnp.bfloat16).reshape(-1, channels)
        point_act = (
            jnp.dot(flat_depth, point_w[branch], preferred_element_type=jnp.float32)
            + point_bias[branch]
        )
        upstream_part = (
            upstream[..., branch * outputs : (branch + 1) * outputs]
            .reshape(-1, outputs)
            .astype(jnp.float32)
        )
        pgrad = (upstream_part * gate_slope(point_act)).astype(jnp.bfloat16)
        bias_terms.append(jnp.sum(pgrad.astype(jnp.float32), axis=0))
        point_terms.append(
            lax.dot_general(
                flat_depth, pgrad, (((0,), (0,)), ((), ())), preferred_element_type=jnp.float32
            )
        )
        dgrad = lax.dot_general(
            pgrad, point_w[branch], (((1,), (1,)), ((), ())), preferred_element_type=jnp.float32
        )
        dgrad_list.append(dgrad.astype(jnp.bfloat16).reshape(field.shape))
    grad_field = jnp.zeros(field.shape, jnp.float32)
    depth_terms = []
    for branch, dilation in enumerate(dilations):
        dgrad_wide = dgrad_list[branch].astype(jnp.float32)
        tap_rows = []
        for lat_step in (-1, 0, 1):
            tap_cols = []
            for lon_step in (-1, 0, 1):
                source = jnp.roll(field, -lon_step * dilation, axis=0)
                tapped = lat_shift(source, dilation, lat_step).astype(jnp.float32)
                tap_cols.append(jnp.sum(tapped * dgrad_wide, axis=(0, 1)))
                behind = jnp.roll(dgrad_list[branch], lon_step * dilation, axis=0)
                behind = lat_shift(behind, dilation, -lat_step).astype(jnp.float32)
                grad_field = grad_field + taps[branch, lat_step + 1, lon_step + 1] * behind
            tap_rows.append(jnp.stack(tap_cols))
        depth_terms.append(jnp.stack(tap_rows))
    feature_grad = from_classes(grad_field.astype(jnp.bfloat16), rows)
    point_grad, depth_grad, bias_grad = sum_over_mesh(
        jnp.stack(point_terms), jnp.stack(depth_terms), jnp.stack(bias_terms), images
    )
    return (feature_grad, depth_grad, point_grad, bias_grad)


def solution(mesh):
    fine = Mesh(mesh.devices.reshape(4, 4, 2, 2, 4, 2), DP + LON)
    placed = (P(DP, LON, None, None), P(), P(), P(), P(DP, LON, None, None))
    return jax.shard_map(
        per_device,
        mesh=fine,
        in_specs=placed,
        out_specs=(P(DP, LON, None, None), P(), P(), P()),
        check_vma=False,
    )
```

time: 734 us -> 220 us (0.30)
  the two profiles are of different devices: /device:TPU:1 before, /device:TPU:32 now
where the time goes in v2:
time: 220 us; the launch traced here: 219 us
  starting transfers between devices  59.5 us (27%)
  waiting for transfers between devices  57.7 us (26%)
  other arithmetic  49.9 us (23%)
  local copies, waits for them, and re-layouts  35.7 us (16%)
  matrix products  14.1 us (6%)
    all_to_all x8, waiting for transfers between devices, exchange(): return lax.all_to_all(blocks, axes, 0, 0, tiled=True)  57.7 us
    all_to_all x8, starting transfers between devices, exchange(): return lax.all_to_all(blocks, axes, 0, 0, tiled=True)  53.3 us
    convert_element_type x1, other arithmetic, per_device(): feature_grad = from_classes(grad_field.astype(jnp.bfloat16), rows)  11.5 us
    reshape x2, other arithmetic, per_device(): flat_depth = depth_acc.astype(jnp.bfloat16).reshape(-1, channels)  10.7 us
    concatenate x3, other arithmetic, per_device(): behind = jnp.roll(dgrad_list[branch], lon_step * dilation, axis=0)  6.95 us
    dot_general x2, matrix products, per_device(): lax.dot_general(pgrad, point_w[branch], (((1,), (1,)), ((), ())), preferr...  6.34 us
    ppermute x3, starting transfers between devices, swap_cores(): return lax.ppermute(block, 'core', [(0, 1), (1, 0)])  6.22 us
    dot_general x2, matrix products, per_device(): jnp.dot(flat_depth, point_w[branch], preferred_element_type=jnp.float32)  5.51 us
  transfers between devices with their start and end apart: 11, of which 6 were waited for; matrix products, arithmetic and copies ran while one was open for 23% of the time, Pallas kernels for 0%

profile of v2, /device:TPU:32, one launch (start us, length us, event | category | flops | bytes accessed | tf_op | source)
XLA Modules:
  0.0 218.6 jit_solution(8314958572813122684)
XLA Ops:
  0.6 2.4 %reshape.141 = bf16[9,4,6,2,1152]{4,3,2,1,0:T(2,128)(2,1)S(1)} reshape(bf16[1,9,48,1152]{3,2,1,0:T(8,128)(2,1)} %param.5) | data formatting | bytes 1990656 | tf_op jit(solution)/shard_map/reshape | solution.py:68
  4.2 1.2 pad.93
  5.4 7.1 %all-to-all-start.1 = ((bf16[8,9,8,1152]{3,2,1,0:T(8,128)(2,1)}), bf16[8,9,8,1152]{3,2,1,0:T(8,128)(2,1)S(1)}, u32[]{:S(2)}, u32[]{:S(2)}) async-start(bf16[8,9,8,1152]{3,2,1,0:T(8,128)(2,1)} %pad.93), calls=%async_computation.1 | async-start | bytes 2654208 | tf_op jit(solution)/shard_map/all_to_all | solution.py:22
  13.1 0.9 pad.92
  14.0 0.8 slice_reduce_fusion.17
  15.4 17.3 %all-to-all-done.1 = bf16[8,9,8,1152]{3,2,1,0:T(8,128)(2,1)S(1)} async-done(((bf16[8,9,8,1152]{3,2,1,0:T(8,128)(2,1)}), bf16[8,9,8,1152]{3,2,1,0:T(8,128)(2,1)S(1)}, u32[]{:S(2)}, u32[]{:S(2)}) %all-to-all-start.1) | async-done | bytes 1327136 | tf_op jit(solution)/shard_map/all_to_all | solution.py:22
  32.6 4.4 %all-to-all-start = ((bf16[8,9,8,512]{3,2,1,0:T(8,128)(2,1)}), bf16[8,9,8,512]{3,2,1,0:T(8,128)(2,1)}, u32[]{:S(2)}, u32[]{:S(2)}) async-start(bf16[8,9,8,512]{3,2,1,0:T(8,128)(2,1)} %pad.92), calls=%async_computation | async-start | bytes 1179648 | tf_op jit(solution)/shard_map/all_to_all | solution.py:22
  37.8 1.6 fusion.63
  39.5 0.8 copy-done.23
  41.0 6.0 %fusion.52 = bf16[576,1152]{1,0:T(8,128)(2,1)} fusion(bf16[72,4,1152]{2,1,0:T(4,128)(2,1)S(1)} %get-tuple-element.59, f32[1152]{0:T(1024)S(1)} %copy-done.48, f32[1152]{0:T(1024)S(1)} %copy-done.49, bf16[72,4,1152]{2,1,0:T(4,128)(2,1)S(1)} %get-tuple-element.58, f32[1152]{0:T(1024)S(1)} %copy-done.50, bf16[72,4,1152]{2,1,0:T(4,128)(2,1)S(1)} %get-tuple-element.57, ...), kind=kLoop, calls=%fused_computation.131 | loop fusion | flops 21897216 | bytes 9331200 | tf_op jit(solution)/shard_map/reshape | solution.py:117
  47.0 2.7 %copy.24 = bf16[576,1152]{0,1:T(8,128)(2,1)} copy(bf16[576,1152]{1,0:T(8,128)(2,1)} %fusion.52) | data formatting | bytes 2654208 | tf_op jit(solution)/shard_map/reshape | solution.py:117
  49.8 2.6 %convert_reduce_fusion.2 = (f32[256]{0:T(256)}, bf16[576,256]{1,0:T(8,128)(2,1)S(1)}) fusion(f32[256]{0:T(256)} %bitcast.199, bf16[576,1152]{1,0:T(8,128)(2,1)S(1)} %copy-done.17, bf16[2,1152,256]{2,1,0:T(8,128)(2,1)} %param.7, bf16[72,8,512]{2,1,0:T(8,128)(2,1)} %bitcast.1), kind=kOutput, calls=%fused_computation.166 | convolution fusion | flops 341655296 | bytes 2508800 | tf_op jit(solution)/shard_map/dot_general | solution.py:119
  52.5 3.7 %fusion.45 = (f32[1152]{0:T(1024)}, f32[1152]{0:T(1024)}, f32[1152]{0:T(1024)}, f32[1152]{0:T(1024)}, f32[1152]{0:T(1024)}, /*index=5*/f32[1152]{0:T(1024)}, bf16[576,1152]{1,0:T(8,128)(2,1)S(1)}) fusion(bf16[72,4,1152]{2,1,0:T(4,128)(2,1)S(1)} %copy-done.30, bf16[72,4,1152]{2,1,0:T(4,128)(2,1)S(1)} %copy-done.26, bf16[72,4,1152]{2,1,0:T(4,128)(2,1)S(1)} %copy-done.22, ...), kind=kOutput, calls=%fused_computation.92 | convolution fusion | flops 353002752 | bytes 6220800 | tf_op jit(solution)/shard_map/dot_general | solution.py:134
  56.2 1.2 fusion.10
  57.4 1.3 slice_bitcast_fusion.1
  58.8 1.0 slice_bitcast_fusion.5
  60.5 1.6 convolution_bitcast_fusion.1
  62.3 1.8 fusion.84
  65.2 4.7 %fusion.51 = bf16[576,1152]{1,0:T(8,128)(2,1)} fusion(f32[1152]{0:T(1024)S(1)} %get-tuple-element.19, f32[1152]{0:T(1024)S(1)} %get-tuple-element.20, f32[1152]{0:T(1024)S(1)} %copy-done.40, bf16[72,2,1152]{2,1,0:T(2,128)(2,1)S(1)} %get-tuple-element.78, f32[1152]{0:T(1024)S(1)} %copy-done.41, f32[1152]{0:T(1024)S(1)} %copy-done.42, ...), kind=kLoop, calls=%fused_computation.130 | loop fusion | flops 17915904 | bytes 5349888 | tf_op jit(solution)/shard_map/reshape | solution.py:117
  69.9 2.6 %copy.25 = bf16[576,1152]{0,1:T(8,128)(2,1)} copy(bf16[576,1152]{1,0:T(8,128)(2,1)} %fusion.51) | data formatting | bytes 2654208 | tf_op jit(solution)/shard_map/reshape | solution.py:117
  72.6 2.9 %convert_reduce_fusion.1 = (f32[256]{0:T(256)}, bf16[576,256]{1,0:T(8,128)(2,1)S(1)}) fusion(f32[256]{0:T(256)S(1)} %bitcast.198, bf16[576,1152]{1,0:T(8,128)(2,1)} %fusion.51, bf16[2,1152,256]{2,1,0:T(8,128)(2,1)} %param.7, bf16[72,8,512]{2,1,0:T(8,128)(2,1)} %bitcast.1), kind=kOutput, calls=%fused_computation.165 | convolution fusion | flops 341655296 | bytes 2508800 | tf_op jit(solution)/shard_map/dot_general | solution.py:119
  75.5 2.6 %fusion.37 = (f32[1152]{0:T(1024)}, f32[1152]{0:T(1024)}, f32[1152]{0:T(1024)}, f32[1152]{0:T(1024)}, bf16[576,1152]{1,0:T(8,128)(2,1)S(1)}) fusion(bf16[72,2,1152]{2,1,0:T(2,128)(2,1)S(1)} %copy-done.38, bf16[72,2,1152]{2,1,0:T(2,128)(2,1)S(1)} %copy-done.36, bf16[72,2,1152]{2,1,0:T(2,128)(2,1)S(1)} %copy-done.34, bf16[72,2,1152]{2,1,0:T(2,128)(2,1)S(1)} %copy-done.32, ...), kind=kOutput, calls=%fused_computation.84 | convolution fusion | flops 349023744 | bytes 3557376 | tf_op jit(solution)/shard_map/dot_general | solution.py:134
  78.8 1.1 copy-done.4
  79.9 1.0 fusion.67
  81.2 1.9 collective-permute-start
  83.2 1.0 fusion.35
  84.2 1.2 fusion.30
  85.7 0.8 stack.145
  86.5 0.7 stack.144
  87.2 0.7 stack.140
  87.9 0.7 stack.141
  88.6 0.7 stack.148
  90.2 0.8 fusion.88
  91.0 2.4 %collective-permute-start.1 = (bf16[16,8,256]{2,1,0:T(8,128)(2,1)S(1)}, bf16[16,8,256]{2,1,0:T(8,128)(2,1)S(1)}, u32[]{:S(2)}, u32[]{:S(2)}) collective-permute-start(bf16[16,8,256]{2,1,0:T(8,128)(2,1)S(1)} %fusion.90), channel_id=1, source_target_pairs={{0,8},{8,0},{1,9},{9,1},{2,10},{10,2},{3,11},{11,3},{4,12},{12,4},... | collective-permute-start | bytes 196616 | tf_op jit(solution)/shard_map/ppermute | solution.py:18
  93.5 1.8 fusion.61
  95.9 7.1 %all-to-all-start.4 = ((bf16[16,8,256]{2,1,0:T(8,128)(2,1)}), bf16[16,8,256]{2,1,0:T(8,128)(2,1)}, u32[]{:S(2)}, u32[]{:S(2)}) async-start(bf16[16,8,256]{2,1,0:T(8,128)(2,1)} %fusion.89), calls=%async_computation.4 | async-start | bytes 131072 | tf_op jit(solution)/shard_map/all_to_all | solution.py:22
  103.0 2.6 %fusion.58 = bf16[16,72,256]{2,1,0:T(8,128)(2,1)} fusion(s32[]{:T(128)S(6)} %select_n.23, f32[1,16,72,256]{3,2,1,0:T(8,128)} %convolution_bitcast_fusion.1, f32[1,16,72,256]{3,2,1,0:T(8,128)} %copy-done.5, bf16[16,72,256]{2,1,0:T(8,128)(2,1)} %collective-permute-done), kind=kLoop, calls=%fused_computation.139 | loop fusion | flops 1179648 | bytes 3538948 | tf_op jit(solution)/shard_map/convert_element_type | solution.py:35
  105.6 5.3 %all-to-all-done.4 = bf16[16,8,256]{2,1,0:T(8,128)(2,1)} async-done(((bf16[16,8,256]{2,1,0:T(8,128)(2,1)}), bf16[16,8,256]{2,1,0:T(8,128)(2,1)}, u32[]{:S(2)}, u32[]{:S(2)}) %all-to-all-start.4) | async-done | bytes 65568 | tf_op jit(solution)/shard_map/all_to_all | solution.py:22
  110.9 4.2 %all-to-all-start.3 = ((bf16[16,72,256]{2,1,0:T(8,128)(2,1)}), bf16[16,72,256]{2,1,0:T(8,128)(2,1)}, u32[]{:S(2)}, u32[]{:S(2)}) async-start(bf16[16,72,256]{2,1,0:T(8,128)(2,1)} %fusion.58), calls=%async_computation.3 | async-start | bytes 1179648 | tf_op jit(solution)/shard_map/all_to_all | solution.py:22
  115.1 1.2 slice_bitcast_fusion.3
  116.3 1.5 convert_reduce_fusion.4
  117.8 8.0 %all-to-all-done.3 = bf16[16,72,256]{2,1,0:T(8,128)(2,1)} async-done(((bf16[16,72,256]{2,1,0:T(8,128)(2,1)}), bf16[16,72,256]{2,1,0:T(8,128)(2,1)}, u32[]{:S(2)}, u32[]{:S(2)}) %all-to-all-start.3) | async-done | bytes 589856 | tf_op jit(solution)/shard_map/all_to_all | solution.py:22
  125.8 1.2 convert_reduce_fusion
  127.0 0.7 pad_maximum_fusion.7
  127.7 0.8 broadcast_in_dim.6
  128.4 6.0 %all-to-all-start.5 = ((f32[4,80,256]{2,1,0:T(8,128)}), f32[4,80,256]{2,1,0:T(8,128)}, u32[]{:S(2)}, u32[]{:S(2)}) async-start(f32[4,80,256]{2,1,0:T(8,128)} %broadcast_in_dim.6), calls=%async_computation.5 | async-start | bytes 655360 | tf_op jit(solution)/shard_map/all_to_all | solution.py:22
  134.5 3.6 %fusion.59 = (bf16[72,4,1152]{2,1,0:T(4,128)(2,1)}, bf16[72,4,1152]{2,1,0:T(4,128)(2,1)}) fusion(bf16[48,8,1152]{2,1,0:T(8,128)(2,1)} %get-tuple-element.47, bf16[24,8,1152]{2,1,0:T(8,128)(2,1)} %get-tuple-element.49), kind=kLoop, calls=%fused_computation.144 | loop fusion | flops 663552 | bytes 2654208 | tf_op jit(solution)/shard_map/jit(_roll_static)/concatenate | solution.py:149
  138.0 1.6 fusion.82
  139.6 1.5 fusion.91
  141.3 1.6 reduce_sum.220
  142.9 1.5 broadcast_in_dim.7
  144.4 13.3 %all-to-all-start.6 = ((bf16[4,80,256]{2,1,0:T(8,128)(2,1)}), bf16[4,80,256]{2,1,0:T(8,128)(2,1)}, u32[]{:S(2)}, u32[]{:S(2)}) async-start(bf16[4,80,256]{2,1,0:T(8,128)(2,1)} %broadcast_in_dim.7), calls=%async_computation.6 | async-start | bytes 327680 | tf_op jit(solution)/shard_map/all_to_all | solution.py:22
  157.6 1.3 fusion.92
  158.9 14.4 %all-to-all-done.6 = bf16[4,80,256]{2,1,0:T(8,128)(2,1)} async-done(((bf16[4,80,256]{2,1,0:T(8,128)(2,1)}), bf16[4,80,256]{2,1,0:T(8,128)(2,1)}, u32[]{:S(2)}, u32[]{:S(2)}) %all-to-all-start.6) | async-done | bytes 163872 | tf_op jit(solution)/shard_map/all_to_all | solution.py:22
  173.3 0.9 convert_reduce_fusion.3
  174.3 1.0 broadcast_in_dim.8
  175.2 4.5 %all-to-all-start.7 = ((bf16[16,80,256]{2,1,0:T(8,128)(2,1)}), bf16[16,80,256]{2,1,0:T(8,128)(2,1)}, u32[]{:S(2)}, u32[]{:S(2)}) async-start(bf16[16,80,256]{2,1,0:T(8,128)(2,1)} %broadcast_in_dim.8), calls=%async_computation.7 | async-start | bytes 1310720 | tf_op jit(solution)/shard_map/all_to_all | solution.py:22
  179.7 11.5 %fusion.29 = bf16[72,8,1152]{2,1,0:T(8,128)(2,1)} fusion(bf16[36,8,1152]{2,1,0:T(8,128)(2,1)} %get-tuple-element.61, bf16[36,8,1152]{2,1,0:T(8,128)(2,1)} %get-tuple-element.60, bf16[48,8,1152]{2,1,0:T(8,128)(2,1)} %get-tuple-element.47, bf16[24,8,1152]{2,1,0:T(8,128)(2,1)} %get-tuple-element.49, bf16[24,8,1152]{2,1,0:T(8,128)(2,1)} %get-tuple-element.48, ...), kind=kLoop, calls=%fused_computation.76 | loop fusion | flops 39813120 | bytes 13353984 | tf_op jit(solution)/shard_map/convert_element_type | solution.py:154
  191.2 6.7 %all-to-all-start.2 = ((bf16[8,9,8,1152]{3,2,1,0:T(8,128)(2,1)}), bf16[8,9,8,1152]{3,2,1,0:T(8,128)(2,1)S(1)}, u32[]{:S(2)}, u32[]{:S(2)}) async-start(bf16[8,9,8,1152]{3,2,1,0:T(8,128)(2,1)} %bitcast.185), calls=%async_computation.2 | async-start | bytes 2654208 | tf_op jit(solution)/shard_map/all_to_all | solution.py:22
  197.9 1.9 collective-permute-start.2
  199.9 12.6 %all-to-all-done.2 = bf16[8,9,8,1152]{3,2,1,0:T(8,128)(2,1)S(1)} async-done(((bf16[8,9,8,1152]{3,2,1,0:T(8,128)(2,1)}), bf16[8,9,8,1152]{3,2,1,0:T(8,128)(2,1)S(1)}, u32[]{:S(2)}, u32[]{:S(2)}) %all-to-all-start.2) | async-done | bytes 1327136 | tf_op jit(solution)/shard_map/all_to_all | solution.py:22
  213.6 1.3 reshape.150
  214.9 1.2 select_bitcast_fusion.1
  216.1 1.1 pad_maximum_fusion.6
  (185 shorter events, 10.9 us)
Async XLA Ops:
  5.3 7.1 %copy-start.56 = (bf16[2,3,3,1152]{3,0,2,1:T(2,128)(2,1)S(1)}, bf16[2,3,3,1152]{3,0,2,1:T(2,128)(2,1)}, u32[]{:S(2)}) copy-start(bf16[2,3,3,1152]{3,0,2,1:T(2,128)(2,1)} %param.6) | copy-start | bytes 124420
  5.4 7.1 %copy-start.39 = (bf16[1,9,48,512]{3,2,1,0:T(8,128)(2,1)S(1)}, bf16[1,9,48,512]{3,2,1,0:T(8,128)(2,1)}, u32[]{:S(2)}) copy-start(bf16[1,9,48,512]{3,2,1,0:T(8,128)(2,1)} %param.9) | copy-start | bytes 1327108
  5.4 27.3 %all-to-all-start.1 = ((bf16[8,9,8,1152]{3,2,1,0:T(8,128)(2,1)}), bf16[8,9,8,1152]{3,2,1,0:T(8,128)(2,1)S(1)}, u32[]{:S(2)}, u32[]{:S(2)}) async-start(bf16[8,9,8,1152]{3,2,1,0:T(8,128)(2,1)} %pad.93), calls=%async_computation.1 | async-start | bytes 2654208 | tf_op jit(solution)/shard_map/all_to_all | solution.py:22
  12.6 2.2 copy-start.65
  32.6 17.0 %all-to-all-start = ((bf16[8,9,8,512]{3,2,1,0:T(8,128)(2,1)}), bf16[8,9,8,512]{3,2,1,0:T(8,128)(2,1)}, u32[]{:S(2)}, u32[]{:S(2)}) async-start(bf16[8,9,8,512]{3,2,1,0:T(8,128)(2,1)} %pad.92), calls=%async_computation | async-start | bytes 1179648 | tf_op jit(solution)/shard_map/all_to_all | solution.py:22
  37.2 2.3 %copy-start.2 = (bf16[48,8,1152]{2,1,0:T(8,128)(2,1)}, bf16[48,8,1152]{2,1,0:T(8,128)(2,1)S(1)}, u32[]{:S(2)}) copy-start(bf16[48,8,1152]{2,1,0:T(8,128)(2,1)S(1)} %get-tuple-element.55) | copy-start | bytes 2654212
  37.3 2.2 %copy-start.9 = (bf16[24,8,1152]{2,1,0:T(8,128)(2,1)}, bf16[24,8,1152]{2,1,0:T(8,128)(2,1)S(1)}, u32[]{:S(2)}) copy-start(bf16[24,8,1152]{2,1,0:T(8,128)(2,1)S(1)} %get-tuple-element.52) | copy-start | bytes 1327108
  37.3 2.2 %copy-start.11 = (bf16[24,8,1152]{2,1,0:T(8,128)(2,1)}, bf16[24,8,1152]{2,1,0:T(8,128)(2,1)S(1)}, u32[]{:S(2)}) copy-start(bf16[24,8,1152]{2,1,0:T(8,128)(2,1)S(1)} %get-tuple-element.53) | copy-start | bytes 1327108
  37.7 3.2 %copy-start.47 = (f32[1152]{0:T(1024)S(1)}, f32[1152]{0:T(1024)}, u32[]{:S(2)}) copy-start(f32[1152]{0:T(1024)} %get-tuple-element.18) | copy-start | bytes 13828
  37.8 3.2 %copy-start.48 = (f32[1152]{0:T(1024)S(1)}, f32[1152]{0:T(1024)}, u32[]{:S(2)}) copy-start(f32[1152]{0:T(1024)} %get-tuple-element.28) | copy-start | bytes 13828
  37.8 3.2 %copy-start.49 = (f32[1152]{0:T(1024)S(1)}, f32[1152]{0:T(1024)}, u32[]{:S(2)}) copy-start(f32[1152]{0:T(1024)} %get-tuple-element.29) | copy-start | bytes 13828
  37.8 3.2 %copy-start.50 = (f32[1152]{0:T(1024)S(1)}, f32[1152]{0:T(1024)}, u32[]{:S(2)}) copy-start(f32[1152]{0:T(1024)} %get-tuple-element.30) | copy-start | bytes 13828
  37.8 3.1 %copy-start.51 = (f32[1152]{0:T(1024)S(1)}, f32[1152]{0:T(1024)}, u32[]{:S(2)}) copy-start(f32[1152]{0:T(1024)} %get-tuple-element.31) | copy-start | bytes 13828
  37.8 3.1 %copy-start.52 = (f32[1152]{0:T(1024)S(1)}, f32[1152]{0:T(1024)}, u32[]{:S(2)}) copy-start(f32[1152]{0:T(1024)} %get-tuple-element.32) | copy-start | bytes 13828
  37.8 3.1 %copy-start.53 = (f32[1152]{0:T(1024)S(1)}, f32[1152]{0:T(1024)}, u32[]{:S(2)}) copy-start(f32[1152]{0:T(1024)} %get-tuple-element.33) | copy-start | bytes 13828
  37.8 3.1 %copy-start.54 = (f32[1152]{0:T(1024)S(1)}, f32[1152]{0:T(1024)}, u32[]{:S(2)}) copy-start(f32[1152]{0:T(1024)} %get-tuple-element.34) | copy-start | bytes 13828
  37.8 3.1 %copy-start.55 = (f32[1152]{0:T(1024)S(1)}, f32[1152]{0:T(1024)}, u32[]{:S(2)}) copy-start(f32[1152]{0:T(1024)} %get-tuple-element.35) | copy-start | bytes 13828
  47.0 2.7 %copy-start.17 = (bf16[576,1152]{1,0:T(8,128)(2,1)S(1)}, bf16[576,1152]{1,0:T(8,128)(2,1)}, u32[]{:S(2)}) copy-start(bf16[576,1152]{1,0:T(8,128)(2,1)} %fusion.52) | copy-start | bytes 3981316
  49.7 2.6 %copy-start.20 = (bf16[72,4,1152]{2,1,0:T(4,128)(2,1)S(1)}, bf16[72,4,1152]{2,1,0:T(4,128)(2,1)}, u32[]{:S(2)}) copy-start(bf16[72,4,1152]{2,1,0:T(4,128)(2,1)} %copy-done.19) | copy-start | bytes 1990660
  49.7 2.6 %copy-start.22 = (bf16[72,4,1152]{2,1,0:T(4,128)(2,1)S(1)}, bf16[72,4,1152]{2,1,0:T(4,128)(2,1)}, u32[]{:S(2)}) copy-start(bf16[72,4,1152]{2,1,0:T(4,128)(2,1)} %copy-done.21) | copy-start | bytes 1990660
  49.7 2.6 %copy-start.24 = (bf16[72,4,1152]{2,1,0:T(4,128)(2,1)S(1)}, bf16[72,4,1152]{2,1,0:T(4,128)(2,1)}, u32[]{:S(2)}) copy-start(bf16[72,4,1152]{2,1,0:T(4,128)(2,1)} %copy-done.23) | copy-start | bytes 1990660
  49.7 2.6 %copy-start.26 = (bf16[72,4,1152]{2,1,0:T(4,128)(2,1)S(1)}, bf16[72,4,1152]{2,1,0:T(4,128)(2,1)}, u32[]{:S(2)}) copy-start(bf16[72,4,1152]{2,1,0:T(4,128)(2,1)} %copy-done.25) | copy-start | bytes 1990660
  49.7 2.6 %copy-start.28 = (bf16[72,4,1152]{2,1,0:T(4,128)(2,1)S(1)}, bf16[72,4,1152]{2,1,0:T(4,128)(2,1)}, u32[]{:S(2)}) copy-start(bf16[72,4,1152]{2,1,0:T(4,128)(2,1)} %copy-done.27) | copy-start | bytes 1990660
  49.7 2.6 %copy-start.30 = (bf16[72,4,1152]{2,1,0:T(4,128)(2,1)S(1)}, bf16[72,4,1152]{2,1,0:T(4,128)(2,1)}, u32[]{:S(2)}) copy-start(bf16[72,4,1152]{2,1,0:T(4,128)(2,1)} %copy-done.29) | copy-start | bytes 1990660
  49.7 2.7 %copy-start.67 = (bf16[2,1152,256]{2,1,0:T(8,128)(2,1)S(1)}, bf16[2,1152,256]{2,1,0:T(8,128)(2,1)}, u32[]{:S(2)}) copy-start(bf16[2,1152,256]{2,1,0:T(8,128)(2,1)} %param.7) | copy-start | bytes 3538948
  52.5 3.7 %copy-start.3 = (bf16[48,8,1152]{2,1,0:T(8,128)(2,1)S(1)}, bf16[48,8,1152]{2,1,0:T(8,128)(2,1)}, u32[]{:S(2)}) copy-start(bf16[48,8,1152]{2,1,0:T(8,128)(2,1)} %copy-done.2) | copy-start | bytes 2654212
  52.5 3.7 %copy-start.10 = (bf16[24,8,1152]{2,1,0:T(8,128)(2,1)S(1)}, bf16[24,8,1152]{2,1,0:T(8,128)(2,1)}, u32[]{:S(2)}) copy-start(bf16[24,8,1152]{2,1,0:T(8,128)(2,1)} %copy-done.9) | copy-start | bytes 1327108
  52.5 3.7 %copy-start.12 = (bf16[24,8,1152]{2,1,0:T(8,128)(2,1)S(1)}, bf16[24,8,1152]{2,1,0:T(8,128)(2,1)}, u32[]{:S(2)}) copy-start(bf16[24,8,1152]{2,1,0:T(8,128)(2,1)} %copy-done.11) | copy-start | bytes 1327108
  62.2 1.9 copy-start.6
  62.2 3.0 %copy-start.40 = (f32[1152]{0:T(1024)S(1)}, f32[1152]{0:T(1024)}, u32[]{:S(2)}) copy-start(f32[1152]{0:T(1024)} %get-tuple-element.21) | copy-start | bytes 13828
  62.2 3.0 %copy-start.41 = (f32[1152]{0:T(1024)S(1)}, f32[1152]{0:T(1024)}, u32[]{:S(2)}) copy-start(f32[1152]{0:T(1024)} %get-tuple-element.22) | copy-start | bytes 13828
  62.3 2.9 %copy-start.42 = (f32[1152]{0:T(1024)S(1)}, f32[1152]{0:T(1024)}, u32[]{:S(2)}) copy-start(f32[1152]{0:T(1024)} %get-tuple-element.23) | copy-start | bytes 13828
  62.3 2.9 %copy-start.43 = (f32[1152]{0:T(1024)S(1)}, f32[1152]{0:T(1024)}, u32[]{:S(2)}) copy-start(f32[1152]{0:T(1024)} %get-tuple-element.24) | copy-start | bytes 13828
  62.3 2.9 %copy-start.44 = (f32[1152]{0:T(1024)S(1)}, f32[1152]{0:T(1024)}, u32[]{:S(2)}) copy-start(f32[1152]{0:T(1024)} %get-tuple-element.25) | copy-start | bytes 13828
  62.3 2.9 %copy-start.45 = (f32[1152]{0:T(1024)S(1)}, f32[1152]{0:T(1024)}, u32[]{:S(2)}) copy-start(f32[1152]{0:T(1024)} %get-tuple-element.26) | copy-start | bytes 13828
  62.3 2.9 %copy-start.46 = (f32[1152]{0:T(1024)S(1)}, f32[1152]{0:T(1024)}, u32[]{:S(2)}) copy-start(f32[1152]{0:T(1024)} %get-tuple-element.27) | copy-start | bytes 13828
  69.9 2.6 %copy-start.66 = (f32[1,256]{1,0:T(1,128)S(1)}, f32[1,256]{1,0:T(1,128)}, u32[]{:S(2)}) copy-start(f32[1,256]{1,0:T(1,128)} %get-tuple-element.71) | copy-start | bytes 3076
  72.5 3.0 %copy-start.32 = (bf16[72,2,1152]{2,1,0:T(2,128)(2,1)S(1)}, bf16[72,2,1152]{2,1,0:T(2,128)(2,1)}, u32[]{:S(2)}) copy-start(bf16[72,2,1152]{2,1,0:T(2,128)(2,1)} %copy-done.31) | copy-start | bytes 995332
  72.5 3.0 %copy-start.34 = (bf16[72,2,1152]{2,1,0:T(2,128)(2,1)S(1)}, bf16[72,2,1152]{2,1,0:T(2,128)(2,1)}, u32[]{:S(2)}) copy-start(bf16[72,2,1152]{2,1,0:T(2,128)(2,1)} %copy-done.33) | copy-start | bytes 995332
  72.5 3.0 %copy-start.36 = (bf16[72,2,1152]{2,1,0:T(2,128)(2,1)S(1)}, bf16[72,2,1152]{2,1,0:T(2,128)(2,1)}, u32[]{:S(2)}) copy-start(bf16[72,2,1152]{2,1,0:T(2,128)(2,1)} %copy-done.35) | copy-start | bytes 995332
  72.5 3.0 %copy-start.38 = (bf16[72,2,1152]{2,1,0:T(2,128)(2,1)S(1)}, bf16[72,2,1152]{2,1,0:T(2,128)(2,1)}, u32[]{:S(2)}) copy-start(bf16[72,2,1152]{2,1,0:T(2,128)(2,1)} %copy-done.37) | copy-start | bytes 995332
  72.6 3.0 %copy-start.68 = (bf16[2,1152,256]{2,1,0:T(8,128)(2,1)S(1)}, bf16[2,1152,256]{2,1,0:T(8,128)(2,1)}, u32[]{:S(2)}) copy-start(bf16[2,1152,256]{2,1,0:T(8,128)(2,1)} %param.7) | copy-start | bytes 3538948
  75.5 2.6 %copy-start.16 = (bf16[576,1152]{0,1:T(8,128)(2,1)S(1)}, bf16[576,1152]{0,1:T(8,128)(2,1)}, u32[]{:S(2)}) copy-start(bf16[576,1152]{0,1:T(8,128)(2,1)} %copy.25) | copy-start | bytes 3981316
  78.1 6.1 %copy-start = (bf16[576,1152]{1,0:T(8,128)(2,1)}, bf16[576,1152]{1,0:T(8,128)(2,1)S(1)}, u32[]{:S(2)}) copy-start(bf16[576,1152]{1,0:T(8,128)(2,1)S(1)} %get-tuple-element.76) | copy-start | bytes 3981316
  79.9 3.2 %copy-start.64 = (f32[1152]{0:T(1024)S(1)}, f32[1152]{0:T(1024)}, u32[]{:S(2)}) copy-start(f32[1152]{0:T(1024)} %get-tuple-element.4) | copy-start | bytes 13828
  79.9 3.2 %copy-start.63 = (f32[1152]{0:T(1024)S(1)}, f32[1152]{0:T(1024)}, u32[]{:S(2)}) copy-start(f32[1152]{0:T(1024)} %get-tuple-element.9) | copy-start | bytes 13828
  79.9 3.2 %copy-start.62 = (f32[1152]{0:T(1024)S(1)}, f32[1152]{0:T(1024)}, u32[]{:S(2)}) copy-start(f32[1152]{0:T(1024)} %get-tuple-element.8) | copy-start | bytes 13828
  79.9 3.2 %copy-start.58 = (f32[1152]{0:T(1024)S(1)}, f32[1152]{0:T(1024)}, u32[]{:S(2)}) copy-start(f32[1152]{0:T(1024)} %get-tuple-element.10) | copy-start | bytes 13828
  79.9 3.2 %copy-start.57 = (f32[1152]{0:T(1024)S(1)}, f32[1152]{0:T(1024)}, u32[]{:S(2)}) copy-start(f32[1152]{0:T(1024)} %get-tuple-element.11) | copy-start | bytes 13828
  79.9 3.3 %copy-start.7 = (bf16[4,9,8,1152]{3,2,1,0:T(8,128)(2,1)S(1)}, bf16[4,9,8,1152]{3,2,1,0:T(8,128)(2,1)}, u32[]{:S(2)}) copy-start(bf16[4,9,8,1152]{3,2,1,0:T(8,128)(2,1)} %copy-done.6) | copy-start | bytes 1990660
  81.2 21.8 %collective-permute-start = (bf16[16,72,256]{2,1,0:T(8,128)(2,1)}, bf16[16,72,256]{2,1,0:T(8,128)(2,1)}, u32[]{:S(2)}, u32[]{:S(2)}) collective-permute-start(bf16[16,72,256]{2,1,0:T(8,128)(2,1)} %fusion.67), channel_id=1, source_target_pairs={{0,8},{8,0},{1,9},{9,1},{2,10},{10,2},{3,11},{11,3},{4,12},{12,4},... | collective-permute-start | bytes 1769480 | tf_op jit(solution)/shard_map/ppermute | solution.py:18
  85.5 8.0 %copy-start.8 = (bf16[48,8,1152]{2,1,0:T(8,128)(2,1)S(1)}, bf16[48,8,1152]{2,1,0:T(8,128)(2,1)}, u32[]{:S(2)}) copy-start(bf16[48,8,1152]{2,1,0:T(8,128)(2,1)} %get-tuple-element.46) | copy-start | bytes 2654212
  85.5 8.0 %copy-start.18 = (bf16[24,8,1152]{2,1,0:T(8,128)(2,1)S(1)}, bf16[24,8,1152]{2,1,0:T(8,128)(2,1)}, u32[]{:S(2)}) copy-start(bf16[24,8,1152]{2,1,0:T(8,128)(2,1)} %get-tuple-element.48) | copy-start | bytes 1327108
  91.0 4.2 %collective-permute-start.1 = (bf16[16,8,256]{2,1,0:T(8,128)(2,1)S(1)}, bf16[16,8,256]{2,1,0:T(8,128)(2,1)S(1)}, u32[]{:S(2)}, u32[]{:S(2)}) collective-permute-start(bf16[16,8,256]{2,1,0:T(8,128)(2,1)S(1)} %fusion.90), channel_id=1, source_target_pairs={{0,8},{8,0},{1,9},{9,1},{2,10},{10,2},{3,11},{11,3},{4,12},{12,4},... | collective-permute-start | bytes 196616 | tf_op jit(solution)/shard_map/ppermute | solution.py:18
  95.9 15.0 %all-to-all-start.4 = ((bf16[16,8,256]{2,1,0:T(8,128)(2,1)}), bf16[16,8,256]{2,1,0:T(8,128)(2,1)}, u32[]{:S(2)}, u32[]{:S(2)}) async-start(bf16[16,8,256]{2,1,0:T(8,128)(2,1)} %fusion.89), calls=%async_computation.4 | async-start | bytes 131072 | tf_op jit(solution)/shard_map/all_to_all | solution.py:22
  103.0 12.1 %copy-start.1 = (bf16[576,1152]{1,0:T(8,128)(2,1)S(1)}, bf16[576,1152]{1,0:T(8,128)(2,1)}, u32[]{:S(2)}) copy-start(bf16[576,1152]{1,0:T(8,128)(2,1)} %copy-done) | copy-start | bytes 3981316
  110.9 14.9 %all-to-all-start.3 = ((bf16[16,72,256]{2,1,0:T(8,128)(2,1)}), bf16[16,72,256]{2,1,0:T(8,128)(2,1)}, u32[]{:S(2)}, u32[]{:S(2)}) async-start(bf16[16,72,256]{2,1,0:T(8,128)(2,1)} %fusion.58), calls=%async_computation.3 | async-start | bytes 1179648 | tf_op jit(solution)/shard_map/all_to_all | solution.py:22
  128.4 12.9 %all-to-all-start.5 = ((f32[4,80,256]{2,1,0:T(8,128)}), f32[4,80,256]{2,1,0:T(8,128)}, u32[]{:S(2)}, u32[]{:S(2)}) async-start(f32[4,80,256]{2,1,0:T(8,128)} %broadcast_in_dim.6), calls=%async_computation.5 | async-start | bytes 655360 | tf_op jit(solution)/shard_map/all_to_all | solution.py:22
  134.5 3.6 %copy-start.13 = (bf16[36,8,1152]{2,1,0:T(8,128)(2,1)S(1)}, bf16[36,8,1152]{2,1,0:T(8,128)(2,1)}, u32[]{:S(2)}) copy-start(bf16[36,8,1152]{2,1,0:T(8,128)(2,1)} %get-tuple-element.60) | copy-start | bytes 1990660
  134.5 3.6 %copy-start.14 = (bf16[36,8,1152]{2,1,0:T(8,128)(2,1)S(1)}, bf16[36,8,1152]{2,1,0:T(8,128)(2,1)}, u32[]{:S(2)}) copy-start(bf16[36,8,1152]{2,1,0:T(8,128)(2,1)} %get-tuple-element.61) | copy-start | bytes 1990660
  144.4 28.9 %all-to-all-start.6 = ((bf16[4,80,256]{2,1,0:T(8,128)(2,1)}), bf16[4,80,256]{2,1,0:T(8,128)(2,1)}, u32[]{:S(2)}, u32[]{:S(2)}) async-start(bf16[4,80,256]{2,1,0:T(8,128)(2,1)} %broadcast_in_dim.7), calls=%async_computation.6 | async-start | bytes 327680 | tf_op jit(solution)/shard_map/all_to_all | solution.py:22
  175.2 16.0 %all-to-all-start.7 = ((bf16[16,80,256]{2,1,0:T(8,128)(2,1)}), bf16[16,80,256]{2,1,0:T(8,128)(2,1)}, u32[]{:S(2)}, u32[]{:S(2)}) async-start(bf16[16,80,256]{2,1,0:T(8,128)(2,1)} %broadcast_in_dim.8), calls=%async_computation.7 | async-start | bytes 1310720 | tf_op jit(solution)/shard_map/all_to_all | solution.py:22
  191.2 21.2 %all-to-all-start.2 = ((bf16[8,9,8,1152]{3,2,1,0:T(8,128)(2,1)}), bf16[8,9,8,1152]{3,2,1,0:T(8,128)(2,1)S(1)}, u32[]{:S(2)}, u32[]{:S(2)}) async-start(bf16[8,9,8,1152]{3,2,1,0:T(8,128)(2,1)} %bitcast.185), calls=%async_computation.2 | async-start | bytes 2654208 | tf_op jit(solution)/shard_map/all_to_all | solution.py:22
  197.9 17.0 %collective-permute-start.2 = (bf16[16,80,256]{2,1,0:T(8,128)(2,1)}, bf16[16,80,256]{2,1,0:T(8,128)(2,1)S(1)}, u32[]{:S(2)}, u32[]{:S(2)}) collective-permute-start(bf16[16,80,256]{2,1,0:T(8,128)(2,1)} %all-to-all-done.7), channel_id=1, source_target_pairs={{0,8},{8,0},{1,9},{9,1},{2,10},{10,2},{3,11},{11,3},{4,12},{12,4},... | collective-permute-start | bytes 1966088 | tf_op jit(solution)/shard_map/ppermute | solution.py:18
  (16 other events, 20.3 us)

commit v3 on v2

v3 whole, which is shorter than its diff:
```python
import jax
import jax.numpy as jnp
from jax import lax
from jax.experimental import pallas as pl
from jax.experimental.pallas import tpu as pltpu
from jax.sharding import Mesh
from jax.sharding import PartitionSpec as P

CLASS = 12
PAIR = 2
HELD = 8
LANES = 128

DP = ("zh", "zl", "xl", "core")
LON = ("y", "xh")
PLANE = ("xl", "y", "xh")


def swap_cores(block):
    return lax.ppermute(block, "core", [(0, 1), (1, 0)])


def exchange(blocks, axes):
    return lax.all_to_all(blocks, axes, 0, 0, tiled=True)


def gather_copies(block, axes):
    peers = lax.axis_size(axes)
    return exchange(jnp.broadcast_to(block[None], (peers,) + block.shape), axes)


def sum_four(own, axis):
    near, far, last = [
        lax.ppermute(own, axis, [(i, i ^ m) for i in range(4)]).astype(jnp.float32) for m in (1, 2, 3)
    ]
    return (own.astype(jnp.float32) + near) + (far + last)


def gate_slope(pre_act):
    sigmoid_val = jax.nn.sigmoid(pre_act)
    return sigmoid_val * (1.0 + pre_act * (1.0 - sigmoid_val))


def half_turn(tile):
    return pltpu.roll(tile, 4, 0)


def ends_swapped(tile, top):
    return jnp.where(top, pltpu.roll(tile, 2, 0), pltpu.roll(tile, 6, 0))


def shard_row(row, main, extra):
    return (row // extra) * (main + extra) + main + row % extra


def local_body(core_ref, cls_ref, taps_ref, pw_ref, pb_ref, kept_ref, sent_ref, fg_ref, depth, dgr, terms):
    channels, outputs = pw_ref.shape[1:]
    shard = terms.shape[1] // 16
    main = channels // 16
    extra = shard - main
    tiles = channels // LANES
    wide = outputs // LANES
    per_tap = -(-tiles // wide)
    sub = lax.broadcasted_iota(jnp.int32, (HELD, LANES), 0)
    top = sub < 4
    first = sub < 2
    end = sub >= 6

    def tap(branch, a, e, lanes):
        row = branch * 9 + (a + 1) * 3 + e + 1
        return jnp.broadcast_to(taps_ref[row : row + 1, lanes], (HELD, LANES))

    def ends(up, down):
        return jnp.where(first, up, jnp.where(end, down, 0.0))

    def both(branch, a, lanes):
        return tap(branch, a, -1, lanes) + tap(branch, a, 1, lanes)

    def read(ref, step, lanes, branch=None):
        out = []
        for k in range(6):
            rows = pl.ds(pl.multiple_of(k * 96 + step * 16, 16), 16)
            tile = (ref[rows, lanes] if branch is None else ref[branch, rows, lanes]).astype(jnp.float32)
            out.append((tile[:HELD], tile[HELD:]))
        return [[pair[h] for pair in out] for h in range(2)]

    for t in range(tiles):
        lanes = slice(t * LANES, (t + 1) * LANES)
        mid_a = [tap(0, 0, e, lanes) for e in (-1, 0, 1)]
        off_a = [jnp.where(top, tap(0, 1, e, lanes), tap(0, -1, e, lanes)) for e in (-1, 0, 1)]
        mid_b = [tap(1, 0, 0, lanes), both(1, 0, lanes)]
        off_b = [
            ends(tap(1, 1, 0, lanes), tap(1, -1, 0, lanes)),
            ends(both(1, 1, lanes), both(1, -1, lanes)),
        ]

        def forward(step, carry):
            made_a, made_b = [], []
            for xs in read(cls_ref, step, lanes):
                turned = [half_turn(x) for x in xs]
                swapped = [ends_swapped(x, top) for x in xs]
                made_a.append(
                    [
                        sum(
                            mid_a[n] * xs[(k + 2 * n - 2) % 6] + off_a[n] * turned[(k + 2 * n - 2) % 6]
                            for n in range(3)
                        )
                        for k in range(6)
                    ]
                )
                made_b.append(
                    [
                        mid_b[0] * xs[k]
                        + mid_b[1] * xs[(k + 3) % 6]
                        + off_b[0] * swapped[k]
                        + off_b[1] * swapped[(k + 3) % 6]
                        for k in range(6)
                    ]
                )
            for k in range(6):
                rows = pl.ds(pl.multiple_of(k * 96 + step * 16, 16), 16)
                for branch, made in enumerate((made_a, made_b)):
                    tile = jnp.concatenate([made[0][k], made[1][k]], axis=0)
                    depth[branch, rows, lanes] = tile.astype(jnp.bfloat16)
            return carry

        lax.fori_loop(0, 6, forward, 0)

    for branch in range(2):
        act = jnp.dot(depth[branch], pw_ref[branch], preferred_element_type=jnp.float32)
        act = act + pb_ref[branch : branch + 1, :]
        start = channels + branch * outputs
        up = cls_ref[:, start : start + outputs].astype(jnp.float32)
        pgrad = (up * gate_slope(act)).astype(jnp.bfloat16)
        point = lax.dot_general(
            depth[branch], pgrad, (((0,), (0,)), ((), ())), preferred_element_type=jnp.float32
        )
        for p in range(16):
            terms[branch, p * shard : p * shard + main, :] = point[p * main : (p + 1) * main]
            terms[branch, p * shard + main : (p + 1) * shard, :] = jnp.zeros((extra, outputs), jnp.float32)
        row = shard_row(9 * per_tap, main, extra)
        terms[branch, row : row + 1, :] = jnp.sum(pgrad.astype(jnp.float32), axis=0, keepdims=True)
        for c in range(0, channels, 384):
            part = lax.dot_general(
                pgrad, pw_ref[branch, c : c + 384, :], (((1,), (1,)), ((), ())), preferred_element_type=jnp.float32
            )
            dgr[branch, :, c : c + 384] = part.astype(jnp.bfloat16)

    for t in range(tiles):
        lanes = slice(t * LANES, (t + 1) * LANES)
        mid_a = [tap(0, 0, e, lanes) for e in (-1, 0, 1)]
        off_a = [jnp.where(top, tap(0, -1, e, lanes), tap(0, 1, e, lanes)) for e in (-1, 0, 1)]
        mid_b = [tap(1, 0, 0, lanes), both(1, 0, lanes)]
        off_b = [
            ends(tap(1, -1, 0, lanes), tap(1, 1, 0, lanes)),
            ends(both(1, -1, lanes), both(1, 1, lanes)),
        ]

        def backward(step, sums):
            sums = list(sums)
            made = []
            sides = zip(read(cls_ref, step, lanes), read(dgr, step, lanes, 0), read(dgr, step, lanes, 1))
            for xs, das, dbs in sides:
                turned = [half_turn(d) for d in das]
                swapped = [ends_swapped(d, top) for d in dbs]
                made.append(
                    [
                        sum(
                            mid_a[n] * das[(k - 2 * n + 2) % 6] + off_a[n] * turned[(k - 2 * n + 2) % 6]
                            for n in range(3)
                        )
                        + mid_b[0] * dbs[k]
                        + mid_b[1] * dbs[(k + 3) % 6]
                        + off_b[0] * swapped[k]
                        + off_b[1] * swapped[(k + 3) % 6]
                        for k in range(6)
                    ]
                )
                for n in range(3):
                    sums[n] += sum(xs[(k + 2 * n - 2) % 6] * das[k] for k in range(6))
                    sums[3 + n] += sum(xs[(k + 2 * n - 2) % 6] * turned[k] for k in range(6))
                for n in range(2):
                    sums[6 + n] += sum(xs[(k + 3 * n) % 6] * dbs[k] for k in range(6))
                    sums[8 + n] += sum(xs[(k + 3 * n) % 6] * swapped[k] for k in range(6))
            for k in range(6):
                rows = pl.ds(pl.multiple_of(k * 96 + step * 16, 16), 16)
                fg_ref[rows, lanes] = jnp.concatenate([made[0][k], made[1][k]], axis=0).astype(jnp.bfloat16)
            return tuple(sums)

        sums = lax.fori_loop(0, 6, backward, tuple(jnp.zeros((HELD, LANES), jnp.float32) for _ in range(10)))

        def keep(branch, a, e, value, mask=None):
            value = value if mask is None else jnp.where(mask, value, 0.0)
            row = shard_row(((a + 1) * 3 + e + 1) * per_tap + t // wide, main, extra)
            at = (t % wide) * LANES
            terms[branch, row : row + 1, at : at + LANES] = jnp.sum(value, axis=0, keepdims=True)

        for n in range(3):
            keep(0, 0, n - 1, sums[n])
            keep(0, 1, n - 1, sums[3 + n], jnp.logical_not(top))
            keep(0, -1, n - 1, sums[3 + n], top)
        for e in (-1, 0, 1):
            keep(1, 0, e, sums[6 + abs(e)])
            keep(1, 1, e, sums[8 + abs(e)], end)
            keep(1, -1, e, sums[8 + abs(e)], first)

    @pl.when(core_ref[0] == 0)
    def _():
        kept_ref[...] = terms[0]
        sent_ref[...] = terms[1].astype(jnp.bfloat16)

    @pl.when(core_ref[0] != 0)
    def _():
        kept_ref[...] = terms[1]
        sent_ref[...] = terms[0].astype(jnp.bfloat16)


def local_work(core, field, taps, point_w, point_bias):
    cells = field.shape[0]
    branches, channels, outputs = point_w.shape
    rows = 16 * (channels // 16 + 8)
    vmem = pl.BlockSpec(memory_space=pltpu.VMEM)
    return pl.pallas_call(
        local_body,
        out_shape=(
            jax.ShapeDtypeStruct((rows, outputs), jnp.float32),
            jax.ShapeDtypeStruct((rows, outputs), jnp.bfloat16),
            jax.ShapeDtypeStruct((cells, channels), jnp.bfloat16),
        ),
        in_specs=[pl.BlockSpec(memory_space=pltpu.SMEM)] + [vmem] * 4,
        out_specs=(vmem, vmem, vmem),
        scratch_shapes=[
            pltpu.VMEM((branches, cells, channels), jnp.bfloat16),
            pltpu.VMEM((branches, cells, channels), jnp.bfloat16),
            pltpu.VMEM((branches, rows, outputs), jnp.float32),
        ],
        compiler_params=pltpu.CompilerParams(vmem_limit_bytes=48 << 20),
        name="local_work",
    )(core, field, taps, point_w, point_bias)


def to_chunks(field):
    _, columns, rows, width = field.shape
    groups = CLASS // PAIR
    chunks = field.reshape(columns, rows // CLASS, groups, PAIR, width).transpose(2, 0, 1, 3, 4)
    return chunks.reshape(groups, columns, rows // groups, width)


def per_device(features, depth_w, point_w, point_bias, cotangent):
    _, columns, rows, channels = features.shape
    branches, _, outputs = point_w.shape
    images = lax.axis_size(DP) * features.shape[0]
    peers = lax.axis_size(LON)
    plane = lax.axis_size(PLANE)
    groups = CLASS // PAIR
    core = lax.axis_index("core")

    chunks = jnp.concatenate([to_chunks(features), to_chunks(cotangent)], axis=3)
    chunks = jnp.pad(chunks, ((0, peers - groups), (0, 0), (0, 0), (0, 0)))
    field = exchange(chunks, LON).reshape(peers * columns * HELD, chunks.shape[3])
    taps = depth_w.astype(jnp.float32).reshape(branches * 9, channels)
    kept, sent, fgrad = local_work(core.reshape(1), field, taps, point_w, point_bias)

    terms = (kept + swap_cores(sent).astype(jnp.float32)).astype(jnp.bfloat16)
    shard = terms.shape[0] // plane
    terms = exchange(terms.reshape(plane, shard, outputs), PLANE)
    fgrad, terms = lax.optimization_barrier((fgrad, terms))
    fgrad = exchange(fgrad.reshape(peers, columns, HELD, channels), LON)
    terms = jnp.sum(terms.astype(jnp.float32), axis=0)
    terms = sum_four(terms, "zl").astype(jnp.bfloat16)
    total = (sum_four(terms, "zh") / images).astype(jnp.bfloat16)
    fgrad, total = lax.optimization_barrier((fgrad, total))
    total = gather_copies(total, PLANE)
    other = swap_cores(total)
    total = jnp.stack([jnp.where(core == 0, total, other), jnp.where(core == 0, other, total)])

    main = channels // plane
    point_grad = total[:, :, :main].reshape(point_w.shape)
    small = total[:, :, main:].reshape(branches, -1, outputs)
    per_tap = -(-channels // outputs)
    depth_grad = small[:, : 9 * per_tap].reshape(branches, 9, -1)[:, :, :channels].reshape(depth_w.shape)
    bias_grad = small[:, 9 * per_tap].astype(jnp.float32)
    fgrad = fgrad[:groups].reshape(groups, columns, rows // CLASS, PAIR, channels)
    feature_grad = fgrad.transpose(1, 2, 0, 3, 4).reshape(features.shape)
    return (feature_grad, depth_grad, point_grad, bias_grad)


def solution(mesh):
    fine = Mesh(mesh.devices.reshape(4, 4, 2, 2, 4, 2), DP + LON)
    placed = (P(DP, LON, None, None), P(), P(), P(), P(DP, LON, None, None))
    return jax.shard_map(
        per_device,
        mesh=fine,
        in_specs=placed,
        out_specs=(P(DP, LON, None, None), P(), P(), P()),
        check_vma=False,
    )
```

time: 220 us -> 152 us (0.69)
  the two profiles are of different devices: /device:TPU:32 before, /device:TPU:1 now
where the time goes in v3:
time: 152 us
  starting transfers between devices  54.3 us (36%)
  waiting for transfers between devices  37.3 us (25%)
  blocking collectives  31.2 us (21%)
  Pallas kernels  14.5 us (10%)
  local copies, waits for them, and re-layouts  8.74 us (6%)
  other arithmetic  4.67 us (3%)
    all_to_all x2, blocking collectives, exchange(): return lax.all_to_all(blocks, axes, 0, 0, tiled=True)  31.2 us
    ppermute x6, starting transfers between devices, sum_four(): lax.ppermute(own, axis, [(i, i ^ m) for i in range(4)]).astype(jnp.float32)  29.1 us
    all_to_all x2, waiting for transfers between devices, exchange(): return lax.all_to_all(blocks, axes, 0, 0, tiled=True)  23.2 us
    pallas_call x1, Pallas kernels, local_work(): pl.pallas_call(local_body, out_shape=(jax.ShapeDtypeStruct((rows, outputs...  14.5 us
    ppermute x2, starting transfers between devices, swap_cores(): return lax.ppermute(block, 'core', [(0, 1), (1, 0)])  14 us
    ppermute x6, waiting for transfers between devices, sum_four(): lax.ppermute(own, axis, [(i, i ^ m) for i in range(4)]).astype(jnp.float32)  12.4 us
    all_to_all x2, starting transfers between devices, exchange(): return lax.all_to_all(blocks, axes, 0, 0, tiled=True)  11.2 us
  transfers between devices with their start and end apart: 10, of which 6 were waited for; matrix products, arithmetic and copies ran while one was open for 2% of the time, Pallas kernels for 0%

profile of v3, /device:TPU:1, one launch (start us, length us, event | category | flops | bytes accessed | tf_op | source)
XLA Modules:
  0.0 151.6 jit_solution(14205647381931819536)
XLA Ops:
  0.6 2.4 %reshape.59 = bf16[9,4,6,2,1152]{4,3,2,1,0:T(2,128)(2,1)S(1)} reshape(bf16[1,9,48,1152]{3,2,1,0:T(8,128)(2,1)} %param.5) | data formatting | bytes 1990656 | tf_op jit(solution)/shard_map/reshape | solution.py:245
  3.1 0.0 copy-start.3
  3.1 0.7 copy.27
  3.8 0.4 reshape.60
  4.2 0.0 copy-done.3
  4.2 0.2 reshape.61
  4.3 0.3 copy.28
  4.7 0.2 reshape.62
  4.8 1.4 fusion.2
  6.3 0.0 copy-start.4
  6.3 0.0 copy-start
  6.3 0.0 copy-start.1
  6.3 7.6 %all-to-all-start = ((bf16[8,9,8,1664]{3,2,1,0:T(8,128)(2,1)}), bf16[8,9,8,1664]{3,2,1,0:T(8,128)(2,1)S(1)}, u32[]{:S(2)}, u32[]{:S(2)}) async-start(bf16[8,9,8,1664]{3,2,1,0:T(8,128)(2,1)} %fusion.2), calls=%async_computation | async-start | bytes 3833856 | tf_op jit(solution)/shard_map/all_to_all | solution.py:24
  13.9 0.0 copy-done.4
  14.0 23.2 %all-to-all-done = bf16[8,9,8,1664]{3,2,1,0:T(8,128)(2,1)S(1)} async-done(((bf16[8,9,8,1664]{3,2,1,0:T(8,128)(2,1)}), bf16[8,9,8,1664]{3,2,1,0:T(8,128)(2,1)S(1)}, u32[]{:S(2)}, u32[]{:S(2)}) %all-to-all-start) | async-done | bytes 1916960 | tf_op jit(solution)/shard_map/all_to_all | solution.py:24
  37.2 0.0 copy-start.2
  37.2 1.3 copy-done.2
  38.5 0.0 copy-done
  38.5 0.0 copy-done.1
  38.5 14.5 %local_work.1 = (f32[1280,256]{1,0:T(8,128)S(1)}, bf16[1280,256]{1,0:T(8,128)(2,1)S(1)}, bf16[576,1152]{1,0:T(8,128)(2,1)}) custom-call(s32[1]{0:T(128)} %bitcast.core_ref, bf16[576,1664]{1,0:T(8,128)(2,1)} %bitcast.28, f32[18,1152]{1,0:T(8,128)S(1)} %reshape.75.taps_ref, bf16[2,1152,256]{2,1,0:T(8,128)(2,1)S(1)} %copy-done, f32[2,256]{1,0:T(2,128)S(1)} %copy-done.1), custom_call_target="tpu_custom_call" | custom-call | tf_op jit(solution)/shard_map/local_work/pallas_call | solution.py:223
  53.0 6.1 %collective-permute-start = (bf16[1280,256]{1,0:T(8,128)(2,1)S(1)}, bf16[1280,256]{1,0:T(8,128)(2,1)S(1)}, u32[]{:S(2)}, u32[]{:S(2)}) collective-permute-start(bf16[1280,256]{1,0:T(8,128)(2,1)S(1)} %get-tuple-element.13), channel_id=1, source_target_pairs={{0,8},{8,0},{1,9},{9,1},{2,10},{10,2},{3,11},{11,3},{4,12},{12,4},... | collective-permute-start | bytes 1966088 | tf_op jit(solution)/shard_map/ppermute | solution.py:20
  59.0 1.7 %collective-permute-done = bf16[1280,256]{1,0:T(8,128)(2,1)S(1)} collective-permute-done((bf16[1280,256]{1,0:T(8,128)(2,1)S(1)}, bf16[1280,256]{1,0:T(8,128)(2,1)S(1)}, u32[]{:S(2)}, u32[]{:S(2)}) %collective-permute-start) | collective-permute-done | bytes 655392 | tf_op jit(solution)/shard_map/ppermute | solution.py:20
  60.7 0.2 add_convert_fusion
  60.9 14.6 %all_to_all.20 = bf16[16,80,256]{2,1,0:T(8,128)(2,1)S(1)} all-to-all(bf16[16,80,256]{2,1,0:T(8,128)(2,1)S(1)} %bitcast.31), channel_id=1, replica_groups=mesh['zh'=4,'zl'=4,'xl'=2,'core'=2,'y'=4,'xh'=2] {'xl','y','xh'}, dimensions={0} | all-to-all | bytes 1310720 | tf_op jit(solution)/shard_map/all_to_all | solution.py:24
  75.5 3.6 %all-to-all-start.2 = ((bf16[8,9,8,1152]{3,2,1,0:T(8,128)(2,1)}), bf16[8,9,8,1152]{3,2,1,0:T(8,128)(2,1)S(1)}, u32[]{:S(2)}, u32[]{:S(2)}) async-start(bf16[8,9,8,1152]{3,2,1,0:T(8,128)(2,1)} %bitcast.5), calls=%async_computation.2 | async-start | bytes 2654208 | tf_op jit(solution)/shard_map/all_to_all | solution.py:24
  79.1 0.1 convert_reduce_fusion
  79.2 3.6 %collective-permute-start.1 = (f32[80,256]{1,0:T(8,128)S(1)}, f32[80,256]{1,0:T(8,128)S(1)}, u32[]{:S(2)}, u32[]{:S(2)}) collective-permute-start(f32[80,256]{1,0:T(8,128)S(1)} %convert_reduce_fusion), channel_id=1, source_target_pairs={{0,32},{32,0},{64,96},{96,64},{1,33},{33,1},{65,97},{97,65},{2,34}... | collective-permute-start | bytes 245768 | tf_op jit(solution)/shard_map/ppermute | solution.py:34
  82.8 4.9 %collective-permute-start.2 = (f32[80,256]{1,0:T(8,128)S(1)}, f32[80,256]{1,0:T(8,128)S(1)}, u32[]{:S(2)}, u32[]{:S(2)}) collective-permute-start(f32[80,256]{1,0:T(8,128)S(1)} %convert_reduce_fusion), channel_id=1, source_target_pairs={{0,64},{32,96},{64,0},{96,32},{1,65},{33,97},{65,1},{97,33},{2,66}... | collective-permute-start | bytes 245768 | tf_op jit(solution)/shard_map/ppermute | solution.py:34
  87.8 1.9 %collective-permute-start.3 = (f32[80,256]{1,0:T(8,128)S(1)}, f32[80,256]{1,0:T(8,128)S(1)}, u32[]{:S(2)}, u32[]{:S(2)}) collective-permute-start(f32[80,256]{1,0:T(8,128)S(1)} %convert_reduce_fusion), channel_id=1, source_target_pairs={{0,96},{32,64},{64,32},{96,0},{1,97},{33,65},{65,33},{97,1},{2,98}... | collective-permute-start | bytes 245768 | tf_op jit(solution)/shard_map/ppermute | solution.py:34
  89.7 0.0 collective-permute-done.1
  89.7 0.8 collective-permute-done.2
  90.5 4.5 %collective-permute-done.3 = f32[80,256]{1,0:T(8,128)S(1)} collective-permute-done((f32[80,256]{1,0:T(8,128)S(1)}, f32[80,256]{1,0:T(8,128)S(1)}, u32[]{:S(2)}, u32[]{:S(2)}) %collective-permute-start.3) | collective-permute-done | bytes 81952 | tf_op jit(solution)/shard_map/ppermute | solution.py:34
  95.1 8.8 %collective-permute-start.4 = (bf16[80,256]{1,0:T(8,128)(2,1)S(1)}, bf16[80,256]{1,0:T(8,128)(2,1)S(1)}, u32[]{:S(2)}, u32[]{:S(2)}) collective-permute-start(bf16[80,256]{1,0:T(8,128)(2,1)S(1)} %add_convert_fusion.1), channel_id=1, source_target_pairs={{0,128},{128,0},{256,384},{384,256},{1,129},{129,1},{257,385},{385... | collective-permute-start | bytes 122888 | tf_op jit(solution)/shard_map/ppermute | solution.py:34
  103.9 7.9 %collective-permute-start.5 = (bf16[80,256]{1,0:T(8,128)(2,1)S(1)}, bf16[80,256]{1,0:T(8,128)(2,1)S(1)}, u32[]{:S(2)}, u32[]{:S(2)}) collective-permute-start(bf16[80,256]{1,0:T(8,128)(2,1)S(1)} %add_convert_fusion.1), channel_id=1, source_target_pairs={{0,256},{128,384},{256,0},{384,128},{1,257},{129,385},{257,1},{385... | collective-permute-start | bytes 122888 | tf_op jit(solution)/shard_map/ppermute | solution.py:34
  111.8 1.9 %collective-permute-start.6 = (bf16[80,256]{1,0:T(8,128)(2,1)S(1)}, bf16[80,256]{1,0:T(8,128)(2,1)S(1)}, u32[]{:S(2)}, u32[]{:S(2)}) collective-permute-start(bf16[80,256]{1,0:T(8,128)(2,1)S(1)} %add_convert_fusion.1), channel_id=1, source_target_pairs={{0,384},{128,256},{256,128},{384,0},{1,385},{129,257},{257,129},{3... | collective-permute-start | bytes 122888 | tf_op jit(solution)/shard_map/ppermute | solution.py:34
  113.8 0.0 collective-permute-done.4
  113.8 3.6 %collective-permute-done.5 = bf16[80,256]{1,0:T(8,128)(2,1)S(1)} collective-permute-done((bf16[80,256]{1,0:T(8,128)(2,1)S(1)}, bf16[80,256]{1,0:T(8,128)(2,1)S(1)}, u32[]{:S(2)}, u32[]{:S(2)}) %collective-permute-start.5) | collective-permute-done | bytes 40992 | tf_op jit(solution)/shard_map/ppermute | solution.py:34
  117.3 3.4 %collective-permute-done.6 = bf16[80,256]{1,0:T(8,128)(2,1)S(1)} collective-permute-done((bf16[80,256]{1,0:T(8,128)(2,1)S(1)}, bf16[80,256]{1,0:T(8,128)(2,1)S(1)}, u32[]{:S(2)}, u32[]{:S(2)}) %collective-permute-start.6) | collective-permute-done | bytes 40992 | tf_op jit(solution)/shard_map/ppermute | solution.py:34
  120.8 0.0 all-to-all-done.2
  120.9 16.5 %all_to_all.21 = bf16[16,80,256]{2,1,0:T(8,128)(2,1)S(1)} all-to-all(bf16[16,80,256]{2,1,0:T(8,128)(2,1)S(1)} %broadcast_in_dim.2), channel_id=1, replica_groups=mesh['zh'=4,'zl'=4,'xl'=2,'core'=2,'y'=4,'xh'=2] {'xl','y','xh'}, dimensions={0} | all-to-all | bytes 1310720 | tf_op jit(solution)/shard_map/all_to_all | solution.py:24
  137.4 7.9 %collective-permute-start.7 = (bf16[16,80,256]{2,1,0:T(8,128)(2,1)S(1)}, bf16[16,80,256]{2,1,0:T(8,128)(2,1)}, u32[]{:S(2)}, u32[]{:S(2)}) collective-permute-start(bf16[16,80,256]{2,1,0:T(8,128)(2,1)S(1)} %all_to_all.21), channel_id=1, source_target_pairs={{0,8},{8,0},{1,9},{9,1},{2,10},{10,2},{3,11},{11,3},{4,12},{12,4},... | collective-permute-start | bytes 1966088 | tf_op jit(solution)/shard_map/ppermute | solution.py:20
  145.4 0.1 slice.18
  145.5 0.4 reshape.68
  145.8 0.7 copy.38
  146.5 1.3 reshape.69
  147.9 0.0 collective-permute-done.7
  147.9 1.3 select_bitcast_fusion.1
  149.1 1.1 pad_maximum_fusion
  150.3 0.1 reshape.71
  150.3 0.7 copy.31
  151.0 0.6 fusion.3
  (9 shorter events, 0.2 us)
Async XLA Ops:
  3.1 1.1 copy-start.3
  6.3 7.6 %copy-start.4 = (bf16[2,3,3,1152]{3,0,2,1:T(2,128)(2,1)S(1)}, bf16[2,3,3,1152]{3,0,2,1:T(2,128)(2,1)}, u32[]{:S(2)}) copy-start(bf16[2,3,3,1152]{3,0,2,1:T(2,128)(2,1)} %param.6) | copy-start | bytes 124420
  6.3 32.2 %copy-start = (bf16[2,1152,256]{2,1,0:T(8,128)(2,1)S(1)}, bf16[2,1152,256]{2,1,0:T(8,128)(2,1)}, u32[]{:S(2)}) copy-start(bf16[2,1152,256]{2,1,0:T(8,128)(2,1)} %pw_ref.1) | copy-start | bytes 3538948
  6.3 32.2 %copy-start.1 = (f32[2,256]{1,0:T(2,128)S(1)}, f32[2,256]{1,0:T(2,128)}, u32[]{:S(2)}) copy-start(f32[2,256]{1,0:T(2,128)} %pb_ref.1) | copy-start | bytes 6148
  6.3 30.9 %all-to-all-start = ((bf16[8,9,8,1664]{3,2,1,0:T(8,128)(2,1)}), bf16[8,9,8,1664]{3,2,1,0:T(8,128)(2,1)S(1)}, u32[]{:S(2)}, u32[]{:S(2)}) async-start(bf16[8,9,8,1664]{3,2,1,0:T(8,128)(2,1)} %fusion.2), calls=%async_computation | async-start | bytes 3833856 | tf_op jit(solution)/shard_map/all_to_all | solution.py:24
  37.2 1.3 copy-start.2
  53.0 7.8 %collective-permute-start = (bf16[1280,256]{1,0:T(8,128)(2,1)S(1)}, bf16[1280,256]{1,0:T(8,128)(2,1)S(1)}, u32[]{:S(2)}, u32[]{:S(2)}) collective-permute-start(bf16[1280,256]{1,0:T(8,128)(2,1)S(1)} %get-tuple-element.13), channel_id=1, source_target_pairs={{0,8},{8,0},{1,9},{9,1},{2,10},{10,2},{3,11},{11,3},{4,12},{12,4},... | collective-permute-start | bytes 1966088 | tf_op jit(solution)/shard_map/ppermute | solution.py:20
  75.5 45.3 %all-to-all-start.2 = ((bf16[8,9,8,1152]{3,2,1,0:T(8,128)(2,1)}), bf16[8,9,8,1152]{3,2,1,0:T(8,128)(2,1)S(1)}, u32[]{:S(2)}, u32[]{:S(2)}) async-start(bf16[8,9,8,1152]{3,2,1,0:T(8,128)(2,1)} %bitcast.5), calls=%async_computation.2 | async-start | bytes 2654208 | tf_op jit(solution)/shard_map/all_to_all | solution.py:24
  79.2 10.5 %collective-permute-start.1 = (f32[80,256]{1,0:T(8,128)S(1)}, f32[80,256]{1,0:T(8,128)S(1)}, u32[]{:S(2)}, u32[]{:S(2)}) collective-permute-start(f32[80,256]{1,0:T(8,128)S(1)} %convert_reduce_fusion), channel_id=1, source_target_pairs={{0,32},{32,0},{64,96},{96,64},{1,33},{33,1},{65,97},{97,65},{2,34}... | collective-permute-start | bytes 245768 | tf_op jit(solution)/shard_map/ppermute | solution.py:34
  82.8 7.7 %collective-permute-start.2 = (f32[80,256]{1,0:T(8,128)S(1)}, f32[80,256]{1,0:T(8,128)S(1)}, u32[]{:S(2)}, u32[]{:S(2)}) collective-permute-start(f32[80,256]{1,0:T(8,128)S(1)} %convert_reduce_fusion), channel_id=1, source_target_pairs={{0,64},{32,96},{64,0},{96,32},{1,65},{33,97},{65,1},{97,33},{2,66}... | collective-permute-start | bytes 245768 | tf_op jit(solution)/shard_map/ppermute | solution.py:34
  87.8 7.3 %collective-permute-start.3 = (f32[80,256]{1,0:T(8,128)S(1)}, f32[80,256]{1,0:T(8,128)S(1)}, u32[]{:S(2)}, u32[]{:S(2)}) collective-permute-start(f32[80,256]{1,0:T(8,128)S(1)} %convert_reduce_fusion), channel_id=1, source_target_pairs={{0,96},{32,64},{64,32},{96,0},{1,97},{33,65},{65,33},{97,1},{2,98}... | collective-permute-start | bytes 245768 | tf_op jit(solution)/shard_map/ppermute | solution.py:34
  95.1 18.7 %collective-permute-start.4 = (bf16[80,256]{1,0:T(8,128)(2,1)S(1)}, bf16[80,256]{1,0:T(8,128)(2,1)S(1)}, u32[]{:S(2)}, u32[]{:S(2)}) collective-permute-start(bf16[80,256]{1,0:T(8,128)(2,1)S(1)} %add_convert_fusion.1), channel_id=1, source_target_pairs={{0,128},{128,0},{256,384},{384,256},{1,129},{129,1},{257,385},{385... | collective-permute-start | bytes 122888 | tf_op jit(solution)/shard_map/ppermute | solution.py:34
  103.9 13.5 %collective-permute-start.5 = (bf16[80,256]{1,0:T(8,128)(2,1)S(1)}, bf16[80,256]{1,0:T(8,128)(2,1)S(1)}, u32[]{:S(2)}, u32[]{:S(2)}) collective-permute-start(bf16[80,256]{1,0:T(8,128)(2,1)S(1)} %add_convert_fusion.1), channel_id=1, source_target_pairs={{0,256},{128,384},{256,0},{384,128},{1,257},{129,385},{257,1},{385... | collective-permute-start | bytes 122888 | tf_op jit(solution)/shard_map/ppermute | solution.py:34
  111.8 8.9 %collective-permute-start.6 = (bf16[80,256]{1,0:T(8,128)(2,1)S(1)}, bf16[80,256]{1,0:T(8,128)(2,1)S(1)}, u32[]{:S(2)}, u32[]{:S(2)}) collective-permute-start(bf16[80,256]{1,0:T(8,128)(2,1)S(1)} %add_convert_fusion.1), channel_id=1, source_target_pairs={{0,384},{128,256},{256,128},{384,0},{1,385},{129,257},{257,129},{3... | collective-permute-start | bytes 122888 | tf_op jit(solution)/shard_map/ppermute | solution.py:34
  137.4 10.4 %collective-permute-start.7 = (bf16[16,80,256]{2,1,0:T(8,128)(2,1)S(1)}, bf16[16,80,256]{2,1,0:T(8,128)(2,1)}, u32[]{:S(2)}, u32[]{:S(2)}) collective-permute-start(bf16[16,80,256]{2,1,0:T(8,128)(2,1)S(1)} %all_to_all.21), channel_id=1, source_target_pairs={{0,8},{8,0},{1,9},{9,1},{2,10},{10,2},{3,11},{11,3},{4,12},{12,4},... | collective-permute-start | bytes 1966088 | tf_op jit(solution)/shard_map/ppermute | solution.py:20

commit v4 on v3

--- a/solution.py
+++ b/solution.py
@@ -13,7 +13,8 @@
 
 DP = ("zh", "zl", "xl", "core")
 LON = ("y", "xh")
-PLANE = ("xl", "y", "xh")
+NEAR = ("zl", "xl", "y", "xh")
+TILES = 320
 
 
 def swap_cores(block):
@@ -49,18 +50,17 @@
     return jnp.where(top, pltpu.roll(tile, 2, 0), pltpu.roll(tile, 6, 0))
 
 
-def shard_row(row, main, extra):
-    return (row // extra) * (main + extra) + main + row % extra
-
-
 def local_body(core_ref, cls_ref, taps_ref, pw_ref, pb_ref, kept_ref, sent_ref, fg_ref, depth, dgr, terms):
     channels, outputs = pw_ref.shape[1:]
-    shard = terms.shape[1] // 16
-    main = channels // 16
-    extra = shard - main
     tiles = channels // LANES
     wide = outputs // LANES
-    per_tap = -(-tiles // wide)
+    blocks = channels // HELD
+
+    def store_row(branch, row, value):
+        tile = blocks * wide + row // HELD
+        at = row % HELD
+        terms[branch, tile // wide, tile % wide, at : at + 1, :] = value
+
     sub = lax.broadcasted_iota(jnp.int32, (HELD, LANES), 0)
     top = sub < 4
     first = sub < 2
@@ -135,11 +135,14 @@
         point = lax.dot_general(
             depth[branch], pgrad, (((0,), (0,)), ((), ())), preferred_element_type=jnp.float32
         )
-        for p in range(16):
-            terms[branch, p * shard : p * shard + main, :] = point[p * main : (p + 1) * main]
-            terms[branch, p * shard + main : (p + 1) * shard, :] = jnp.zeros((extra, outputs), jnp.float32)
-        row = shard_row(9 * per_tap, main, extra)
-        terms[branch, row : row + 1, :] = jnp.sum(pgrad.astype(jnp.float32), axis=0, keepdims=True)
+        point = point.reshape(blocks, HELD, outputs)
+        bias = jnp.sum(pgrad.astype(jnp.float32), axis=0, keepdims=True)
+        rest = terms.shape[1] - blocks
+        terms[branch, blocks:] = jnp.zeros((rest, wide, HELD, LANES), jnp.float32)
+        for h in range(wide):
+            lanes = slice(h * LANES, (h + 1) * LANES)
+            terms[branch, :blocks, h] = point[:, :, lanes]
+            store_row(branch, 9 * tiles + h, bias[:, lanes])
         for c in range(0, channels, 384):
             part = lax.dot_general(
                 pgrad, pw_ref[branch, c : c + 384, :], (((1,), (1,)), ((), ())), preferred_element_type=jnp.float32
@@ -191,9 +194,8 @@
 
         def keep(branch, a, e, value, mask=None):
             value = value if mask is None else jnp.where(mask, value, 0.0)
-            row = shard_row(((a + 1) * 3 + e + 1) * per_tap + t // wide, main, extra)
-            at = (t % wide) * LANES
-            terms[branch, row : row + 1, at : at + LANES] = jnp.sum(value, axis=0, keepdims=True)
+            row = ((a + 1) * 3 + e + 1) * tiles + t
+            store_row(branch, row, jnp.sum(value, axis=0, keepdims=True))
 
         for n in range(3):
             keep(0, 0, n - 1, sums[n])
@@ -218,13 +220,14 @@
 def local_work(core, field, taps, point_w, point_bias):
     cells = field.shape[0]
     branches, channels, outputs = point_w.shape
-    rows = 16 * (channels // 16 + 8)
+    wide = outputs // LANES
+    packed = (TILES // wide, wide, HELD, LANES)
     vmem = pl.BlockSpec(memory_space=pltpu.VMEM)
     return pl.pallas_call(
         local_body,
         out_shape=(
-            jax.ShapeDtypeStruct((rows, outputs), jnp.float32),
-            jax.ShapeDtypeStruct((rows, outputs), jnp.bfloat16),
+            jax.ShapeDtypeStruct(packed, jnp.float32),
+            jax.ShapeDtypeStruct(packed, jnp.bfloat16),
             jax.ShapeDtypeStruct((cells, channels), jnp.bfloat16),
         ),
         in_specs=[pl.BlockSpec(memory_space=pltpu.SMEM)] + [vmem] * 4,
@@ -232,7 +235,7 @@
         scratch_shapes=[
             pltpu.VMEM((branches, cells, channels), jnp.bfloat16),
             pltpu.VMEM((branches, cells, channels), jnp.bfloat16),
-            pltpu.VMEM((branches, rows, outputs), jnp.float32),
+            pltpu.VMEM((branches,) + packed, jnp.float32),
         ],
         compiler_params=pltpu.CompilerParams(vmem_limit_bytes=48 << 20),
         name="local_work",
@@ -251,7 +254,7 @@
     branches, _, outputs = point_w.shape
     images = lax.axis_size(DP) * features.shape[0]
     peers = lax.axis_size(LON)
-    plane = lax.axis_size(PLANE)
+    near = lax.axis_size(NEAR)
     groups = CLASS // PAIR
     core = lax.axis_index("core")
 
@@ -262,24 +265,22 @@
     kept, sent, fgrad = local_work(core.reshape(1), field, taps, point_w, point_bias)
 
     terms = (kept + swap_cores(sent).astype(jnp.float32)).astype(jnp.bfloat16)
-    shard = terms.shape[0] // plane
-    terms = exchange(terms.reshape(plane, shard, outputs), PLANE)
+    terms = exchange(terms.reshape(near, -1, LANES), NEAR)
     fgrad, terms = lax.optimization_barrier((fgrad, terms))
     fgrad = exchange(fgrad.reshape(peers, columns, HELD, channels), LON)
     terms = jnp.sum(terms.astype(jnp.float32), axis=0)
-    terms = sum_four(terms, "zl").astype(jnp.bfloat16)
     total = (sum_four(terms, "zh") / images).astype(jnp.bfloat16)
     fgrad, total = lax.optimization_barrier((fgrad, total))
-    total = gather_copies(total, PLANE)
+    total = gather_copies(total, NEAR).reshape(-1, LANES)
     other = swap_cores(total)
     total = jnp.stack([jnp.where(core == 0, total, other), jnp.where(core == 0, other, total)])
 
-    main = channels // plane
-    point_grad = total[:, :, :main].reshape(point_w.shape)
-    small = total[:, :, main:].reshape(branches, -1, outputs)
-    per_tap = -(-channels // outputs)
-    depth_grad = small[:, : 9 * per_tap].reshape(branches, 9, -1)[:, :, :channels].reshape(depth_w.shape)
-    bias_grad = small[:, 9 * per_tap].astype(jnp.float32)
+    main = channels * outputs // LANES
+    point_grad = total[:, :main].reshape(branches, channels // HELD, outputs // LANES, HELD, LANES)
+    point_grad = point_grad.transpose(0, 1, 3, 2, 4).reshape(point_w.shape)
+    last = main + 9 * channels // LANES
+    depth_grad = total[:, main:last].reshape(depth_w.shape)
+    bias_grad = total[:, last : last + outputs // LANES].reshape(branches, outputs).astype(jnp.float32)
     fgrad = fgrad[:groups].reshape(groups, columns, rows // CLASS, PAIR, channels)
     feature_grad = fgrad.transpose(1, 2, 0, 3, 4).reshape(features.shape)
     return (feature_grad, depth_grad, point_grad, bias_grad)

time: 152 us -> 158 us (1.039)
  blocking collectives: 31.2 us -> 55.6 us
  starting transfers between devices: 54.3 us -> 40.9 us
  waiting for transfers between devices: 37.3 us -> 31.4 us
    all_to_all x2, blocking collectives: 31.2 us -> 55.6 us  [exchange(): return lax.all_to_all(blocks, axes, 0, 0, tiled=True)]
    ppermute x6 -> x3, starting transfers between devices: 29.1 us -> 18.7 us  [sum_four(): lax.ppermute(own, axis, [(i, i ^ m) for i in range(4)]).astype(jnp.float32)]
    ppermute x6 -> x3, waiting for transfers between devices: 12.4 us -> 6.5 us  [sum_four(): lax.ppermute(own, axis, [(i, i ^ m) for i in range(4)]).astype(jnp.float32)]
    ppermute x2, starting transfers between devices: 14 us -> 11 us  [swap_cores(): return lax.ppermute(block, 'core', [(0, 1), (1, 0)])]
    unnamed x10 -> x12, local copies, waits for them, and re-layouts: 1.3 us -> 3.15 us
  transfers between devices with their start and end apart: 10 -> 7, of which waited for: 6 -> 4; matrix products, arithmetic and copies ran while one was open for 2% -> 2% of each run, Pallas kernels for 0% -> 0%
where the time goes in v4:
time: 158 us; the launch traced here: 157 us
  blocking collectives  55.6 us (35%)
  starting transfers between devices  40.9 us (26%)
  waiting for transfers between devices  31.4 us (20%)
  Pallas kernels  14.5 us (9%)
  local copies, waits for them, and re-layouts  9.93 us (6%)
  other arithmetic  4.01 us (3%)
    all_to_all x2, blocking collectives, exchange(): return lax.all_to_all(blocks, axes, 0, 0, tiled=True)  55.6 us
    all_to_all x2, waiting for transfers between devices, exchange(): return lax.all_to_all(blocks, axes, 0, 0, tiled=True)  23.2 us
    ppermute x3, starting transfers between devices, sum_four(): lax.ppermute(own, axis, [(i, i ^ m) for i in range(4)]).astype(jnp.float32)  18.7 us
    pallas_call x1, Pallas kernels, local_work(): pl.pallas_call(local_body, out_shape=(jax.ShapeDtypeStruct(packed, jnp.fl...  14.5 us
    all_to_all x2, starting transfers between devices, exchange(): return lax.all_to_all(blocks, axes, 0, 0, tiled=True)  11.2 us
    ppermute x2, starting transfers between devices, swap_cores(): return lax.ppermute(block, 'core', [(0, 1), (1, 0)])  11 us
    ppermute x3, waiting for transfers between devices, sum_four(): lax.ppermute(own, axis, [(i, i ^ m) for i in range(4)]).astype(jnp.float32)  6.5 us
  transfers between devices with their start and end apart: 7, of which 4 were waited for; matrix products, arithmetic and copies ran while one was open for 2% of the time, Pallas kernels for 0%

profile of v4, /device:TPU:1, one launch (start us, length us, event | category | flops | bytes accessed | tf_op | source)
XLA Modules:
  0.0 157.1 jit_solution(983725595738975741)
XLA Ops:
  0.6 2.4 %reshape.60 = bf16[9,4,6,2,1152]{4,3,2,1,0:T(2,128)(2,1)S(1)} reshape(bf16[1,9,48,1152]{3,2,1,0:T(8,128)(2,1)} %param.5) | data formatting | bytes 1990656 | tf_op jit(solution)/shard_map/reshape | solution.py:248
  3.1 0.7 copy.13
  3.8 0.0 copy-start.3
  3.8 0.4 reshape.61
  4.2 0.6 copy-done.3
  4.8 0.2 reshape.62
  5.0 0.3 copy.14
  5.3 0.2 reshape.63
  5.4 1.4 fusion.2
  6.9 0.0 copy-start.4
  6.9 0.0 copy-start
  6.9 0.0 copy-start.1
  6.9 7.6 %all-to-all-start = ((bf16[8,9,8,1664]{3,2,1,0:T(8,128)(2,1)}), bf16[8,9,8,1664]{3,2,1,0:T(8,128)(2,1)S(1)}, u32[]{:S(2)}, u32[]{:S(2)}) async-start(bf16[8,9,8,1664]{3,2,1,0:T(8,128)(2,1)} %fusion.2), calls=%async_computation | async-start | bytes 3833856 | tf_op jit(solution)/shard_map/all_to_all | solution.py:25
  14.5 0.0 copy-done.4
  14.6 23.2 %all-to-all-done = bf16[8,9,8,1664]{3,2,1,0:T(8,128)(2,1)S(1)} async-done(((bf16[8,9,8,1664]{3,2,1,0:T(8,128)(2,1)}), bf16[8,9,8,1664]{3,2,1,0:T(8,128)(2,1)S(1)}, u32[]{:S(2)}, u32[]{:S(2)}) %all-to-all-start) | async-done | bytes 1916960 | tf_op jit(solution)/shard_map/all_to_all | solution.py:25
  37.8 0.0 copy-start.2
  37.8 1.3 copy-done.2
  39.1 0.0 copy-done
  39.1 0.0 copy-done.1
  39.1 14.5 %local_work.1 = (f32[160,2,8,128]{3,2,1,0:T(8,128)S(1)}, bf16[160,2,8,128]{3,2,1,0:T(8,128)(2,1)S(1)}, bf16[576,1152]{1,0:T(8,128)(2,1)}) custom-call(s32[1]{0:T(128)} %bitcast.core_ref, bf16[576,1664]{1,0:T(8,128)(2,1)} %bitcast.32, f32[18,1152]{1,0:T(8,128)S(1)} %reshape.76.taps_ref, bf16[2,1152,256]{2,1,0:T(8,128)(2,1)S(1)} %copy-done, f32[2,256]{1,0:T(2,128)S(1)} %copy-done.1), custom_call_target="tpu_custom_call" | custom-call | tf_op jit(solution)/shard_map/local_work/pallas_call | solution.py:226
  53.6 6.0 %collective-permute-start = (bf16[160,2,8,128]{3,2,1,0:T(8,128)(2,1)S(1)}, bf16[160,2,8,128]{3,2,1,0:T(8,128)(2,1)S(1)}, u32[]{:S(2)}, u32[]{:S(2)}) collective-permute-start(bf16[160,2,8,128]{3,2,1,0:T(8,128)(2,1)S(1)} %get-tuple-element.13), channel_id=1, source_target_pairs={{0,8},{8,0},{1,9},{9,1},{2,10},{10,2},{3,11},{11,3},{4,12},{12,4},... | collective-permute-start | bytes 1966088 | tf_op jit(solution)/shard_map/ppermute | solution.py:21
  59.6 1.7 %collective-permute-done = bf16[160,2,8,128]{3,2,1,0:T(8,128)(2,1)S(1)} collective-permute-done((bf16[160,2,8,128]{3,2,1,0:T(8,128)(2,1)S(1)}, bf16[160,2,8,128]{3,2,1,0:T(8,128)(2,1)S(1)}, u32[]{:S(2)}, u32[]{:S(2)}) %collective-permute-start) | collective-permute-done | bytes 655392 | tf_op jit(solution)/shard_map/ppermute | solution.py:21
  61.3 0.2 add_convert_fusion
  61.5 27.5 %all_to_all.20 = bf16[64,40,128]{2,1,0:T(8,128)(2,1)S(1)} all-to-all(bf16[64,40,128]{2,1,0:T(8,128)(2,1)S(1)} %bitcast.35), channel_id=1, replica_groups=mesh['zh'=4,'zl'=4,'xl'=2,'core'=2,'y'=4,'xh'=2] {'zl','xl','y','xh'}, dimensions={0} | all-to-all | bytes 1310720 | tf_op jit(solution)/shard_map/all_to_all | solution.py:25
  89.0 3.6 %all-to-all-start.2 = ((bf16[8,9,8,1152]{3,2,1,0:T(8,128)(2,1)}), bf16[8,9,8,1152]{3,2,1,0:T(8,128)(2,1)S(1)}, u32[]{:S(2)}, u32[]{:S(2)}) async-start(bf16[8,9,8,1152]{3,2,1,0:T(8,128)(2,1)} %bitcast.5), calls=%async_computation.2 | async-start | bytes 2654208 | tf_op jit(solution)/shard_map/all_to_all | solution.py:25
  92.6 0.1 convert_reduce_fusion
  92.7 8.8 %collective-permute-start.1 = (f32[40,128]{1,0:T(8,128)S(1)}, f32[40,128]{1,0:T(8,128)S(1)}, u32[]{:S(2)}, u32[]{:S(2)}) collective-permute-start(f32[40,128]{1,0:T(8,128)S(1)} %convert_reduce_fusion), channel_id=1, source_target_pairs={{0,128},{128,0},{256,384},{384,256},{1,129},{129,1},{257,385},{385... | collective-permute-start | bytes 61448 | tf_op jit(solution)/shard_map/ppermute | solution.py:35
  101.5 7.9 %collective-permute-start.2 = (f32[40,128]{1,0:T(8,128)S(1)}, f32[40,128]{1,0:T(8,128)S(1)}, u32[]{:S(2)}, u32[]{:S(2)}) collective-permute-start(f32[40,128]{1,0:T(8,128)S(1)} %convert_reduce_fusion), channel_id=1, source_target_pairs={{0,256},{128,384},{256,0},{384,128},{1,257},{129,385},{257,1},{385... | collective-permute-start | bytes 61448 | tf_op jit(solution)/shard_map/ppermute | solution.py:35
  109.5 1.9 %collective-permute-start.3 = (f32[40,128]{1,0:T(8,128)S(1)}, f32[40,128]{1,0:T(8,128)S(1)}, u32[]{:S(2)}, u32[]{:S(2)}) collective-permute-start(f32[40,128]{1,0:T(8,128)S(1)} %convert_reduce_fusion), channel_id=1, source_target_pairs={{0,384},{128,256},{256,128},{384,0},{1,385},{129,257},{257,129},{3... | collective-permute-start | bytes 61448 | tf_op jit(solution)/shard_map/ppermute | solution.py:35
  111.4 0.0 collective-permute-done.1
  111.4 3.4 %collective-permute-done.2 = f32[40,128]{1,0:T(8,128)S(1)} collective-permute-done((f32[40,128]{1,0:T(8,128)S(1)}, f32[40,128]{1,0:T(8,128)S(1)}, u32[]{:S(2)}, u32[]{:S(2)}) %collective-permute-start.2) | collective-permute-done | bytes 20512 | tf_op jit(solution)/shard_map/ppermute | solution.py:35
  114.7 3.1 %collective-permute-done.3 = f32[40,128]{1,0:T(8,128)S(1)} collective-permute-done((f32[40,128]{1,0:T(8,128)S(1)}, f32[40,128]{1,0:T(8,128)S(1)}, u32[]{:S(2)}, u32[]{:S(2)}) %collective-permute-start.3) | collective-permute-done | bytes 20512 | tf_op jit(solution)/shard_map/ppermute | solution.py:35
  117.9 0.0 all-to-all-done.2
  117.9 0.1 broadcast_in_dim.2
  118.0 28.1 %all_to_all.21 = bf16[64,40,128]{2,1,0:T(8,128)(2,1)S(1)} all-to-all(bf16[64,40,128]{2,1,0:T(8,128)(2,1)S(1)} %broadcast_in_dim.2), channel_id=1, replica_groups=mesh['zh'=4,'zl'=4,'xl'=2,'core'=2,'y'=4,'xh'=2] {'zl','xl','y','xh'}, dimensions={0} | all-to-all | bytes 1310720 | tf_op jit(solution)/shard_map/all_to_all | solution.py:25
  146.1 5.0 %collective-permute-start.4 = (bf16[2560,128]{1,0:T(8,128)(2,1)S(1)}, bf16[2560,128]{1,0:T(8,128)(2,1)}, u32[]{:S(2)}, u32[]{:S(2)}) collective-permute-start(bf16[2560,128]{1,0:T(8,128)(2,1)S(1)} %bitcast.36), channel_id=1, source_target_pairs={{0,8},{8,0},{1,9},{9,1},{2,10},{10,2},{3,11},{11,3},{4,12},{12,4},... | collective-permute-start | bytes 1966088 | tf_op jit(solution)/shard_map/ppermute | solution.py:21
  151.0 0.1 slice.12
  151.1 0.4 reshape.69
  151.5 0.7 copy.21
  152.2 1.3 reshape.70
  153.5 0.0 collective-permute-done.4
  153.5 1.2 select_bitcast_fusion.1
  154.7 1.1 fusion.3
  155.8 0.6 copy.22
  156.4 0.7 copy.17
  (6 shorter events, 0.1 us)
Async XLA Ops:
  3.8 1.0 copy-start.3
  6.9 7.6 %copy-start.4 = (bf16[2,3,3,1152]{3,0,2,1:T(2,128)(2,1)S(1)}, bf16[2,3,3,1152]{3,0,2,1:T(2,128)(2,1)}, u32[]{:S(2)}) copy-start(bf16[2,3,3,1152]{3,0,2,1:T(2,128)(2,1)} %param.6) | copy-start | bytes 124420
  6.9 32.2 %copy-start = (bf16[2,1152,256]{2,1,0:T(8,128)(2,1)S(1)}, bf16[2,1152,256]{2,1,0:T(8,128)(2,1)}, u32[]{:S(2)}) copy-start(bf16[2,1152,256]{2,1,0:T(8,128)(2,1)} %pw_ref.1) | copy-start | bytes 3538948
  6.9 32.2 %copy-start.1 = (f32[2,256]{1,0:T(2,128)S(1)}, f32[2,256]{1,0:T(2,128)}, u32[]{:S(2)}) copy-start(f32[2,256]{1,0:T(2,128)} %pb_ref.1) | copy-start | bytes 6148
  6.9 30.9 %all-to-all-start = ((bf16[8,9,8,1664]{3,2,1,0:T(8,128)(2,1)}), bf16[8,9,8,1664]{3,2,1,0:T(8,128)(2,1)S(1)}, u32[]{:S(2)}, u32[]{:S(2)}) async-start(bf16[8,9,8,1664]{3,2,1,0:T(8,128)(2,1)} %fusion.2), calls=%async_computation | async-start | bytes 3833856 | tf_op jit(solution)/shard_map/all_to_all | solution.py:25
  37.8 1.3 copy-start.2
  53.6 7.8 %collective-permute-start = (bf16[160,2,8,128]{3,2,1,0:T(8,128)(2,1)S(1)}, bf16[160,2,8,128]{3,2,1,0:T(8,128)(2,1)S(1)}, u32[]{:S(2)}, u32[]{:S(2)}) collective-permute-start(bf16[160,2,8,128]{3,2,1,0:T(8,128)(2,1)S(1)} %get-tuple-element.13), channel_id=1, source_target_pairs={{0,8},{8,0},{1,9},{9,1},{2,10},{10,2},{3,11},{11,3},{4,12},{12,4},... | collective-permute-start | bytes 1966088 | tf_op jit(solution)/shard_map/ppermute | solution.py:21
  89.0 28.9 %all-to-all-start.2 = ((bf16[8,9,8,1152]{3,2,1,0:T(8,128)(2,1)}), bf16[8,9,8,1152]{3,2,1,0:T(8,128)(2,1)S(1)}, u32[]{:S(2)}, u32[]{:S(2)}) async-start(bf16[8,9,8,1152]{3,2,1,0:T(8,128)(2,1)} %bitcast.5), calls=%async_computation.2 | async-start | bytes 2654208 | tf_op jit(solution)/shard_map/all_to_all | solution.py:25
  92.7 18.7 %collective-permute-start.1 = (f32[40,128]{1,0:T(8,128)S(1)}, f32[40,128]{1,0:T(8,128)S(1)}, u32[]{:S(2)}, u32[]{:S(2)}) collective-permute-start(f32[40,128]{1,0:T(8,128)S(1)} %convert_reduce_fusion), channel_id=1, source_target_pairs={{0,128},{128,0},{256,384},{384,256},{1,129},{129,1},{257,385},{385... | collective-permute-start | bytes 61448 | tf_op jit(solution)/shard_map/ppermute | solution.py:35
  101.5 13.2 %collective-permute-start.2 = (f32[40,128]{1,0:T(8,128)S(1)}, f32[40,128]{1,0:T(8,128)S(1)}, u32[]{:S(2)}, u32[]{:S(2)}) collective-permute-start(f32[40,128]{1,0:T(8,128)S(1)} %convert_reduce_fusion), channel_id=1, source_target_pairs={{0,256},{128,384},{256,0},{384,128},{1,257},{129,385},{257,1},{385... | collective-permute-start | bytes 61448 | tf_op jit(solution)/shard_map/ppermute | solution.py:35
  109.5 8.4 %collective-permute-start.3 = (f32[40,128]{1,0:T(8,128)S(1)}, f32[40,128]{1,0:T(8,128)S(1)}, u32[]{:S(2)}, u32[]{:S(2)}) collective-permute-start(f32[40,128]{1,0:T(8,128)S(1)} %convert_reduce_fusion), channel_id=1, source_target_pairs={{0,384},{128,256},{256,128},{384,0},{1,385},{129,257},{257,129},{3... | collective-permute-start | bytes 61448 | tf_op jit(solution)/shard_map/ppermute | solution.py:35
  146.1 7.5 %collective-permute-start.4 = (bf16[2560,128]{1,0:T(8,128)(2,1)S(1)}, bf16[2560,128]{1,0:T(8,128)(2,1)}, u32[]{:S(2)}, u32[]{:S(2)}) collective-permute-start(bf16[2560,128]{1,0:T(8,128)(2,1)S(1)} %bitcast.36), channel_id=1, source_target_pairs={{0,8},{8,0},{1,9},{9,1},{2,10},{10,2},{3,11},{11,3},{4,12},{12,4},... | collective-permute-start | bytes 1966088 | tf_op jit(solution)/shard_map/ppermute | solution.py:21

commit v5 on v3

--- a/solution.py
+++ b/solution.py
@@ -29,11 +29,9 @@
     return exchange(jnp.broadcast_to(block[None], (peers,) + block.shape), axes)
 
 
-def sum_four(own, axis):
-    near, far, last = [
-        lax.ppermute(own, axis, [(i, i ^ m) for i in range(4)]).astype(jnp.float32) for m in (1, 2, 3)
-    ]
-    return (own.astype(jnp.float32) + near) + (far + last)
+def sum_pair(own, axis, apart):
+    pairs = [(i, i ^ apart) for i in range(lax.axis_size(axis))]
+    return own.astype(jnp.float32) + lax.ppermute(own, axis, pairs).astype(jnp.float32)
 
 
 def gate_slope(pre_act):
@@ -267,10 +265,15 @@
     fgrad, terms = lax.optimization_barrier((fgrad, terms))
     fgrad = exchange(fgrad.reshape(peers, columns, HELD, channels), LON)
     terms = jnp.sum(terms.astype(jnp.float32), axis=0)
-    terms = sum_four(terms, "zl").astype(jnp.bfloat16)
-    total = (sum_four(terms, "zh") / images).astype(jnp.bfloat16)
+    terms = sum_pair(sum_pair(terms, "zl", 1), "zl", 2)
+    terms = sum_pair(terms.astype(jnp.bfloat16), "zh", 1)
+    terms = sum_pair(terms.astype(jnp.bfloat16), "zh", 2)
+    total = (terms / images).astype(jnp.bfloat16)
     fgrad, total = lax.optimization_barrier((fgrad, total))
     total = gather_copies(total, PLANE)
+    fgrad = fgrad[:groups].reshape(groups, columns, rows // CLASS, PAIR, channels)
+    feature_grad = fgrad.transpose(1, 2, 0, 3, 4).reshape(features.shape)
+    feature_grad, total = lax.optimization_barrier((feature_grad, total))
     other = swap_cores(total)
     total = jnp.stack([jnp.where(core == 0, total, other), jnp.where(core == 0, other, total)])
 
@@ -280,8 +283,6 @@
     per_tap = -(-channels // outputs)
     depth_grad = small[:, : 9 * per_tap].reshape(branches, 9, -1)[:, :, :channels].reshape(depth_w.shape)
     bias_grad = small[:, 9 * per_tap].astype(jnp.float32)
-    fgrad = fgrad[:groups].reshape(groups, columns, rows // CLASS, PAIR, channels)
-    feature_grad = fgrad.transpose(1, 2, 0, 3, 4).reshape(features.shape)
     return (feature_grad, depth_grad, point_grad, bias_grad)
 
 

time: 152 us -> 149 us (0.980)
  blocking collectives: 31.2 us -> 14.6 us
  starting transfers between devices: 54.3 us -> 64.9 us
  waiting for transfers between devices: 37.3 us -> 40.2 us
    all_to_all x2 -> x1, blocking collectives: 31.2 us -> 14.6 us  [exchange(): return lax.all_to_all(blocks, axes, 0, 0, tiled=True)]
    all_to_all x2 -> x3, starting transfers between devices: 11.2 us -> 17.9 us  [exchange(): return lax.all_to_all(blocks, axes, 0, 0, tiled=True)]
    all_to_all x2 -> x3, waiting for transfers between devices: 23.2 us -> 29.8 us  [exchange(): return lax.all_to_all(blocks, axes, 0, 0, tiled=True)]
    ppermute x6 -> x4, waiting for transfers between devices: 12.4 us -> 6.97 us  [sum_pair(): lax.ppermute(own, axis, pairs).astype(jnp.float32)]
    ppermute x6 -> x4, starting transfers between devices: 29.1 us -> 31.8 us  [sum_pair(): lax.ppermute(own, axis, pairs).astype(jnp.float32)]
    ppermute x2, waiting for transfers between devices: 1.7 us -> 3.4 us  [swap_cores(): return lax.ppermute(block, 'core', [(0, 1), (1, 0)])]
  transfers between devices with their start and end apart: 10 -> 9, of which waited for: 6 -> 8; matrix products, arithmetic and copies ran while one was open for 2% -> 2% of each run, Pallas kernels for 0% -> 0%
where the time goes in v5:
time: 149 us; the launch traced here: 148 us
  starting transfers between devices  64.9 us (44%)
  waiting for transfers between devices  40.2 us (27%)
  blocking collectives  14.6 us (10%)
  Pallas kernels  14.5 us (10%)
  local copies, waits for them, and re-layouts  9.58 us (6%)
  other arithmetic  3.58 us (2%)
    ppermute x4, starting transfers between devices, sum_pair(): lax.ppermute(own, axis, pairs).astype(jnp.float32)  31.8 us
    all_to_all x3, waiting for transfers between devices, exchange(): return lax.all_to_all(blocks, axes, 0, 0, tiled=True)  29.8 us
    all_to_all x3, starting transfers between devices, exchange(): return lax.all_to_all(blocks, axes, 0, 0, tiled=True)  17.9 us
    ppermute x2, starting transfers between devices, swap_cores(): return lax.ppermute(block, 'core', [(0, 1), (1, 0)])  15.3 us
    all_to_all x1, blocking collectives, exchange(): return lax.all_to_all(blocks, axes, 0, 0, tiled=True)  14.6 us
    pallas_call x1, Pallas kernels, local_work(): pl.pallas_call(local_body, out_shape=(jax.ShapeDtypeStruct((rows, outputs...  14.5 us
    ppermute x4, waiting for transfers between devices, sum_pair(): lax.ppermute(own, axis, pairs).astype(jnp.float32)  6.97 us
    ppermute x2, waiting for transfers between devices, swap_cores(): return lax.ppermute(block, 'core', [(0, 1), (1, 0)])  3.4 us
  transfers between devices with their start and end apart: 9, of which 8 were waited for; matrix products, arithmetic and copies ran while one was open for 2% of the time, Pallas kernels for 0%

profile of v5, /device:TPU:1, one launch (start us, length us, event | category | flops | bytes accessed | tf_op | source)
XLA Modules:
  0.0 148.2 jit_solution(1063523754592233815)
XLA Ops:
  0.6 2.4 %reshape.59 = bf16[9,4,6,2,1152]{4,3,2,1,0:T(2,128)(2,1)S(1)} reshape(bf16[1,9,48,1152]{3,2,1,0:T(8,128)(2,1)} %param.5) | data formatting | bytes 1990656 | tf_op jit(solution)/shard_map/reshape | solution.py:243
  3.1 0.0 copy-start.3
  3.1 0.7 copy.27
  3.8 0.4 reshape.60
  4.2 0.0 copy-done.3
  4.2 0.2 reshape.61
  4.3 0.3 copy.28
  4.7 0.2 reshape.62
  4.8 1.4 fusion.2
  6.3 0.0 copy-start.4
  6.3 0.0 copy-start
  6.3 0.0 copy-start.1
  6.3 7.6 %all-to-all-start = ((bf16[8,9,8,1664]{3,2,1,0:T(8,128)(2,1)}), bf16[8,9,8,1664]{3,2,1,0:T(8,128)(2,1)S(1)}, u32[]{:S(2)}, u32[]{:S(2)}) async-start(bf16[8,9,8,1664]{3,2,1,0:T(8,128)(2,1)} %fusion.2), calls=%async_computation | async-start | bytes 3833856 | tf_op jit(solution)/shard_map/all_to_all | solution.py:24
  13.9 0.0 copy-done.4
  14.0 23.2 %all-to-all-done = bf16[8,9,8,1664]{3,2,1,0:T(8,128)(2,1)S(1)} async-done(((bf16[8,9,8,1664]{3,2,1,0:T(8,128)(2,1)}), bf16[8,9,8,1664]{3,2,1,0:T(8,128)(2,1)S(1)}, u32[]{:S(2)}, u32[]{:S(2)}) %all-to-all-start) | async-done | bytes 1916960 | tf_op jit(solution)/shard_map/all_to_all | solution.py:24
  37.2 0.0 copy-start.2
  37.2 1.3 copy-done.2
  38.5 0.0 copy-done
  38.5 0.0 copy-done.1
  38.5 14.5 %local_work.1 = (f32[1280,256]{1,0:T(8,128)S(1)}, bf16[1280,256]{1,0:T(8,128)(2,1)S(1)}, bf16[576,1152]{1,0:T(8,128)(2,1)}) custom-call(s32[1]{0:T(128)} %bitcast.core_ref, bf16[576,1664]{1,0:T(8,128)(2,1)} %bitcast.28, f32[18,1152]{1,0:T(8,128)S(1)} %reshape.75.taps_ref, bf16[2,1152,256]{2,1,0:T(8,128)(2,1)S(1)} %copy-done, f32[2,256]{1,0:T(2,128)S(1)} %copy-done.1), custom_call_target="tpu_custom_call" | custom-call | tf_op jit(solution)/shard_map/local_work/pallas_call | solution.py:221
  53.0 6.1 %collective-permute-start = (bf16[1280,256]{1,0:T(8,128)(2,1)S(1)}, bf16[1280,256]{1,0:T(8,128)(2,1)S(1)}, u32[]{:S(2)}, u32[]{:S(2)}) collective-permute-start(bf16[1280,256]{1,0:T(8,128)(2,1)S(1)} %get-tuple-element.15), channel_id=1, source_target_pairs={{0,8},{8,0},{1,9},{9,1},{2,10},{10,2},{3,11},{11,3},{4,12},{12,4},... | collective-permute-start | bytes 1966088 | tf_op jit(solution)/shard_map/ppermute | solution.py:20
  59.0 1.7 %collective-permute-done = bf16[1280,256]{1,0:T(8,128)(2,1)S(1)} collective-permute-done((bf16[1280,256]{1,0:T(8,128)(2,1)S(1)}, bf16[1280,256]{1,0:T(8,128)(2,1)S(1)}, u32[]{:S(2)}, u32[]{:S(2)}) %collective-permute-start) | collective-permute-done | bytes 655392 | tf_op jit(solution)/shard_map/ppermute | solution.py:20
  60.7 0.2 add_convert_fusion
  60.9 14.6 %all_to_all.20 = bf16[16,80,256]{2,1,0:T(8,128)(2,1)S(1)} all-to-all(bf16[16,80,256]{2,1,0:T(8,128)(2,1)S(1)} %bitcast.31), channel_id=1, replica_groups=mesh['zh'=4,'zl'=4,'xl'=2,'core'=2,'y'=4,'xh'=2] {'xl','y','xh'}, dimensions={0} | all-to-all | bytes 1310720 | tf_op jit(solution)/shard_map/all_to_all | solution.py:24
  75.5 3.6 %all-to-all-start.2 = ((bf16[8,9,8,1152]{3,2,1,0:T(8,128)(2,1)}), bf16[8,9,8,1152]{3,2,1,0:T(8,128)(2,1)S(1)}, u32[]{:S(2)}, u32[]{:S(2)}) async-start(bf16[8,9,8,1152]{3,2,1,0:T(8,128)(2,1)} %bitcast.5), calls=%async_computation.2 | async-start | bytes 2654208 | tf_op jit(solution)/shard_map/all_to_all | solution.py:24
  79.1 0.1 convert_reduce_fusion
  79.2 3.6 %collective-permute-start.1 = (f32[80,256]{1,0:T(8,128)S(1)}, f32[80,256]{1,0:T(8,128)S(1)}, u32[]{:S(2)}, u32[]{:S(2)}) collective-permute-start(f32[80,256]{1,0:T(8,128)S(1)} %convert_reduce_fusion), channel_id=1, source_target_pairs={{0,32},{32,0},{64,96},{96,64},{1,33},{33,1},{65,97},{97,65},{2,34}... | collective-permute-start | bytes 245768 | tf_op jit(solution)/shard_map/ppermute | solution.py:34
  82.8 2.1 %collective-permute-done.1 = f32[80,256]{1,0:T(8,128)S(1)} collective-permute-done((f32[80,256]{1,0:T(8,128)S(1)}, f32[80,256]{1,0:T(8,128)S(1)}, u32[]{:S(2)}, u32[]{:S(2)}) %collective-permute-start.1) | collective-permute-done | bytes 81952 | tf_op jit(solution)/shard_map/ppermute | solution.py:34
  85.0 4.9 %collective-permute-start.2 = (f32[80,256]{1,0:T(8,128)S(1)}, f32[80,256]{1,0:T(8,128)S(1)}, u32[]{:S(2)}, u32[]{:S(2)}) collective-permute-start(f32[80,256]{1,0:T(8,128)S(1)} %add.18), channel_id=1, source_target_pairs={{0,64},{32,96},{64,0},{96,32},{1,65},{33,97},{65,1},{97,33},{2,66}... | collective-permute-start | bytes 245768 | tf_op jit(solution)/shard_map/ppermute | solution.py:34
  89.9 2.1 %collective-permute-done.2 = f32[80,256]{1,0:T(8,128)S(1)} collective-permute-done((f32[80,256]{1,0:T(8,128)S(1)}, f32[80,256]{1,0:T(8,128)S(1)}, u32[]{:S(2)}, u32[]{:S(2)}) %collective-permute-start.2) | collective-permute-done | bytes 81952 | tf_op jit(solution)/shard_map/ppermute | solution.py:34
  92.0 8.8 %collective-permute-start.3 = (bf16[80,256]{1,0:T(8,128)(2,1)S(1)}, bf16[80,256]{1,0:T(8,128)(2,1)S(1)}, u32[]{:S(2)}, u32[]{:S(2)}) collective-permute-start(bf16[80,256]{1,0:T(8,128)(2,1)S(1)} %add_convert_fusion.2), channel_id=1, source_target_pairs={{0,128},{128,0},{256,384},{384,256},{1,129},{129,1},{257,385},{385... | collective-permute-start | bytes 122888 | tf_op jit(solution)/shard_map/ppermute | solution.py:34
  100.8 1.4 collective-permute-done.3
  102.2 14.4 %collective-permute-start.4 = (bf16[80,256]{1,0:T(8,128)(2,1)S(1)}, bf16[80,256]{1,0:T(8,128)(2,1)S(1)}, u32[]{:S(2)}, u32[]{:S(2)}) collective-permute-start(bf16[80,256]{1,0:T(8,128)(2,1)S(1)} %add_convert_fusion.1), channel_id=1, source_target_pairs={{0,256},{128,384},{256,0},{384,128},{1,257},{129,385},{257,1},{385... | collective-permute-start | bytes 122888 | tf_op jit(solution)/shard_map/ppermute | solution.py:34
  116.6 1.4 collective-permute-done.4
  118.0 0.0 all-to-all-done.2
  118.0 0.9 broadcast_in_dim.2
  118.9 6.7 %all-to-all-start.3 = ((bf16[16,80,256]{2,1,0:T(8,128)(2,1)}), bf16[16,80,256]{2,1,0:T(8,128)(2,1)S(1)}, u32[]{:S(2)}, u32[]{:S(2)}) async-start(bf16[16,80,256]{2,1,0:T(8,128)(2,1)} %broadcast_in_dim.2), calls=%async_computation.3 | async-start | bytes 1310720 | tf_op jit(solution)/shard_map/all_to_all | solution.py:24
  125.6 0.1 slice.18
  125.7 0.4 reshape.68
  126.1 0.7 copy.38
  126.8 1.3 reshape.69
  128.1 6.6 %all-to-all-done.3 = bf16[16,80,256]{2,1,0:T(8,128)(2,1)S(1)} async-done(((bf16[16,80,256]{2,1,0:T(8,128)(2,1)}), bf16[16,80,256]{2,1,0:T(8,128)(2,1)S(1)}, u32[]{:S(2)}, u32[]{:S(2)}) %all-to-all-start.3) | async-done | bytes 655392 | tf_op jit(solution)/shard_map/all_to_all | solution.py:24
  134.7 9.2 %collective-permute-start.5 = (bf16[16,80,256]{2,1,0:T(8,128)(2,1)S(1)}, bf16[16,80,256]{2,1,0:T(8,128)(2,1)S(1)}, u32[]{:S(2)}, u32[]{:S(2)}) collective-permute-start(bf16[16,80,256]{2,1,0:T(8,128)(2,1)S(1)} %all-to-all-done.3), channel_id=1, source_target_pairs={{0,8},{8,0},{1,9},{9,1},{2,10},{10,2},{3,11},{11,3},{4,12},{12,4},... | collective-permute-start | bytes 1966088 | tf_op jit(solution)/shard_map/ppermute | solution.py:20
  143.9 1.7 %collective-permute-done.5 = bf16[16,80,256]{2,1,0:T(8,128)(2,1)S(1)} collective-permute-done((bf16[16,80,256]{2,1,0:T(8,128)(2,1)S(1)}, bf16[16,80,256]{2,1,0:T(8,128)(2,1)S(1)}, u32[]{:S(2)}, u32[]{:S(2)}) %collective-permute-start.5) | collective-permute-done | bytes 655392 | tf_op jit(solution)/shard_map/ppermute | solution.py:20
  145.6 0.2 select_bitcast_fusion.1
  145.8 1.1 pad_maximum_fusion
  146.9 0.1 reshape.71
  147.0 0.7 copy.31
  147.6 0.6 fusion.3
  (10 shorter events, 0.1 us)
Async XLA Ops:
  3.1 1.1 copy-start.3
  6.3 7.6 %copy-start.4 = (bf16[2,3,3,1152]{3,0,2,1:T(2,128)(2,1)S(1)}, bf16[2,3,3,1152]{3,0,2,1:T(2,128)(2,1)}, u32[]{:S(2)}) copy-start(bf16[2,3,3,1152]{3,0,2,1:T(2,128)(2,1)} %param.6) | copy-start | bytes 124420
  6.3 32.2 %copy-start = (bf16[2,1152,256]{2,1,0:T(8,128)(2,1)S(1)}, bf16[2,1152,256]{2,1,0:T(8,128)(2,1)}, u32[]{:S(2)}) copy-start(bf16[2,1152,256]{2,1,0:T(8,128)(2,1)} %pw_ref.1) | copy-start | bytes 3538948
  6.3 32.2 %copy-start.1 = (f32[2,256]{1,0:T(2,128)S(1)}, f32[2,256]{1,0:T(2,128)}, u32[]{:S(2)}) copy-start(f32[2,256]{1,0:T(2,128)} %pb_ref.1) | copy-start | bytes 6148
  6.3 30.9 %all-to-all-start = ((bf16[8,9,8,1664]{3,2,1,0:T(8,128)(2,1)}), bf16[8,9,8,1664]{3,2,1,0:T(8,128)(2,1)S(1)}, u32[]{:S(2)}, u32[]{:S(2)}) async-start(bf16[8,9,8,1664]{3,2,1,0:T(8,128)(2,1)} %fusion.2), calls=%async_computation | async-start | bytes 3833856 | tf_op jit(solution)/shard_map/all_to_all | solution.py:24
  37.2 1.3 copy-start.2
  53.0 7.8 %collective-permute-start = (bf16[1280,256]{1,0:T(8,128)(2,1)S(1)}, bf16[1280,256]{1,0:T(8,128)(2,1)S(1)}, u32[]{:S(2)}, u32[]{:S(2)}) collective-permute-start(bf16[1280,256]{1,0:T(8,128)(2,1)S(1)} %get-tuple-element.15), channel_id=1, source_target_pairs={{0,8},{8,0},{1,9},{9,1},{2,10},{10,2},{3,11},{11,3},{4,12},{12,4},... | collective-permute-start | bytes 1966088 | tf_op jit(solution)/shard_map/ppermute | solution.py:20
  75.5 42.5 %all-to-all-start.2 = ((bf16[8,9,8,1152]{3,2,1,0:T(8,128)(2,1)}), bf16[8,9,8,1152]{3,2,1,0:T(8,128)(2,1)S(1)}, u32[]{:S(2)}, u32[]{:S(2)}) async-start(bf16[8,9,8,1152]{3,2,1,0:T(8,128)(2,1)} %bitcast.5), calls=%async_computation.2 | async-start | bytes 2654208 | tf_op jit(solution)/shard_map/all_to_all | solution.py:24
  79.2 5.7 %collective-permute-start.1 = (f32[80,256]{1,0:T(8,128)S(1)}, f32[80,256]{1,0:T(8,128)S(1)}, u32[]{:S(2)}, u32[]{:S(2)}) collective-permute-start(f32[80,256]{1,0:T(8,128)S(1)} %convert_reduce_fusion), channel_id=1, source_target_pairs={{0,32},{32,0},{64,96},{96,64},{1,33},{33,1},{65,97},{97,65},{2,34}... | collective-permute-start | bytes 245768 | tf_op jit(solution)/shard_map/ppermute | solution.py:34
  85.0 7.0 %collective-permute-start.2 = (f32[80,256]{1,0:T(8,128)S(1)}, f32[80,256]{1,0:T(8,128)S(1)}, u32[]{:S(2)}, u32[]{:S(2)}) collective-permute-start(f32[80,256]{1,0:T(8,128)S(1)} %add.18), channel_id=1, source_target_pairs={{0,64},{32,96},{64,0},{96,32},{1,65},{33,97},{65,1},{97,33},{2,66}... | collective-permute-start | bytes 245768 | tf_op jit(solution)/shard_map/ppermute | solution.py:34
  92.0 10.2 %collective-permute-start.3 = (bf16[80,256]{1,0:T(8,128)(2,1)S(1)}, bf16[80,256]{1,0:T(8,128)(2,1)S(1)}, u32[]{:S(2)}, u32[]{:S(2)}) collective-permute-start(bf16[80,256]{1,0:T(8,128)(2,1)S(1)} %add_convert_fusion.2), channel_id=1, source_target_pairs={{0,128},{128,0},{256,384},{384,256},{1,129},{129,1},{257,385},{385... | collective-permute-start | bytes 122888 | tf_op jit(solution)/shard_map/ppermute | solution.py:34
  102.2 15.8 %collective-permute-start.4 = (bf16[80,256]{1,0:T(8,128)(2,1)S(1)}, bf16[80,256]{1,0:T(8,128)(2,1)S(1)}, u32[]{:S(2)}, u32[]{:S(2)}) collective-permute-start(bf16[80,256]{1,0:T(8,128)(2,1)S(1)} %add_convert_fusion.1), channel_id=1, source_target_pairs={{0,256},{128,384},{256,0},{384,128},{1,257},{129,385},{257,1},{385... | collective-permute-start | bytes 122888 | tf_op jit(solution)/shard_map/ppermute | solution.py:34
  118.9 15.7 %all-to-all-start.3 = ((bf16[16,80,256]{2,1,0:T(8,128)(2,1)}), bf16[16,80,256]{2,1,0:T(8,128)(2,1)S(1)}, u32[]{:S(2)}, u32[]{:S(2)}) async-start(bf16[16,80,256]{2,1,0:T(8,128)(2,1)} %broadcast_in_dim.2), calls=%async_computation.3 | async-start | bytes 1310720 | tf_op jit(solution)/shard_map/all_to_all | solution.py:24
  134.7 11.0 %collective-permute-start.5 = (bf16[16,80,256]{2,1,0:T(8,128)(2,1)S(1)}, bf16[16,80,256]{2,1,0:T(8,128)(2,1)S(1)}, u32[]{:S(2)}, u32[]{:S(2)}) collective-permute-start(bf16[16,80,256]{2,1,0:T(8,128)(2,1)S(1)} %all-to-all-done.3), channel_id=1, source_target_pairs={{0,8},{8,0},{1,9},{9,1},{2,10},{10,2},{3,11},{11,3},{4,12},{12,4},... | collective-permute-start | bytes 1966088 | tf_op jit(solution)/shard_map/ppermute | solution.py:20

commit v6 on v5

v6 whole, which is shorter than its diff:
```python
import jax
import jax.numpy as jnp
import numpy as np
from jax import lax
from jax.experimental import pallas as pl
from jax.experimental.pallas import tpu as pltpu
from jax.sharding import Mesh
from jax.sharding import PartitionSpec as P

CLASS = 12
PAIRS = 6
PEERS = 8
SLOTS = 7
HELD = 8
LANES = 128

DP = ("zh", "zl", "xl", "core")
LON = ("y", "xh")
PLANE = ("xl", "y", "xh")


def swap_cores(block):
    return lax.ppermute(block, "core", [(0, 1), (1, 0)])


def exchange(blocks, axes):
    return lax.all_to_all(blocks, axes, 0, 0, tiled=True)


def gather_copies(block, axes):
    peers = lax.axis_size(axes)
    return exchange(jnp.broadcast_to(block[None], (peers,) + block.shape), axes)


def sum_pair(own, axis, apart):
    pairs = [(i, i ^ apart) for i in range(lax.axis_size(axis))]
    return own.astype(jnp.float32) + lax.ppermute(own, axis, pairs).astype(jnp.float32)


def deal_units(columns):
    blocks = CLASS // 3
    owned = [[] for _ in range(PEERS)]
    for m in range(blocks):
        units = iter([(c, q) for q in range(PAIRS) for c in range(3 * m, 3 * m + 3)])
        for e in range(PEERS):
            owned[e] += [next(units) for _ in range(2 + (e % blocks == m))]
    home = np.zeros((PEERS, columns * PAIRS), np.int32)
    away = np.zeros((PEERS, columns * PAIRS), np.int32)
    used = np.zeros((PEERS, PEERS), np.int32)
    for e in range(PEERS):
        for u, (c, q) in enumerate(owned[e]):
            for k in range(6):
                d, j = divmod(c + CLASS * k, columns)
                home[d, j * PAIRS + q] = e * SLOTS + used[d, e]
                away[e, u * 6 + k] = d * SLOTS + used[d, e]
                used[d, e] += 1
    assert used.max() == SLOTS and used.min() == SLOTS - 1
    return home.reshape(-1), away.reshape(-1)


def blank_slots(ref, lon):
    for block in (3 - lon % 4, 7 - lon % 4):
        ref[block * SLOTS + SLOTS - 1] = jnp.zeros(ref.shape[1:], ref.dtype)


def pack_body(who_ref, home_ref, feat_ref, cot_ref, out_ref):
    columns, _, channels = feat_ref.shape
    lon = who_ref[0]
    blank_slots(out_ref, lon)

    def column(j, carry):
        for source, start in ((feat_ref, 0), (cot_ref, channels)):
            width = source.shape[2]
            rows = source[j].astype(jnp.float32)
            for q in range(PAIRS):
                slot = home_ref[(lon * columns + j) * PAIRS + q]
                tile = jnp.concatenate([rows[12 * n + 2 * q : 12 * n + 2 * q + 2] for n in range(4)], axis=0)
                out_ref[slot, :, start : start + width] = tile.astype(out_ref.dtype)
        return carry

    lax.fori_loop(0, columns, column, 0)


def unpack_body(who_ref, home_ref, tiles_ref, out_ref):
    columns = out_ref.shape[0]
    lon = who_ref[0]

    def column(j, carry):
        tiles = [tiles_ref[home_ref[(lon * columns + j) * PAIRS + q]].astype(jnp.float32) for q in range(PAIRS)]
        rows = [tiles[q][2 * n : 2 * n + 2] for n in range(4) for q in range(PAIRS)]
        out_ref[j] = jnp.concatenate(rows, axis=0).astype(out_ref.dtype)
        return carry

    lax.fori_loop(0, columns, column, 0)


def on_chip(body, out_shape, scalars, arrays, scratch=(), name=None):
    vmem = pl.BlockSpec(memory_space=pltpu.VMEM)
    smem = pl.BlockSpec(memory_space=pltpu.SMEM)
    return pl.pallas_call(
        body,
        out_shape=out_shape,
        in_specs=[smem] * len(scalars) + [vmem] * len(arrays),
        out_specs=jax.tree.map(lambda _: vmem, out_shape),
        scratch_shapes=list(scratch),
        compiler_params=pltpu.CompilerParams(vmem_limit_bytes=48 << 20),
        name=name,
    )(*scalars, *arrays)


def gate_slope(pre_act):
    sigmoid_val = jax.nn.sigmoid(pre_act)
    return sigmoid_val * (1.0 + pre_act * (1.0 - sigmoid_val))


def half_turn(tile):
    return pltpu.roll(tile, 4, 0)


def ends_swapped(tile, top):
    return jnp.where(top, pltpu.roll(tile, 2, 0), pltpu.roll(tile, 6, 0))


def shard_row(row, main, extra):
    return (row // extra) * (main + extra) + main + row % extra


def local_body(
    who_ref, core_ref, away_ref, cls_ref, taps_ref, pw_ref, pb_ref, kept_ref, sent_ref, fg_ref, depth, dgr, upstream, terms
):
    channels, outputs = pw_ref.shape[1:]
    shard = terms.shape[1] // 16
    main = channels // 16
    extra = shard - main
    tiles = channels // LANES
    wide = outputs // LANES
    per_tap = -(-tiles // wide)
    sub = lax.broadcasted_iota(jnp.int32, (HELD, LANES), 0)
    top = sub < 4
    first = sub < 2
    end = sub >= 6

    def tap(branch, a, e, lanes):
        row = branch * 9 + (a + 1) * 3 + e + 1
        return jnp.broadcast_to(taps_ref[row : row + 1, lanes], (HELD, LANES))

    def ends(up, down):
        return jnp.where(first, up, jnp.where(end, down, 0.0))

    def both(branch, a, lanes):
        return tap(branch, a, -1, lanes) + tap(branch, a, 1, lanes)

    units = depth.shape[1] // (6 * HELD)
    lon = who_ref[0]
    blank_slots(fg_ref, lon)

    def slots(u):
        return [away_ref[(lon * units + u) * 6 + k] for k in range(6)]

    def pair_rows(u, k):
        return pl.ds(pl.multiple_of((u * 6 + k) * HELD, 16), 16)

    def read_pairs(ref, branch, u, lanes):
        out = []
        for k in range(0, 6, 2):
            pair = ref[branch, pair_rows(u, k), lanes].astype(jnp.float32)
            out += [pair[:HELD], pair[HELD:]]
        return out

    def write_pairs(ref, branch, u, lanes, made):
        for k in range(0, 6, 2):
            pair = jnp.concatenate([made[k], made[k + 1]], axis=0)
            ref[branch, pair_rows(u, k), lanes] = pair.astype(jnp.bfloat16)

    def gather_upstream(u, carry):
        at = slots(u)
        for k in range(0, 6, 2):
            for c in range(channels, cls_ref.shape[2], LANES):
                lanes = slice(c, c + LANES)
                pair = jnp.concatenate([cls_ref[at[k + n], :, lanes].astype(jnp.float32) for n in range(2)], axis=0)
                upstream[pair_rows(u, k), c - channels : c - channels + LANES] = pair
        return carry

    lax.fori_loop(0, units, gather_upstream, 0)

    for t in range(tiles):
        lanes = slice(t * LANES, (t + 1) * LANES)
        mid_a = [tap(0, 0, e, lanes) for e in (-1, 0, 1)]
        off_a = [jnp.where(top, tap(0, 1, e, lanes), tap(0, -1, e, lanes)) for e in (-1, 0, 1)]
        mid_b = [tap(1, 0, 0, lanes), both(1, 0, lanes)]
        off_b = [
            ends(tap(1, 1, 0, lanes), tap(1, -1, 0, lanes)),
            ends(both(1, 1, lanes), both(1, -1, lanes)),
        ]

        def forward(u, carry):
            xs = [cls_ref[slot, :, lanes].astype(jnp.float32) for slot in slots(u)]
            turned = [half_turn(x) for x in xs]
            swapped = [ends_swapped(x, top) for x in xs]
            made_a = [
                sum(
                    mid_a[n] * xs[(k + 2 * n - 2) % 6] + off_a[n] * turned[(k + 2 * n - 2) % 6] for n in range(3)
                )
                for k in range(6)
            ]
            made_b = [
                mid_b[0] * xs[k]
                + mid_b[1] * xs[(k + 3) % 6]
                + off_b[0] * swapped[k]
                + off_b[1] * swapped[(k + 3) % 6]
                for k in range(6)
            ]
            write_pairs(depth, 0, u, lanes, made_a)
            write_pairs(depth, 1, u, lanes, made_b)
            return carry

        lax.fori_loop(0, units, forward, 0)

    for branch in range(2):
        act = jnp.dot(depth[branch], pw_ref[branch], preferred_element_type=jnp.float32)
        act = act + pb_ref[branch : branch + 1, :]
        up = upstream[:, branch * outputs : (branch + 1) * outputs]
        pgrad = (up * gate_slope(act)).astype(jnp.bfloat16)
        point = lax.dot_general(
            depth[branch], pgrad, (((0,), (0,)), ((), ())), preferred_element_type=jnp.float32
        )
        for p in range(16):
            terms[branch, p * shard : p * shard + main, :] = point[p * main : (p + 1) * main]
            terms[branch, p * shard + main : (p + 1) * shard, :] = jnp.zeros((extra, outputs), jnp.float32)
        row = shard_row(9 * per_tap, main, extra)
        terms[branch, row : row + 1, :] = jnp.sum(pgrad.astype(jnp.float32), axis=0, keepdims=True)
        for c in range(0, channels, 384):
            part = lax.dot_general(
                pgrad, pw_ref[branch, c : c + 384, :], (((1,), (1,)), ((), ())), preferred_element_type=jnp.float32
            )
            dgr[branch, :, c : c + 384] = part.astype(jnp.bfloat16)

    for t in range(tiles):
        lanes = slice(t * LANES, (t + 1) * LANES)
        mid_a = [tap(0, 0, e, lanes) for e in (-1, 0, 1)]
        off_a = [jnp.where(top, tap(0, -1, e, lanes), tap(0, 1, e, lanes)) for e in (-1, 0, 1)]
        mid_b = [tap(1, 0, 0, lanes), both(1, 0, lanes)]
        off_b = [
            ends(tap(1, -1, 0, lanes), tap(1, 1, 0, lanes)),
            ends(both(1, -1, lanes), both(1, 1, lanes)),
        ]

        def backward(u, sums):
            sums = list(sums)
            at = slots(u)
            xs = [cls_ref[slot, :, lanes].astype(jnp.float32) for slot in at]
            das = read_pairs(dgr, 0, u, lanes)
            dbs = read_pairs(dgr, 1, u, lanes)
            turned = [half_turn(d) for d in das]
            swapped = [ends_swapped(d, top) for d in dbs]
            for k in range(6):
                made = (
                    sum(
                        mid_a[n] * das[(k - 2 * n + 2) % 6] + off_a[n] * turned[(k - 2 * n + 2) % 6]
                        for n in range(3)
                    )
                    + mid_b[0] * dbs[k]
                    + mid_b[1] * dbs[(k + 3) % 6]
                    + off_b[0] * swapped[k]
                    + off_b[1] * swapped[(k + 3) % 6]
                )
                fg_ref[at[k], :, lanes] = made.astype(jnp.bfloat16)
            for n in range(3):
                sums[n] += sum(xs[(k + 2 * n - 2) % 6] * das[k] for k in range(6))
                sums[3 + n] += sum(xs[(k + 2 * n - 2) % 6] * turned[k] for k in range(6))
            for n in range(2):
                sums[6 + n] += sum(xs[(k + 3 * n) % 6] * dbs[k] for k in range(6))
                sums[8 + n] += sum(xs[(k + 3 * n) % 6] * swapped[k] for k in range(6))
            return tuple(sums)

        zero = jnp.zeros((HELD, LANES), jnp.float32)
        sums = lax.fori_loop(0, units, backward, (zero,) * 10)

        def keep(branch, a, e, value, mask=None):
            value = value if mask is None else jnp.where(mask, value, 0.0)
            row = shard_row(((a + 1) * 3 + e + 1) * per_tap + t // wide, main, extra)
            at = (t % wide) * LANES
            terms[branch, row : row + 1, at : at + LANES] = jnp.sum(value, axis=0, keepdims=True)

        for n in range(3):
            keep(0, 0, n - 1, sums[n])
            keep(0, 1, n - 1, sums[3 + n], jnp.logical_not(top))
            keep(0, -1, n - 1, sums[3 + n], top)
        for e in (-1, 0, 1):
            keep(1, 0, e, sums[6 + abs(e)])
            keep(1, 1, e, sums[8 + abs(e)], end)
            keep(1, -1, e, sums[8 + abs(e)], first)

    @pl.when(core_ref[0] == 0)
    def _():
        kept_ref[...] = terms[0]
        sent_ref[...] = terms[1].astype(jnp.bfloat16)

    @pl.when(core_ref[0] != 0)
    def _():
        kept_ref[...] = terms[1]
        sent_ref[...] = terms[0].astype(jnp.bfloat16)


def per_device(features, depth_w, point_w, point_bias, cotangent):
    _, columns, rows, channels = features.shape
    branches, _, outputs = point_w.shape
    images = lax.axis_size(DP) * features.shape[0]
    plane = lax.axis_size(PLANE)
    core = lax.axis_index("core")
    who = lax.axis_index(LON).reshape(1)
    home, away = deal_units(columns)
    cells = columns * rows
    packed_rows = 16 * (channels // 16 + 8)
    width = channels + cotangent.shape[3]
    act = jnp.bfloat16

    packed = on_chip(
        pack_body,
        jax.ShapeDtypeStruct((PEERS * SLOTS, HELD, width), act),
        (who, home),
        (features[0], cotangent[0]),
        name="pack",
    )
    field = exchange(packed.reshape(PEERS, SLOTS, HELD, width), LON).reshape(packed.shape)
    taps = depth_w.astype(jnp.float32).reshape(branches * 9, channels)
    kept, sent, fgrad = on_chip(
        local_body,
        (
            jax.ShapeDtypeStruct((packed_rows, outputs), jnp.float32),
            jax.ShapeDtypeStruct((packed_rows, outputs), act),
            jax.ShapeDtypeStruct((PEERS * SLOTS, HELD, channels), act),
        ),
        (who, core.reshape(1), away),
        (field, taps, point_w, point_bias),
        (
            pltpu.VMEM((branches, cells, channels), act),
            pltpu.VMEM((branches, cells, channels), act),
            pltpu.VMEM((cells, branches * outputs), jnp.float32),
            pltpu.VMEM((branches, packed_rows, outputs), jnp.float32),
        ),
        name="local_work",
    )

    terms = (kept + swap_cores(sent).astype(jnp.float32)).astype(jnp.bfloat16)
    shard = terms.shape[0] // plane
    terms = exchange(terms.reshape(plane, shard, outputs), PLANE)
    fgrad, terms = lax.optimization_barrier((fgrad, terms))
    fgrad = exchange(fgrad.reshape(PEERS, SLOTS, HELD, channels), LON)
    terms = jnp.sum(terms.astype(jnp.float32), axis=0)
    terms = sum_pair(sum_pair(terms, "zl", 1), "zl", 2)
    terms = sum_pair(terms.astype(jnp.bfloat16), "zh", 1)
    terms = sum_pair(terms.astype(jnp.bfloat16), "zh", 2)
    total = (terms / images).astype(jnp.bfloat16)
    fgrad, total = lax.optimization_barrier((fgrad, total))
    total = gather_copies(total, PLANE)
    feature_grad = on_chip(
        unpack_body,
        jax.ShapeDtypeStruct((columns, rows, channels), act),
        (who, home),
        (fgrad.reshape(PEERS * SLOTS, HELD, channels),),
        name="unpack",
    )[None]
    feature_grad, total = lax.optimization_barrier((feature_grad, total))
    other = swap_cores(total)
    total = jnp.stack([jnp.where(core == 0, total, other), jnp.where(core == 0, other, total)])

    main = channels // plane
    point_grad = total[:, :, :main].reshape(point_w.shape)
    small = total[:, :, main:].reshape(branches, -1, outputs)
    per_tap = -(-channels // outputs)
    depth_grad = small[:, : 9 * per_tap].reshape(branches, 9, -1)[:, :, :channels].reshape(depth_w.shape)
    bias_grad = small[:, 9 * per_tap].astype(jnp.float32)
    return (feature_grad, depth_grad, point_grad, bias_grad)


def solution(mesh):
    fine = Mesh(mesh.devices.reshape(4, 4, 2, 2, 4, 2), DP + LON)
    placed = (P(DP, LON, None, None), P(), P(), P(), P(DP, LON, None, None))
    return jax.shard_map(
        per_device,
        mesh=fine,
        in_specs=placed,
        out_specs=(P(DP, LON, None, None), P(), P(), P()),
        check_vma=False,
    )
```

time: 149 us -> 135 us (0.906)
  waiting for transfers between devices: 40.2 us -> 34.5 us
  local copies, waits for them, and re-layouts: 9.58 us -> 4.59 us
  starting transfers between devices: 64.9 us -> 63.4 us
  other arithmetic: 3.58 us -> 2.08 us
    reshape x7 -> x0, local copies, waits for them, and re-layouts: 5.54 us -> none  [the longest x2 2.61 us: to_chunks(): field.reshape(columns, rows // CLASS, groups, PAIR, width)]
    all_to_all x3, waiting for transfers between devices: 29.8 us -> 25.6 us  [exchange(): return lax.all_to_all(blocks, axes, 0, 0, tiled=True)]
    unnamed x10 -> x18, local copies, waits for them, and re-layouts: 1.3 us -> 2.92 us
    ppermute x4, waiting for transfers between devices: 6.97 us -> 5.47 us  [sum_pair(): lax.ppermute(own, axis, pairs).astype(jnp.float32)]
    pallas_call x1 -> x3, Pallas kernels: 14.5 us -> 14.6 us  [on_chip(): pl.pallas_call(body, out_shape=out_shape, in_specs=[smem] * len(scalars)...]
  transfers between devices with their start and end apart: 9 -> 9, of which waited for: 8 -> 7; matrix products, arithmetic and copies ran while one was open for 2% -> 0% of each run, Pallas kernels for 0% -> 2%
where the time goes in v6:
time: 135 us
  starting transfers between devices  63.4 us (47%)
  waiting for transfers between devices  34.5 us (26%)
  blocking collectives  14.7 us (11%)
  Pallas kernels  14.6 us (11%)
  local copies, waits for them, and re-layouts  4.59 us (3%)
  other arithmetic  2.08 us (2%)
    ppermute x4, starting transfers between devices, sum_pair(): lax.ppermute(own, axis, pairs).astype(jnp.float32)  30.6 us
    all_to_all x3, waiting for transfers between devices, exchange(): return lax.all_to_all(blocks, axes, 0, 0, tiled=True)  25.6 us
    all_to_all x3, starting transfers between devices, exchange(): return lax.all_to_all(blocks, axes, 0, 0, tiled=True)  17.7 us
    ppermute x2, starting transfers between devices, swap_cores(): return lax.ppermute(block, 'core', [(0, 1), (1, 0)])  15.1 us
    all_to_all x1, blocking collectives, exchange(): return lax.all_to_all(blocks, axes, 0, 0, tiled=True)  14.7 us
    pallas_call x3, Pallas kernels, on_chip(): pl.pallas_call(body, out_shape=out_shape, in_specs=[smem] * len(scalars)...  14.6 us
    ppermute x4, waiting for transfers between devices, sum_pair(): lax.ppermute(own, axis, pairs).astype(jnp.float32)  5.47 us
    ppermute x2, waiting for transfers between devices, swap_cores(): return lax.ppermute(block, 'core', [(0, 1), (1, 0)])  3.4 us
  transfers between devices with their start and end apart: 9, of which 7 were waited for; matrix products, arithmetic and copies ran while one was open for 0% of the time, Pallas kernels for 2%

profile of v6, /device:TPU:1, one launch (start us, length us, event | category | flops | bytes accessed | tf_op | source)
XLA Modules:
  0.0 134.7 jit_solution(11987218635664330669)
XLA Ops:
  0.6 0.0 copy-start.2
  0.6 1.2 copy-done.2
  1.8 0.0 copy-start.3
  1.8 1.0 copy-done.3
  2.9 0.0 copy-start.4
  2.9 0.7 copy-done.4
  3.5 2.5 %pack.1 = bf16[56,8,1664]{2,1,0:T(8,128)(2,1)} custom-call(s32[1]{0:T(128)} %bitcast.who_ref, s32[432]{0:T(512)S(1)} %copy-done.4, bf16[9,48,1152]{2,1,0:T(8,128)(2,1)S(1)} %bitcast.26, bf16[9,48,512]{2,1,0:T(8,128)(2,1)S(1)} %bitcast.27), custom_call_target="tpu_custom_call" | custom-call | tf_op jit(solution)/shard_map/pack/pallas_call | solution.py:100
  6.0 0.0 copy-start.8
  6.0 0.0 copy-start
  6.0 0.0 copy-start.6
  6.0 0.0 copy-start.7
  6.0 7.6 %all-to-all-start = ((bf16[8,7,8,1664]{3,2,1,0:T(8,128)(2,1)}), bf16[8,7,8,1664]{3,2,1,0:T(8,128)(2,1)S(1)}, u32[]{:S(2)}, u32[]{:S(2)}) async-start(bf16[8,7,8,1664]{3,2,1,0:T(8,128)(2,1)} %bitcast.4), calls=%async_computation | async-start | bytes 2981888 | tf_op jit(solution)/shard_map/all_to_all | solution.py:27
  13.6 0.0 copy-done.8
  13.7 18.7 %all-to-all-done = bf16[8,7,8,1664]{3,2,1,0:T(8,128)(2,1)S(1)} async-done(((bf16[8,7,8,1664]{3,2,1,0:T(8,128)(2,1)}), bf16[8,7,8,1664]{3,2,1,0:T(8,128)(2,1)S(1)}, u32[]{:S(2)}, u32[]{:S(2)}) %all-to-all-start) | async-done | bytes 1490976 | tf_op jit(solution)/shard_map/all_to_all | solution.py:27
  32.4 0.0 copy-done
  32.4 0.0 copy-done.6
  32.4 0.0 copy-done.7
  32.4 10.0 %local_work.1 = (f32[1280,256]{1,0:T(8,128)S(1)}, bf16[1280,256]{1,0:T(8,128)(2,1)S(1)}, bf16[56,8,1152]{2,1,0:T(8,128)(2,1)S(1)}) custom-call(s32[1]{0:T(128)} %bitcast.who_ref, s32[1]{0:T(128)} %bitcast.1.core_ref, s32[432]{0:T(512)S(1)} %copy-done.7, bf16[56,8,1664]{2,1,0:T(8,128)(2,1)S(1)} %bitcast.23, f32[18,1152]{1,0:T(8,128)S(1)} %reshape.63.taps_ref, ...), custom_call_target="tpu_custom_call" | custom-call | tf_op jit(solution)/shard_map/local_work/pallas_call | solution.py:100
  42.4 0.0 copy-start.1
  42.4 6.0 %collective-permute-start = (bf16[1280,256]{1,0:T(8,128)(2,1)S(1)}, bf16[1280,256]{1,0:T(8,128)(2,1)S(1)}, u32[]{:S(2)}, u32[]{:S(2)}) collective-permute-start(bf16[1280,256]{1,0:T(8,128)(2,1)S(1)} %get-tuple-element.15), channel_id=1, source_target_pairs={{0,8},{8,0},{1,9},{9,1},{2,10},{10,2},{3,11},{11,3},{4,12},{12,4},... | collective-permute-start | bytes 1966088 | tf_op jit(solution)/shard_map/ppermute | solution.py:23
  48.5 1.7 %collective-permute-done = bf16[1280,256]{1,0:T(8,128)(2,1)S(1)} collective-permute-done((bf16[1280,256]{1,0:T(8,128)(2,1)S(1)}, bf16[1280,256]{1,0:T(8,128)(2,1)S(1)}, u32[]{:S(2)}, u32[]{:S(2)}) %collective-permute-start) | collective-permute-done | bytes 655392 | tf_op jit(solution)/shard_map/ppermute | solution.py:23
  50.2 0.2 add_convert_fusion
  50.4 14.7 %all_to_all.20 = bf16[16,80,256]{2,1,0:T(8,128)(2,1)S(1)} all-to-all(bf16[16,80,256]{2,1,0:T(8,128)(2,1)S(1)} %bitcast.28), channel_id=1, replica_groups=mesh['zh'=4,'zl'=4,'xl'=2,'core'=2,'y'=4,'xh'=2] {'xl','y','xh'}, dimensions={0} | all-to-all | bytes 1310720 | tf_op jit(solution)/shard_map/all_to_all | solution.py:27
  65.1 0.1 convert_reduce_fusion
  65.2 3.7 %collective-permute-start.1 = (f32[80,256]{1,0:T(8,128)S(1)}, f32[80,256]{1,0:T(8,128)S(1)}, u32[]{:S(2)}, u32[]{:S(2)}) collective-permute-start(f32[80,256]{1,0:T(8,128)S(1)} %convert_reduce_fusion), channel_id=1, source_target_pairs={{0,32},{32,0},{64,96},{96,64},{1,33},{33,1},{65,97},{97,65},{2,34}... | collective-permute-start | bytes 245768 | tf_op jit(solution)/shard_map/ppermute | solution.py:37
  68.9 0.0 copy-done.1
  68.9 3.6 %all-to-all-start.2 = ((bf16[8,7,8,1152]{3,2,1,0:T(8,128)(2,1)}), bf16[8,7,8,1152]{3,2,1,0:T(8,128)(2,1)S(1)}, u32[]{:S(2)}, u32[]{:S(2)}) async-start(bf16[8,7,8,1152]{3,2,1,0:T(8,128)(2,1)} %bitcast.25), calls=%async_computation.2 | async-start | bytes 2064384 | tf_op jit(solution)/shard_map/all_to_all | solution.py:27
  72.5 0.0 copy-start.5
  72.5 0.0 collective-permute-done.1
  72.5 4.9 %collective-permute-start.2 = (f32[80,256]{1,0:T(8,128)S(1)}, f32[80,256]{1,0:T(8,128)S(1)}, u32[]{:S(2)}, u32[]{:S(2)}) collective-permute-start(f32[80,256]{1,0:T(8,128)S(1)} %add.20), channel_id=1, source_target_pairs={{0,64},{32,96},{64,0},{96,32},{1,65},{33,97},{65,1},{97,33},{2,66}... | collective-permute-start | bytes 245768 | tf_op jit(solution)/shard_map/ppermute | solution.py:37
  77.4 2.7 %collective-permute-done.2 = f32[80,256]{1,0:T(8,128)S(1)} collective-permute-done((f32[80,256]{1,0:T(8,128)S(1)}, f32[80,256]{1,0:T(8,128)S(1)}, u32[]{:S(2)}, u32[]{:S(2)}) %collective-permute-start.2) | collective-permute-done | bytes 81952 | tf_op jit(solution)/shard_map/ppermute | solution.py:37
  80.1 8.8 %collective-permute-start.3 = (bf16[80,256]{1,0:T(8,128)(2,1)S(1)}, bf16[80,256]{1,0:T(8,128)(2,1)S(1)}, u32[]{:S(2)}, u32[]{:S(2)}) collective-permute-start(bf16[80,256]{1,0:T(8,128)(2,1)S(1)} %add_convert_fusion.2), channel_id=1, source_target_pairs={{0,128},{128,0},{256,384},{384,256},{1,129},{129,1},{257,385},{385... | collective-permute-start | bytes 122888 | tf_op jit(solution)/shard_map/ppermute | solution.py:37
  89.0 1.4 %collective-permute-done.3 = bf16[80,256]{1,0:T(8,128)(2,1)S(1)} collective-permute-done((bf16[80,256]{1,0:T(8,128)(2,1)S(1)}, bf16[80,256]{1,0:T(8,128)(2,1)S(1)}, u32[]{:S(2)}, u32[]{:S(2)}) %collective-permute-start.3) | collective-permute-done | bytes 40992 | tf_op jit(solution)/shard_map/ppermute | solution.py:37
  90.3 13.2 %collective-permute-start.4 = (bf16[80,256]{1,0:T(8,128)(2,1)S(1)}, bf16[80,256]{1,0:T(8,128)(2,1)S(1)}, u32[]{:S(2)}, u32[]{:S(2)}) collective-permute-start(bf16[80,256]{1,0:T(8,128)(2,1)S(1)} %add_convert_fusion.1), channel_id=1, source_target_pairs={{0,256},{128,384},{256,0},{384,128},{1,257},{129,385},{257,1},{385... | collective-permute-start | bytes 122888 | tf_op jit(solution)/shard_map/ppermute | solution.py:37
  103.6 1.4 %collective-permute-done.4 = bf16[80,256]{1,0:T(8,128)(2,1)S(1)} collective-permute-done((bf16[80,256]{1,0:T(8,128)(2,1)S(1)}, bf16[80,256]{1,0:T(8,128)(2,1)S(1)}, u32[]{:S(2)}, u32[]{:S(2)}) %collective-permute-start.4) | collective-permute-done | bytes 40992 | tf_op jit(solution)/shard_map/ppermute | solution.py:37
  105.0 0.0 all-to-all-done.2
  105.0 0.9 broadcast_in_dim.10
  105.9 6.5 %all-to-all-start.3 = ((bf16[16,80,256]{2,1,0:T(8,128)(2,1)}), bf16[16,80,256]{2,1,0:T(8,128)(2,1)S(1)}, u32[]{:S(2)}, u32[]{:S(2)}) async-start(bf16[16,80,256]{2,1,0:T(8,128)(2,1)} %broadcast_in_dim.10), calls=%async_computation.3 | async-start | bytes 1310720 | tf_op jit(solution)/shard_map/all_to_all | solution.py:27
  112.4 0.0 copy-done.5
  112.4 2.1 %unpack.1 = bf16[9,48,1152]{2,1,0:T(8,128)(2,1)} custom-call(s32[1]{0:T(128)} %bitcast.who_ref, s32[432]{0:T(512)S(1)} %copy-done.5, bf16[56,8,1152]{2,1,0:T(8,128)(2,1)S(1)} %bitcast.24), custom_call_target="tpu_custom_call" | custom-call | tf_op jit(solution)/shard_map/unpack/pallas_call | solution.py:100
  114.5 7.0 %all-to-all-done.3 = bf16[16,80,256]{2,1,0:T(8,128)(2,1)S(1)} async-done(((bf16[16,80,256]{2,1,0:T(8,128)(2,1)}), bf16[16,80,256]{2,1,0:T(8,128)(2,1)S(1)}, u32[]{:S(2)}, u32[]{:S(2)}) %all-to-all-start.3) | async-done | bytes 655392 | tf_op jit(solution)/shard_map/all_to_all | solution.py:27
  121.4 9.0 %collective-permute-start.5 = (bf16[16,80,256]{2,1,0:T(8,128)(2,1)S(1)}, bf16[16,80,256]{2,1,0:T(8,128)(2,1)S(1)}, u32[]{:S(2)}, u32[]{:S(2)}) collective-permute-start(bf16[16,80,256]{2,1,0:T(8,128)(2,1)S(1)} %all-to-all-done.3), channel_id=1, source_target_pairs={{0,8},{8,0},{1,9},{9,1},{2,10},{10,2},{3,11},{11,3},{4,12},{12,4},... | collective-permute-start | bytes 1966088 | tf_op jit(solution)/shard_map/ppermute | solution.py:23
  130.5 1.7 %collective-permute-done.5 = bf16[16,80,256]{2,1,0:T(8,128)(2,1)S(1)} collective-permute-done((bf16[16,80,256]{2,1,0:T(8,128)(2,1)S(1)}, bf16[16,80,256]{2,1,0:T(8,128)(2,1)S(1)}, u32[]{:S(2)}, u32[]{:S(2)}) %collective-permute-start.5) | collective-permute-done | bytes 655392 | tf_op jit(solution)/shard_map/ppermute | solution.py:23
  132.2 0.1 select_bitcast_fusion.1
  132.3 1.1 pad_maximum_fusion
  133.4 0.1 reshape.59
  133.5 0.7 copy.21
  134.1 0.6 fusion
  (10 shorter events, 0.1 us)
Async XLA Ops:
  0.6 1.2 copy-start.2
  1.8 1.0 copy-start.3
  2.9 0.7 copy-start.4
  6.0 7.6 %copy-start.8 = (bf16[2,3,3,1152]{3,0,2,1:T(2,128)(2,1)S(1)}, bf16[2,3,3,1152]{3,0,2,1:T(2,128)(2,1)}, u32[]{:S(2)}) copy-start(bf16[2,3,3,1152]{3,0,2,1:T(2,128)(2,1)} %param.8) | copy-start | bytes 124420
  6.0 26.4 %copy-start = (bf16[2,1152,256]{2,1,0:T(8,128)(2,1)S(1)}, bf16[2,1152,256]{2,1,0:T(8,128)(2,1)}, u32[]{:S(2)}) copy-start(bf16[2,1152,256]{2,1,0:T(8,128)(2,1)} %pw_ref.1) | copy-start | bytes 3538948
  6.0 26.4 %copy-start.6 = (f32[2,256]{1,0:T(2,128)S(1)}, f32[2,256]{1,0:T(2,128)}, u32[]{:S(2)}) copy-start(f32[2,256]{1,0:T(2,128)} %pb_ref.1) | copy-start | bytes 6148
  6.0 26.4 %copy-start.7 = (s32[432]{0:T(512)S(1)}, s32[432]{0:T(512)}, u32[]{:S(2)}) copy-start(s32[432]{0:T(512)} %constant.25.clone.away_ref) | copy-start | bytes 5188
  6.0 26.4 %all-to-all-start = ((bf16[8,7,8,1664]{3,2,1,0:T(8,128)(2,1)}), bf16[8,7,8,1664]{3,2,1,0:T(8,128)(2,1)S(1)}, u32[]{:S(2)}, u32[]{:S(2)}) async-start(bf16[8,7,8,1664]{3,2,1,0:T(8,128)(2,1)} %bitcast.4), calls=%async_computation | async-start | bytes 2981888 | tf_op jit(solution)/shard_map/all_to_all | solution.py:27
  42.4 26.4 %copy-start.1 = (bf16[56,8,1152]{2,1,0:T(8,128)(2,1)}, bf16[56,8,1152]{2,1,0:T(8,128)(2,1)S(1)}, u32[]{:S(2)}) copy-start(bf16[56,8,1152]{2,1,0:T(8,128)(2,1)S(1)} %get-tuple-element.16) | copy-start | bytes 3096580
  42.4 7.8 %collective-permute-start = (bf16[1280,256]{1,0:T(8,128)(2,1)S(1)}, bf16[1280,256]{1,0:T(8,128)(2,1)S(1)}, u32[]{:S(2)}, u32[]{:S(2)}) collective-permute-start(bf16[1280,256]{1,0:T(8,128)(2,1)S(1)} %get-tuple-element.15), channel_id=1, source_target_pairs={{0,8},{8,0},{1,9},{9,1},{2,10},{10,2},{3,11},{11,3},{4,12},{12,4},... | collective-permute-start | bytes 1966088 | tf_op jit(solution)/shard_map/ppermute | solution.py:23
  65.2 7.3 %collective-permute-start.1 = (f32[80,256]{1,0:T(8,128)S(1)}, f32[80,256]{1,0:T(8,128)S(1)}, u32[]{:S(2)}, u32[]{:S(2)}) collective-permute-start(f32[80,256]{1,0:T(8,128)S(1)} %convert_reduce_fusion), channel_id=1, source_target_pairs={{0,32},{32,0},{64,96},{96,64},{1,33},{33,1},{65,97},{97,65},{2,34}... | collective-permute-start | bytes 245768 | tf_op jit(solution)/shard_map/ppermute | solution.py:37
  68.9 36.1 %all-to-all-start.2 = ((bf16[8,7,8,1152]{3,2,1,0:T(8,128)(2,1)}), bf16[8,7,8,1152]{3,2,1,0:T(8,128)(2,1)S(1)}, u32[]{:S(2)}, u32[]{:S(2)}) async-start(bf16[8,7,8,1152]{3,2,1,0:T(8,128)(2,1)} %bitcast.25), calls=%async_computation.2 | async-start | bytes 2064384 | tf_op jit(solution)/shard_map/all_to_all | solution.py:27
  72.5 39.9 %copy-start.5 = (s32[432]{0:T(512)S(1)}, s32[432]{0:T(512)}, u32[]{:S(2)}) copy-start(s32[432]{0:T(512)} %constant.24.clone.home_ref) | copy-start | bytes 5188
  72.5 7.6 %collective-permute-start.2 = (f32[80,256]{1,0:T(8,128)S(1)}, f32[80,256]{1,0:T(8,128)S(1)}, u32[]{:S(2)}, u32[]{:S(2)}) collective-permute-start(f32[80,256]{1,0:T(8,128)S(1)} %add.20), channel_id=1, source_target_pairs={{0,64},{32,96},{64,0},{96,32},{1,65},{33,97},{65,1},{97,33},{2,66}... | collective-permute-start | bytes 245768 | tf_op jit(solution)/shard_map/ppermute | solution.py:37
  80.1 10.2 %collective-permute-start.3 = (bf16[80,256]{1,0:T(8,128)(2,1)S(1)}, bf16[80,256]{1,0:T(8,128)(2,1)S(1)}, u32[]{:S(2)}, u32[]{:S(2)}) collective-permute-start(bf16[80,256]{1,0:T(8,128)(2,1)S(1)} %add_convert_fusion.2), channel_id=1, source_target_pairs={{0,128},{128,0},{256,384},{384,256},{1,129},{129,1},{257,385},{385... | collective-permute-start | bytes 122888 | tf_op jit(solution)/shard_map/ppermute | solution.py:37
  90.3 14.6 %collective-permute-start.4 = (bf16[80,256]{1,0:T(8,128)(2,1)S(1)}, bf16[80,256]{1,0:T(8,128)(2,1)S(1)}, u32[]{:S(2)}, u32[]{:S(2)}) collective-permute-start(bf16[80,256]{1,0:T(8,128)(2,1)S(1)} %add_convert_fusion.1), channel_id=1, source_target_pairs={{0,256},{128,384},{256,0},{384,128},{1,257},{129,385},{257,1},{385... | collective-permute-start | bytes 122888 | tf_op jit(solution)/shard_map/ppermute | solution.py:37
  105.9 15.6 %all-to-all-start.3 = ((bf16[16,80,256]{2,1,0:T(8,128)(2,1)}), bf16[16,80,256]{2,1,0:T(8,128)(2,1)S(1)}, u32[]{:S(2)}, u32[]{:S(2)}) async-start(bf16[16,80,256]{2,1,0:T(8,128)(2,1)} %broadcast_in_dim.10), calls=%async_computation.3 | async-start | bytes 1310720 | tf_op jit(solution)/shard_map/all_to_all | solution.py:27
  121.4 10.7 %collective-permute-start.5 = (bf16[16,80,256]{2,1,0:T(8,128)(2,1)S(1)}, bf16[16,80,256]{2,1,0:T(8,128)(2,1)S(1)}, u32[]{:S(2)}, u32[]{:S(2)}) collective-permute-start(bf16[16,80,256]{2,1,0:T(8,128)(2,1)S(1)} %all-to-all-done.3), channel_id=1, source_target_pairs={{0,8},{8,0},{1,9},{9,1},{2,10},{10,2},{3,11},{11,3},{4,12},{12,4},... | collective-permute-start | bytes 1966088 | tf_op jit(solution)/shard_map/ppermute | solution.py:23

commit v7 on v6

--- a/solution.py
+++ b/solution.py
@@ -16,6 +16,7 @@
 
 DP = ("zh", "zl", "xl", "core")
 LON = ("y", "xh")
+Z = ("zh", "zl")
 PLANE = ("xl", "y", "xh")
 
 
@@ -32,9 +33,17 @@
     return exchange(jnp.broadcast_to(block[None], (peers,) + block.shape), axes)
 
 
-def sum_pair(own, axis, apart):
-    pairs = [(i, i ^ apart) for i in range(lax.axis_size(axis))]
-    return own.astype(jnp.float32) + lax.ppermute(own, axis, pairs).astype(jnp.float32)
+def sum_ring(own, apart):
+    planes = lax.axis_size(Z)
+
+    def fetch(block, ahead):
+        return lax.ppermute(block, Z, [((i + ahead) % planes, i) for i in range(planes)])
+
+    after = fetch(own, apart)
+    before = fetch(own, -apart)
+    far = fetch(after, apart)
+    own, after, before, far = [x.astype(jnp.float32) for x in (own, after, before, far)]
+    return (own + far) + (before + after)
 
 
 def deal_units(columns):
@@ -63,12 +72,27 @@
         ref[block * SLOTS + SLOTS - 1] = jnp.zeros(ref.shape[1:], ref.dtype)
 
 
-def pack_body(who_ref, home_ref, feat_ref, cot_ref, out_ref):
+def pack_body(who_ref, home_hbm, feat_hbm, cot_hbm, out_ref, home_ref, feat_ref, cot_ref, table_sem, sems):
     columns, _, channels = feat_ref.shape
     lon = who_ref[0]
+    table = pltpu.make_async_copy(home_hbm, home_ref, table_sem)
+    table.start()
+
+    def fetch(j):
+        return [
+            pltpu.make_async_copy(source.at[j], held.at[j], sems.at[n, j])
+            for n, (source, held) in enumerate(((feat_hbm, feat_ref), (cot_hbm, cot_ref)))
+        ]
+
+    for j in range(columns):
+        for copy in fetch(j):
+            copy.start()
     blank_slots(out_ref, lon)
+    table.wait()
 
     def column(j, carry):
+        for copy in fetch(j):
+            copy.wait()
         for source, start in ((feat_ref, 0), (cot_ref, channels)):
             width = source.shape[2]
             rows = source[j].astype(jnp.float32)
@@ -94,13 +118,13 @@
     lax.fori_loop(0, columns, column, 0)
 
 
-def on_chip(body, out_shape, scalars, arrays, scratch=(), name=None):
+def on_chip(body, out_shape, scalars, arrays, scratch=(), name=None, space=pltpu.VMEM):
     vmem = pl.BlockSpec(memory_space=pltpu.VMEM)
     smem = pl.BlockSpec(memory_space=pltpu.SMEM)
     return pl.pallas_call(
         body,
         out_shape=out_shape,
-        in_specs=[smem] * len(scalars) + [vmem] * len(arrays),
+        in_specs=[smem] * len(scalars) + [pl.BlockSpec(memory_space=space)] * len(arrays),
         out_specs=jax.tree.map(lambda _: vmem, out_shape),
         scratch_shapes=list(scratch),
         compiler_params=pltpu.CompilerParams(vmem_limit_bytes=48 << 20),
@@ -214,7 +238,7 @@
             write_pairs(depth, 1, u, lanes, made_b)
             return carry
 
-        lax.fori_loop(0, units, forward, 0)
+        lax.fori_loop(0, units, forward, 0, unroll=True)
 
     for branch in range(2):
         act = jnp.dot(depth[branch], pw_ref[branch], preferred_element_type=jnp.float32)
@@ -274,7 +298,7 @@
             return tuple(sums)
 
         zero = jnp.zeros((HELD, LANES), jnp.float32)
-        sums = lax.fori_loop(0, units, backward, (zero,) * 10)
+        sums = lax.fori_loop(0, units, backward, (zero,) * 10, unroll=True)
 
         def keep(branch, a, e, value, mask=None):
             value = value if mask is None else jnp.where(mask, value, 0.0)
@@ -318,9 +342,17 @@
     packed = on_chip(
         pack_body,
         jax.ShapeDtypeStruct((PEERS * SLOTS, HELD, width), act),
-        (who, home),
-        (features[0], cotangent[0]),
+        (who,),
+        [pltpu.with_memory_space_constraint(x, pltpu.HBM) for x in (home, features[0], cotangent[0])],
+        (
+            pltpu.SMEM(home.shape, jnp.int32),
+            pltpu.VMEM((columns, rows, channels), act),
+            pltpu.VMEM((columns, rows, cotangent.shape[3]), act),
+            pltpu.SemaphoreType.DMA(()),
+            pltpu.SemaphoreType.DMA((2, columns)),
+        ),
         name="pack",
+        space=pltpu.HBM,
     )
     field = exchange(packed.reshape(PEERS, SLOTS, HELD, width), LON).reshape(packed.shape)
     taps = depth_w.astype(jnp.float32).reshape(branches * 9, channels)
@@ -348,9 +380,8 @@
     fgrad, terms = lax.optimization_barrier((fgrad, terms))
     fgrad = exchange(fgrad.reshape(PEERS, SLOTS, HELD, channels), LON)
     terms = jnp.sum(terms.astype(jnp.float32), axis=0)
-    terms = sum_pair(sum_pair(terms, "zl", 1), "zl", 2)
-    terms = sum_pair(terms.astype(jnp.bfloat16), "zh", 1)
-    terms = sum_pair(terms.astype(jnp.bfloat16), "zh", 2)
+    terms = sum_ring(terms.astype(jnp.bfloat16), 4)
+    terms = sum_ring(terms, 1)
     total = (terms / images).astype(jnp.bfloat16)
     fgrad, total = lax.optimization_barrier((fgrad, total))
     total = gather_copies(total, PLANE)

time: 135 us -> 132 us (0.978)
  starting transfers between devices: 63.4 us -> 67.1 us
  local copies, waits for them, and re-layouts: 4.59 us -> 1.7 us
  waiting for transfers between devices: 34.5 us -> 31.9 us
    ppermute x4 -> x6, starting transfers between devices: 30.6 us -> 34.2 us  [fetch(): lax.ppermute(block, Z, [((i + ahead) % planes, i) for i in range(planes)])]
    unnamed x18 -> x10, local copies, waits for them, and re-layouts: 2.92 us -> 0.03 us
    ppermute x4 -> x6, waiting for transfers between devices: 5.47 us -> 2.83 us  [fetch(): lax.ppermute(block, Z, [((i + ahead) % planes, i) for i in range(planes)])]
  transfers between devices with their start and end apart: 9 -> 11, of which waited for: 7 -> 6; matrix products, arithmetic and copies ran while one was open for 0% -> 0% of each run, Pallas kernels for 2% -> 2%
where the time goes in v7:
time: 132 us
  starting transfers between devices  67.1 us (51%)
  waiting for transfers between devices  31.9 us (24%)
  blocking collectives  14.7 us (11%)
  Pallas kernels  13.3 us (10%)
  other arithmetic  2.08 us (2%)
  local copies, waits for them, and re-layouts  1.7 us (1%)
    ppermute x6, starting transfers between devices, fetch(): lax.ppermute(block, Z, [((i + ahead) % planes, i) for i in range(planes)])  34.2 us
    all_to_all x3, waiting for transfers between devices, exchange(): return lax.all_to_all(blocks, axes, 0, 0, tiled=True)  25.6 us
    all_to_all x3, starting transfers between devices, exchange(): return lax.all_to_all(blocks, axes, 0, 0, tiled=True)  17.9 us
    ppermute x2, starting transfers between devices, swap_cores(): return lax.ppermute(block, 'core', [(0, 1), (1, 0)])  15 us
    all_to_all x1, blocking collectives, exchange(): return lax.all_to_all(blocks, axes, 0, 0, tiled=True)  14.7 us
    pallas_call x3, Pallas kernels, on_chip(): pl.pallas_call(body, out_shape=out_shape, in_specs=[smem] * len(scalars)...  13.3 us
    ppermute x2, waiting for transfers between devices, swap_cores(): return lax.ppermute(block, 'core', [(0, 1), (1, 0)])  3.4 us
    ppermute x6, waiting for transfers between devices, fetch(): lax.ppermute(block, Z, [((i + ahead) % planes, i) for i in range(planes)])  2.83 us
  transfers between devices with their start and end apart: 11, of which 6 were waited for; matrix products, arithmetic and copies ran while one was open for 0% of the time, Pallas kernels for 2%

profile of v7, /device:TPU:1, one launch (start us, length us, event | category | flops | bytes accessed | tf_op | source)
XLA Modules:
  0.0 131.6 jit_solution(13333139592810228387)
XLA Ops:
  0.6 2.9 %pack.1 = bf16[56,8,1664]{2,1,0:T(8,128)(2,1)} custom-call(s32[1]{0:T(128)} %bitcast.who_ref, s32[432]{0:T(512)} %constant.25.clone.home_hbm.home_ref, bf16[9,48,1152]{2,1,0:T(8,128)(2,1)} %bitcast.27, bf16[9,48,512]{2,1,0:T(8,128)(2,1)} %bitcast.29), custom_call_target="tpu_custom_call" | custom-call | tf_op jit(solution)/shard_map/pack/pallas_call | solution.py:124
  3.6 0.0 copy-start.4
  3.6 0.0 copy-start
  3.6 0.0 copy-start.2
  3.6 0.0 copy-start.3
  3.6 7.6 %all-to-all-start = ((bf16[8,7,8,1664]{3,2,1,0:T(8,128)(2,1)}), bf16[8,7,8,1664]{3,2,1,0:T(8,128)(2,1)S(1)}, u32[]{:S(2)}, u32[]{:S(2)}) async-start(bf16[8,7,8,1664]{3,2,1,0:T(8,128)(2,1)} %bitcast.4), calls=%async_computation | async-start | bytes 2981888 | tf_op jit(solution)/shard_map/all_to_all | solution.py:28
  11.2 0.0 copy-done.4
  11.3 18.7 %all-to-all-done = bf16[8,7,8,1664]{3,2,1,0:T(8,128)(2,1)S(1)} async-done(((bf16[8,7,8,1664]{3,2,1,0:T(8,128)(2,1)}), bf16[8,7,8,1664]{3,2,1,0:T(8,128)(2,1)S(1)}, u32[]{:S(2)}, u32[]{:S(2)}) %all-to-all-start) | async-done | bytes 1490976 | tf_op jit(solution)/shard_map/all_to_all | solution.py:28
  30.0 0.0 copy-done
  30.0 0.0 copy-done.2
  30.0 0.0 copy-done.3
  30.0 8.3 %local_work.1 = (f32[1280,256]{1,0:T(8,128)S(1)}, bf16[1280,256]{1,0:T(8,128)(2,1)S(1)}, bf16[56,8,1152]{2,1,0:T(8,128)(2,1)}) custom-call(s32[1]{0:T(128)} %bitcast.who_ref, s32[1]{0:T(128)} %bitcast.1.core_ref, s32[432]{0:T(512)S(1)} %copy-done.3, bf16[56,8,1664]{2,1,0:T(8,128)(2,1)S(1)} %bitcast.23, f32[18,1152]{1,0:T(8,128)S(1)} %reshape.63.taps_ref, ...), custom_call_target="tpu_custom_call" | custom-call | tf_op jit(solution)/shard_map/local_work/pallas_call | solution.py:124
  38.3 6.0 %collective-permute-start = (bf16[1280,256]{1,0:T(8,128)(2,1)S(1)}, bf16[1280,256]{1,0:T(8,128)(2,1)S(1)}, u32[]{:S(2)}, u32[]{:S(2)}) collective-permute-start(bf16[1280,256]{1,0:T(8,128)(2,1)S(1)} %get-tuple-element.15), channel_id=1, source_target_pairs={{0,8},{8,0},{1,9},{9,1},{2,10},{10,2},{3,11},{11,3},{4,12},{12,4},... | collective-permute-start | bytes 1966088 | tf_op jit(solution)/shard_map/ppermute | solution.py:24
  44.4 1.7 %collective-permute-done = bf16[1280,256]{1,0:T(8,128)(2,1)S(1)} collective-permute-done((bf16[1280,256]{1,0:T(8,128)(2,1)S(1)}, bf16[1280,256]{1,0:T(8,128)(2,1)S(1)}, u32[]{:S(2)}, u32[]{:S(2)}) %collective-permute-start) | collective-permute-done | bytes 655392 | tf_op jit(solution)/shard_map/ppermute | solution.py:24
  46.1 0.2 add_convert_fusion
  46.2 14.7 %all_to_all.20 = bf16[16,80,256]{2,1,0:T(8,128)(2,1)S(1)} all-to-all(bf16[16,80,256]{2,1,0:T(8,128)(2,1)S(1)} %bitcast.25), channel_id=1, replica_groups=mesh['zh'=4,'zl'=4,'xl'=2,'core'=2,'y'=4,'xh'=2] {'xl','y','xh'}, dimensions={0} | all-to-all | bytes 1310720 | tf_op jit(solution)/shard_map/all_to_all | solution.py:28
  60.9 3.6 %all-to-all-start.2 = ((bf16[8,7,8,1152]{3,2,1,0:T(8,128)(2,1)}), bf16[8,7,8,1152]{3,2,1,0:T(8,128)(2,1)S(1)}, u32[]{:S(2)}, u32[]{:S(2)}) async-start(bf16[8,7,8,1152]{3,2,1,0:T(8,128)(2,1)} %bitcast.7), calls=%async_computation.2 | async-start | bytes 2064384 | tf_op jit(solution)/shard_map/all_to_all | solution.py:28
  64.5 0.1 reduce_sum.12
  64.6 0.0 copy-start.1
  64.6 12.6 %collective-permute-start.1 = (bf16[80,256]{1,0:T(8,128)(2,1)S(1)}, bf16[80,256]{1,0:T(8,128)(2,1)S(1)}, u32[]{:S(2)}, u32[]{:S(2)}) collective-permute-start(bf16[80,256]{1,0:T(8,128)(2,1)S(1)} %reduce_sum.12), channel_id=1, source_target_pairs={{128,0},{160,32},{192,64},{224,96},{256,128},{288,160},{320,192},{... | collective-permute-start | bytes 122888 | tf_op jit(solution)/shard_map/ppermute | solution.py:40
  77.2 1.9 %collective-permute-start.3 = (bf16[80,256]{1,0:T(8,128)(2,1)S(1)}, bf16[80,256]{1,0:T(8,128)(2,1)S(1)}, u32[]{:S(2)}, u32[]{:S(2)}) collective-permute-start(bf16[80,256]{1,0:T(8,128)(2,1)S(1)} %reduce_sum.12), channel_id=1, source_target_pairs={{384,0},{416,32},{448,64},{480,96},{0,128},{32,160},{64,192},{96,2... | collective-permute-start | bytes 122888 | tf_op jit(solution)/shard_map/ppermute | solution.py:40
  79.1 0.0 collective-permute-done.1
  79.1 7.3 %collective-permute-start.2 = (bf16[80,256]{1,0:T(8,128)(2,1)S(1)}, bf16[80,256]{1,0:T(8,128)(2,1)S(1)}, u32[]{:S(2)}, u32[]{:S(2)}) collective-permute-start(bf16[80,256]{1,0:T(8,128)(2,1)S(1)} %collective-permute-done.1), channel_id=1, source_target_pairs={{128,0},{160,32},{192,64},{224,96},{256,128},{288,160},{320,192},{... | collective-permute-start | bytes 122888 | tf_op jit(solution)/shard_map/ppermute | solution.py:40
  86.4 0.0 collective-permute-done.3
  86.4 1.4 %collective-permute-done.2 = bf16[80,256]{1,0:T(8,128)(2,1)S(1)} collective-permute-done((bf16[80,256]{1,0:T(8,128)(2,1)S(1)}, bf16[80,256]{1,0:T(8,128)(2,1)S(1)}, u32[]{:S(2)}, u32[]{:S(2)}) %collective-permute-start.2) | collective-permute-done | bytes 40992 | tf_op jit(solution)/shard_map/ppermute | solution.py:40
  87.8 5.9 %collective-permute-start.4 = (f32[80,256]{1,0:T(8,128)S(1)}, f32[80,256]{1,0:T(8,128)S(1)}, u32[]{:S(2)}, u32[]{:S(2)}) collective-permute-start(f32[80,256]{1,0:T(8,128)S(1)} %add_add_fusion), channel_id=1, source_target_pairs={{32,0},{64,32},{96,64},{128,96},{160,128},{192,160},{224,192},{256... | collective-permute-start | bytes 245768 | tf_op jit(solution)/shard_map/ppermute | solution.py:40
  93.8 1.9 %collective-permute-start.6 = (f32[80,256]{1,0:T(8,128)S(1)}, f32[80,256]{1,0:T(8,128)S(1)}, u32[]{:S(2)}, u32[]{:S(2)}) collective-permute-start(f32[80,256]{1,0:T(8,128)S(1)} %add_add_fusion), channel_id=1, source_target_pairs={{480,0},{0,32},{32,64},{64,96},{96,128},{128,160},{160,192},{192,2... | collective-permute-start | bytes 245768 | tf_op jit(solution)/shard_map/ppermute | solution.py:40
  95.7 0.0 collective-permute-done.4
  95.7 4.6 %collective-permute-start.5 = (f32[80,256]{1,0:T(8,128)S(1)}, f32[80,256]{1,0:T(8,128)S(1)}, u32[]{:S(2)}, u32[]{:S(2)}) collective-permute-start(f32[80,256]{1,0:T(8,128)S(1)} %collective-permute-done.4), channel_id=1, source_target_pairs={{32,0},{64,32},{96,64},{128,96},{160,128},{192,160},{224,192},{256... | collective-permute-start | bytes 245768 | tf_op jit(solution)/shard_map/ppermute | solution.py:40
  100.3 0.0 collective-permute-done.6
  100.3 1.5 %collective-permute-done.5 = f32[80,256]{1,0:T(8,128)S(1)} collective-permute-done((f32[80,256]{1,0:T(8,128)S(1)}, f32[80,256]{1,0:T(8,128)S(1)}, u32[]{:S(2)}, u32[]{:S(2)}) %collective-permute-start.5) | collective-permute-done | bytes 81952 | tf_op jit(solution)/shard_map/ppermute | solution.py:40
  101.8 0.0 all-to-all-done.2
  101.8 0.9 broadcast_in_dim.10
  102.7 6.7 %all-to-all-start.3 = ((bf16[16,80,256]{2,1,0:T(8,128)(2,1)}), bf16[16,80,256]{2,1,0:T(8,128)(2,1)S(1)}, u32[]{:S(2)}, u32[]{:S(2)}) async-start(bf16[16,80,256]{2,1,0:T(8,128)(2,1)} %broadcast_in_dim.10), calls=%async_computation.3 | async-start | bytes 1310720 | tf_op jit(solution)/shard_map/all_to_all | solution.py:28
  109.3 0.0 copy-done.1
  109.4 2.1 %unpack.1 = bf16[9,48,1152]{2,1,0:T(8,128)(2,1)} custom-call(s32[1]{0:T(128)} %bitcast.who_ref, s32[432]{0:T(512)S(1)} %copy-done.1, bf16[56,8,1152]{2,1,0:T(8,128)(2,1)S(1)} %bitcast.24), custom_call_target="tpu_custom_call" | custom-call | tf_op jit(solution)/shard_map/unpack/pallas_call | solution.py:124
  111.5 7.0 %all-to-all-done.3 = bf16[16,80,256]{2,1,0:T(8,128)(2,1)S(1)} async-done(((bf16[16,80,256]{2,1,0:T(8,128)(2,1)}), bf16[16,80,256]{2,1,0:T(8,128)(2,1)S(1)}, u32[]{:S(2)}, u32[]{:S(2)}) %all-to-all-start.3) | async-done | bytes 655392 | tf_op jit(solution)/shard_map/all_to_all | solution.py:28
  118.4 9.0 %collective-permute-start.7 = (bf16[16,80,256]{2,1,0:T(8,128)(2,1)S(1)}, bf16[16,80,256]{2,1,0:T(8,128)(2,1)S(1)}, u32[]{:S(2)}, u32[]{:S(2)}) collective-permute-start(bf16[16,80,256]{2,1,0:T(8,128)(2,1)S(1)} %all-to-all-done.3), channel_id=1, source_target_pairs={{0,8},{8,0},{1,9},{9,1},{2,10},{10,2},{3,11},{11,3},{4,12},{12,4},... | collective-permute-start | bytes 1966088 | tf_op jit(solution)/shard_map/ppermute | solution.py:24
  127.4 1.7 %collective-permute-done.7 = bf16[16,80,256]{2,1,0:T(8,128)(2,1)S(1)} collective-permute-done((bf16[16,80,256]{2,1,0:T(8,128)(2,1)S(1)}, bf16[16,80,256]{2,1,0:T(8,128)(2,1)S(1)}, u32[]{:S(2)}, u32[]{:S(2)}) %collective-permute-start.7) | collective-permute-done | bytes 655392 | tf_op jit(solution)/shard_map/ppermute | solution.py:24
  129.1 0.1 select_bitcast_fusion.1
  129.2 1.1 pad_maximum_fusion
  130.3 0.1 reshape.59
  130.4 0.7 copy.21
  131.1 0.6 fusion
  (8 shorter events, 0.1 us)
Async XLA Ops:
  3.6 7.7 %copy-start.4 = (bf16[2,3,3,1152]{3,0,2,1:T(2,128)(2,1)S(1)}, bf16[2,3,3,1152]{3,0,2,1:T(2,128)(2,1)}, u32[]{:S(2)}) copy-start(bf16[2,3,3,1152]{3,0,2,1:T(2,128)(2,1)} %param.8) | copy-start | bytes 124420
  3.6 26.4 %copy-start = (bf16[2,1152,256]{2,1,0:T(8,128)(2,1)S(1)}, bf16[2,1152,256]{2,1,0:T(8,128)(2,1)}, u32[]{:S(2)}) copy-start(bf16[2,1152,256]{2,1,0:T(8,128)(2,1)} %pw_ref.1) | copy-start | bytes 3538948
  3.6 26.4 %copy-start.2 = (f32[2,256]{1,0:T(2,128)S(1)}, f32[2,256]{1,0:T(2,128)}, u32[]{:S(2)}) copy-start(f32[2,256]{1,0:T(2,128)} %pb_ref.1) | copy-start | bytes 6148
  3.6 26.4 %copy-start.3 = (s32[432]{0:T(512)S(1)}, s32[432]{0:T(512)}, u32[]{:S(2)}) copy-start(s32[432]{0:T(512)} %constant.26.clone.away_ref) | copy-start | bytes 5188
  3.6 26.4 %all-to-all-start = ((bf16[8,7,8,1664]{3,2,1,0:T(8,128)(2,1)}), bf16[8,7,8,1664]{3,2,1,0:T(8,128)(2,1)S(1)}, u32[]{:S(2)}, u32[]{:S(2)}) async-start(bf16[8,7,8,1664]{3,2,1,0:T(8,128)(2,1)} %bitcast.4), calls=%async_computation | async-start | bytes 2981888 | tf_op jit(solution)/shard_map/all_to_all | solution.py:28
  38.3 7.7 %collective-permute-start = (bf16[1280,256]{1,0:T(8,128)(2,1)S(1)}, bf16[1280,256]{1,0:T(8,128)(2,1)S(1)}, u32[]{:S(2)}, u32[]{:S(2)}) collective-permute-start(bf16[1280,256]{1,0:T(8,128)(2,1)S(1)} %get-tuple-element.15), channel_id=1, source_target_pairs={{0,8},{8,0},{1,9},{9,1},{2,10},{10,2},{3,11},{11,3},{4,12},{12,4},... | collective-permute-start | bytes 1966088 | tf_op jit(solution)/shard_map/ppermute | solution.py:24
  60.9 40.8 %all-to-all-start.2 = ((bf16[8,7,8,1152]{3,2,1,0:T(8,128)(2,1)}), bf16[8,7,8,1152]{3,2,1,0:T(8,128)(2,1)S(1)}, u32[]{:S(2)}, u32[]{:S(2)}) async-start(bf16[8,7,8,1152]{3,2,1,0:T(8,128)(2,1)} %bitcast.7), calls=%async_computation.2 | async-start | bytes 2064384 | tf_op jit(solution)/shard_map/all_to_all | solution.py:28
  64.6 44.7 %copy-start.1 = (s32[432]{0:T(512)S(1)}, s32[432]{0:T(512)}, u32[]{:S(2)}) copy-start(s32[432]{0:T(512)} %constant.25.clone.home_hbm.home_ref) | copy-start | bytes 5188
  64.6 14.5 %collective-permute-start.1 = (bf16[80,256]{1,0:T(8,128)(2,1)S(1)}, bf16[80,256]{1,0:T(8,128)(2,1)S(1)}, u32[]{:S(2)}, u32[]{:S(2)}) collective-permute-start(bf16[80,256]{1,0:T(8,128)(2,1)S(1)} %reduce_sum.12), channel_id=1, source_target_pairs={{128,0},{160,32},{192,64},{224,96},{256,128},{288,160},{320,192},{... | collective-permute-start | bytes 122888 | tf_op jit(solution)/shard_map/ppermute | solution.py:40
  77.2 9.2 %collective-permute-start.3 = (bf16[80,256]{1,0:T(8,128)(2,1)S(1)}, bf16[80,256]{1,0:T(8,128)(2,1)S(1)}, u32[]{:S(2)}, u32[]{:S(2)}) collective-permute-start(bf16[80,256]{1,0:T(8,128)(2,1)S(1)} %reduce_sum.12), channel_id=1, source_target_pairs={{384,0},{416,32},{448,64},{480,96},{0,128},{32,160},{64,192},{96,2... | collective-permute-start | bytes 122888 | tf_op jit(solution)/shard_map/ppermute | solution.py:40
  79.1 8.7 %collective-permute-start.2 = (bf16[80,256]{1,0:T(8,128)(2,1)S(1)}, bf16[80,256]{1,0:T(8,128)(2,1)S(1)}, u32[]{:S(2)}, u32[]{:S(2)}) collective-permute-start(bf16[80,256]{1,0:T(8,128)(2,1)S(1)} %collective-permute-done.1), channel_id=1, source_target_pairs={{128,0},{160,32},{192,64},{224,96},{256,128},{288,160},{320,192},{... | collective-permute-start | bytes 122888 | tf_op jit(solution)/shard_map/ppermute | solution.py:40
  87.8 7.9 %collective-permute-start.4 = (f32[80,256]{1,0:T(8,128)S(1)}, f32[80,256]{1,0:T(8,128)S(1)}, u32[]{:S(2)}, u32[]{:S(2)}) collective-permute-start(f32[80,256]{1,0:T(8,128)S(1)} %add_add_fusion), channel_id=1, source_target_pairs={{32,0},{64,32},{96,64},{128,96},{160,128},{192,160},{224,192},{256... | collective-permute-start | bytes 245768 | tf_op jit(solution)/shard_map/ppermute | solution.py:40
  93.8 6.5 %collective-permute-start.6 = (f32[80,256]{1,0:T(8,128)S(1)}, f32[80,256]{1,0:T(8,128)S(1)}, u32[]{:S(2)}, u32[]{:S(2)}) collective-permute-start(f32[80,256]{1,0:T(8,128)S(1)} %add_add_fusion), channel_id=1, source_target_pairs={{480,0},{0,32},{32,64},{64,96},{96,128},{128,160},{160,192},{192,2... | collective-permute-start | bytes 245768 | tf_op jit(solution)/shard_map/ppermute | solution.py:40
  95.7 6.0 %collective-permute-start.5 = (f32[80,256]{1,0:T(8,128)S(1)}, f32[80,256]{1,0:T(8,128)S(1)}, u32[]{:S(2)}, u32[]{:S(2)}) collective-permute-start(f32[80,256]{1,0:T(8,128)S(1)} %collective-permute-done.4), channel_id=1, source_target_pairs={{32,0},{64,32},{96,64},{128,96},{160,128},{192,160},{224,192},{256... | collective-permute-start | bytes 245768 | tf_op jit(solution)/shard_map/ppermute | solution.py:40
  102.7 15.7 %all-to-all-start.3 = ((bf16[16,80,256]{2,1,0:T(8,128)(2,1)}), bf16[16,80,256]{2,1,0:T(8,128)(2,1)S(1)}, u32[]{:S(2)}, u32[]{:S(2)}) async-start(bf16[16,80,256]{2,1,0:T(8,128)(2,1)} %broadcast_in_dim.10), calls=%async_computation.3 | async-start | bytes 1310720 | tf_op jit(solution)/shard_map/all_to_all | solution.py:28
  118.4 10.7 %collective-permute-start.7 = (bf16[16,80,256]{2,1,0:T(8,128)(2,1)S(1)}, bf16[16,80,256]{2,1,0:T(8,128)(2,1)S(1)}, u32[]{:S(2)}, u32[]{:S(2)}) collective-permute-start(bf16[16,80,256]{2,1,0:T(8,128)(2,1)S(1)} %all-to-all-done.3), channel_id=1, source_target_pairs={{0,8},{8,0},{1,9},{9,1},{2,10},{10,2},{3,11},{11,3},{4,12},{12,4},... | collective-permute-start | bytes 1966088 | tf_op jit(solution)/shard_map/ppermute | solution.py:24

commit v8 on v7

--- a/solution.py
+++ b/solution.py
@@ -44,6 +44,11 @@
     far = fetch(after, apart)
     own, after, before, far = [x.astype(jnp.float32) for x in (own, after, before, far)]
     return (own + far) + (before + after)
+
+
+def sum_pair(own, apart):
+    planes = lax.axis_size("zl")
+    return own + lax.ppermute(own, "zl", [(i, i ^ apart) for i in range(planes)])
 
 
 def deal_units(columns):
@@ -380,10 +385,10 @@
     fgrad, terms = lax.optimization_barrier((fgrad, terms))
     fgrad = exchange(fgrad.reshape(PEERS, SLOTS, HELD, channels), LON)
     terms = jnp.sum(terms.astype(jnp.float32), axis=0)
-    terms = sum_ring(terms.astype(jnp.bfloat16), 4)
-    terms = sum_ring(terms, 1)
+    terms = sum_pair(sum_pair(terms, 1), 2)
+    terms = sum_ring(terms.astype(jnp.bfloat16), lax.axis_size("zl"))
+    fgrad, terms = lax.optimization_barrier((fgrad, terms))
     total = (terms / images).astype(jnp.bfloat16)
-    fgrad, total = lax.optimization_barrier((fgrad, total))
     total = gather_copies(total, PLANE)
     feature_grad = on_chip(
         unpack_body,

time: 132 us -> 130 us (0.985)
  starting transfers between devices: 67.1 us -> 62.8 us
  waiting for transfers between devices: 31.9 us -> 35.1 us
    ppermute x6 -> x3, starting transfers between devices: 34.2 us -> 21.8 us  [fetch(): lax.ppermute(block, Z, [((i + ahead) % planes, i) for i in range(planes)])]
    ppermute x0 -> x2, starting transfers between devices: none -> 8.56 us  [sum_pair(): lax.ppermute(own, 'zl', [(i, i ^ apart) for i in range(planes)])]
    ppermute x0 -> x2, waiting for transfers between devices: none -> 4.22 us  [sum_pair(): lax.ppermute(own, 'zl', [(i, i ^ apart) for i in range(planes)])]
    ppermute x6 -> x3, waiting for transfers between devices: 2.83 us -> 1.88 us  [fetch(): lax.ppermute(block, Z, [((i + ahead) % planes, i) for i in range(planes)])]
  transfers between devices with their start and end apart: 11 -> 10, of which waited for: 6 -> 7; matrix products, arithmetic and copies ran while one was open for 0% -> 0% of each run, Pallas kernels for 2% -> 2%
where the time goes in v8:
time: 130 us
  starting transfers between devices  62.8 us (48%)
  waiting for transfers between devices  35.1 us (27%)
  blocking collectives  14.7 us (11%)
  Pallas kernels  12.3 us (9%)
  other arithmetic  2.08 us (2%)
  local copies, waits for them, and re-layouts  1.71 us (1%)
    all_to_all x3, waiting for transfers between devices, exchange(): return lax.all_to_all(blocks, axes, 0, 0, tiled=True)  25.6 us
    ppermute x3, starting transfers between devices, fetch(): lax.ppermute(block, Z, [((i + ahead) % planes, i) for i in range(planes)])  21.8 us
    all_to_all x3, starting transfers between devices, exchange(): return lax.all_to_all(blocks, axes, 0, 0, tiled=True)  18 us
    all_to_all x1, blocking collectives, exchange(): return lax.all_to_all(blocks, axes, 0, 0, tiled=True)  14.7 us
    ppermute x2, starting transfers between devices, swap_cores(): return lax.ppermute(block, 'core', [(0, 1), (1, 0)])  14.6 us
    pallas_call x3, Pallas kernels, on_chip(): pl.pallas_call(body, out_shape=out_shape, in_specs=[smem] * len(scalars)...  12.3 us
    ppermute x2, starting transfers between devices, sum_pair(): lax.ppermute(own, 'zl', [(i, i ^ apart) for i in range(planes)])  8.56 us
    ppermute x2, waiting for transfers between devices, sum_pair(): lax.ppermute(own, 'zl', [(i, i ^ apart) for i in range(planes)])  4.22 us
  transfers between devices with their start and end apart: 10, of which 7 were waited for; matrix products, arithmetic and copies ran while one was open for 0% of the time, Pallas kernels for 2%

profile of v8, /device:TPU:1, one launch (start us, length us, event | category | flops | bytes accessed | tf_op | source)
XLA Modules:
  0.0 129.7 jit_solution(17901577203846611296)
XLA Ops:
  0.6 2.9 %pack.1 = bf16[56,8,1664]{2,1,0:T(8,128)(2,1)} custom-call(s32[1]{0:T(128)} %bitcast.who_ref, s32[432]{0:T(512)} %constant.24.clone.home_hbm.home_ref, bf16[9,48,1152]{2,1,0:T(8,128)(2,1)} %bitcast.28, bf16[9,48,512]{2,1,0:T(8,128)(2,1)} %bitcast.30), custom_call_target="tpu_custom_call" | custom-call | tf_op jit(solution)/shard_map/pack/pallas_call | solution.py:129
  3.6 0.0 copy-start.5
  3.6 0.0 copy-start
  3.6 0.0 copy-start.3
  3.6 0.0 copy-start.4
  3.6 7.6 %all-to-all-start = ((bf16[8,7,8,1664]{3,2,1,0:T(8,128)(2,1)}), bf16[8,7,8,1664]{3,2,1,0:T(8,128)(2,1)S(1)}, u32[]{:S(2)}, u32[]{:S(2)}) async-start(bf16[8,7,8,1664]{3,2,1,0:T(8,128)(2,1)} %bitcast.4), calls=%async_computation | async-start | bytes 2981888 | tf_op jit(solution)/shard_map/all_to_all | solution.py:28
  11.2 0.0 copy-done.5
  11.3 18.7 %all-to-all-done = bf16[8,7,8,1664]{3,2,1,0:T(8,128)(2,1)S(1)} async-done(((bf16[8,7,8,1664]{3,2,1,0:T(8,128)(2,1)}), bf16[8,7,8,1664]{3,2,1,0:T(8,128)(2,1)S(1)}, u32[]{:S(2)}, u32[]{:S(2)}) %all-to-all-start) | async-done | bytes 1490976 | tf_op jit(solution)/shard_map/all_to_all | solution.py:28
  30.0 0.0 copy-done
  30.0 0.0 copy-done.3
  30.0 0.0 copy-done.4
  30.0 7.3 %local_work.1 = (f32[1280,256]{1,0:T(8,128)S(1)}, bf16[1280,256]{1,0:T(8,128)(2,1)S(1)}, bf16[56,8,1152]{2,1,0:T(8,128)(2,1)S(1)}) custom-call(s32[1]{0:T(128)} %bitcast.who_ref, s32[1]{0:T(128)} %bitcast.1.core_ref, s32[432]{0:T(512)S(1)} %copy-done.4, bf16[56,8,1664]{2,1,0:T(8,128)(2,1)S(1)} %bitcast.23, f32[18,1152]{1,0:T(8,128)S(1)} %reshape.63.taps_ref, ...), custom_call_target="tpu_custom_call" | custom-call | tf_op jit(solution)/shard_map/local_work/pallas_call | solution.py:129
  37.3 0.0 copy-start.1
  37.4 6.0 %collective-permute-start = (bf16[1280,256]{1,0:T(8,128)(2,1)S(1)}, bf16[1280,256]{1,0:T(8,128)(2,1)S(1)}, u32[]{:S(2)}, u32[]{:S(2)}) collective-permute-start(bf16[1280,256]{1,0:T(8,128)(2,1)S(1)} %get-tuple-element.15), channel_id=1, source_target_pairs={{0,8},{8,0},{1,9},{9,1},{2,10},{10,2},{3,11},{11,3},{4,12},{12,4},... | collective-permute-start | bytes 1966088 | tf_op jit(solution)/shard_map/ppermute | solution.py:24
  43.4 1.7 %collective-permute-done = bf16[1280,256]{1,0:T(8,128)(2,1)S(1)} collective-permute-done((bf16[1280,256]{1,0:T(8,128)(2,1)S(1)}, bf16[1280,256]{1,0:T(8,128)(2,1)S(1)}, u32[]{:S(2)}, u32[]{:S(2)}) %collective-permute-start) | collective-permute-done | bytes 655392 | tf_op jit(solution)/shard_map/ppermute | solution.py:24
  45.1 0.2 add_convert_fusion
  45.3 14.7 %all_to_all.20 = bf16[16,80,256]{2,1,0:T(8,128)(2,1)S(1)} all-to-all(bf16[16,80,256]{2,1,0:T(8,128)(2,1)S(1)} %bitcast.26), channel_id=1, replica_groups=mesh['zh'=4,'zl'=4,'xl'=2,'core'=2,'y'=4,'xh'=2] {'xl','y','xh'}, dimensions={0} | all-to-all | bytes 1310720 | tf_op jit(solution)/shard_map/all_to_all | solution.py:28
  60.0 0.0 copy-done.1
  60.0 3.6 %all-to-all-start.2 = ((bf16[8,7,8,1152]{3,2,1,0:T(8,128)(2,1)}), bf16[8,7,8,1152]{3,2,1,0:T(8,128)(2,1)S(1)}, u32[]{:S(2)}, u32[]{:S(2)}) async-start(bf16[8,7,8,1152]{3,2,1,0:T(8,128)(2,1)} %bitcast.25), calls=%async_computation.2 | async-start | bytes 2064384 | tf_op jit(solution)/shard_map/all_to_all | solution.py:28
  63.6 0.1 convert_reduce_fusion
  63.7 3.7 %collective-permute-start.1 = (f32[80,256]{1,0:T(8,128)S(1)}, f32[80,256]{1,0:T(8,128)S(1)}, u32[]{:S(2)}, u32[]{:S(2)}) collective-permute-start(f32[80,256]{1,0:T(8,128)S(1)} %convert_reduce_fusion), channel_id=1, source_target_pairs={{0,32},{32,0},{64,96},{96,64},{1,33},{33,1},{65,97},{97,65},{2,34}... | collective-permute-start | bytes 245768 | tf_op jit(solution)/shard_map/ppermute | solution.py:51
  67.3 2.1 %collective-permute-done.1 = f32[80,256]{1,0:T(8,128)S(1)} collective-permute-done((f32[80,256]{1,0:T(8,128)S(1)}, f32[80,256]{1,0:T(8,128)S(1)}, u32[]{:S(2)}, u32[]{:S(2)}) %collective-permute-start.1) | collective-permute-done | bytes 81952 | tf_op jit(solution)/shard_map/ppermute | solution.py:51
  69.5 0.0 copy-start.2
  69.5 4.9 %collective-permute-start.2 = (f32[80,256]{1,0:T(8,128)S(1)}, f32[80,256]{1,0:T(8,128)S(1)}, u32[]{:S(2)}, u32[]{:S(2)}) collective-permute-start(f32[80,256]{1,0:T(8,128)S(1)} %add.23), channel_id=1, source_target_pairs={{0,64},{32,96},{64,0},{96,32},{1,65},{33,97},{65,1},{97,33},{2,66}... | collective-permute-start | bytes 245768 | tf_op jit(solution)/shard_map/ppermute | solution.py:51
  74.4 2.1 %collective-permute-done.2 = f32[80,256]{1,0:T(8,128)S(1)} collective-permute-done((f32[80,256]{1,0:T(8,128)S(1)}, f32[80,256]{1,0:T(8,128)S(1)}, u32[]{:S(2)}, u32[]{:S(2)}) %collective-permute-start.2) | collective-permute-done | bytes 81952 | tf_op jit(solution)/shard_map/ppermute | solution.py:51
  76.5 12.5 %collective-permute-start.3 = (bf16[80,256]{1,0:T(8,128)(2,1)S(1)}, bf16[80,256]{1,0:T(8,128)(2,1)S(1)}, u32[]{:S(2)}, u32[]{:S(2)}) collective-permute-start(bf16[80,256]{1,0:T(8,128)(2,1)S(1)} %add_convert_fusion.1), channel_id=1, source_target_pairs={{128,0},{160,32},{192,64},{224,96},{256,128},{288,160},{320,192},{... | collective-permute-start | bytes 122888 | tf_op jit(solution)/shard_map/ppermute | solution.py:40
  89.0 1.9 %collective-permute-start.5 = (bf16[80,256]{1,0:T(8,128)(2,1)S(1)}, bf16[80,256]{1,0:T(8,128)(2,1)S(1)}, u32[]{:S(2)}, u32[]{:S(2)}) collective-permute-start(bf16[80,256]{1,0:T(8,128)(2,1)S(1)} %add_convert_fusion.1), channel_id=1, source_target_pairs={{384,0},{416,32},{448,64},{480,96},{0,128},{32,160},{64,192},{96,2... | collective-permute-start | bytes 122888 | tf_op jit(solution)/shard_map/ppermute | solution.py:40
  91.0 0.0 collective-permute-done.3
  91.0 7.3 %collective-permute-start.4 = (bf16[80,256]{1,0:T(8,128)(2,1)S(1)}, bf16[80,256]{1,0:T(8,128)(2,1)S(1)}, u32[]{:S(2)}, u32[]{:S(2)}) collective-permute-start(bf16[80,256]{1,0:T(8,128)(2,1)S(1)} %collective-permute-done.3), channel_id=1, source_target_pairs={{128,0},{160,32},{192,64},{224,96},{256,128},{288,160},{320,192},{... | collective-permute-start | bytes 122888 | tf_op jit(solution)/shard_map/ppermute | solution.py:40
  98.3 0.0 collective-permute-done.5
  98.3 1.9 %collective-permute-done.4 = bf16[80,256]{1,0:T(8,128)(2,1)S(1)} collective-permute-done((bf16[80,256]{1,0:T(8,128)(2,1)S(1)}, bf16[80,256]{1,0:T(8,128)(2,1)S(1)}, u32[]{:S(2)}, u32[]{:S(2)}) %collective-permute-start.4) | collective-permute-done | bytes 40992 | tf_op jit(solution)/shard_map/ppermute | solution.py:40
  100.2 0.0 all-to-all-done.2
  100.2 0.9 broadcast_in_dim.10
  101.1 6.8 %all-to-all-start.3 = ((bf16[16,80,256]{2,1,0:T(8,128)(2,1)}), bf16[16,80,256]{2,1,0:T(8,128)(2,1)S(1)}, u32[]{:S(2)}, u32[]{:S(2)}) async-start(bf16[16,80,256]{2,1,0:T(8,128)(2,1)} %broadcast_in_dim.10), calls=%async_computation.3 | async-start | bytes 1310720 | tf_op jit(solution)/shard_map/all_to_all | solution.py:28
  107.9 0.0 copy-done.2
  107.9 2.1 %unpack.1 = bf16[9,48,1152]{2,1,0:T(8,128)(2,1)} custom-call(s32[1]{0:T(128)} %bitcast.who_ref, s32[432]{0:T(512)S(1)} %copy-done.2, bf16[56,8,1152]{2,1,0:T(8,128)(2,1)S(1)} %bitcast.24), custom_call_target="tpu_custom_call" | custom-call | tf_op jit(solution)/shard_map/unpack/pallas_call | solution.py:129
  110.0 7.0 %all-to-all-done.3 = bf16[16,80,256]{2,1,0:T(8,128)(2,1)S(1)} async-done(((bf16[16,80,256]{2,1,0:T(8,128)(2,1)}), bf16[16,80,256]{2,1,0:T(8,128)(2,1)S(1)}, u32[]{:S(2)}, u32[]{:S(2)}) %all-to-all-start.3) | async-done | bytes 655392 | tf_op jit(solution)/shard_map/all_to_all | solution.py:28
  117.0 8.5 %collective-permute-start.6 = (bf16[16,80,256]{2,1,0:T(8,128)(2,1)S(1)}, bf16[16,80,256]{2,1,0:T(8,128)(2,1)S(1)}, u32[]{:S(2)}, u32[]{:S(2)}) collective-permute-start(bf16[16,80,256]{2,1,0:T(8,128)(2,1)S(1)} %all-to-all-done.3), channel_id=1, source_target_pairs={{0,8},{8,0},{1,9},{9,1},{2,10},{10,2},{3,11},{11,3},{4,12},{12,4},... | collective-permute-start | bytes 1966088 | tf_op jit(solution)/shard_map/ppermute | solution.py:24
  125.5 1.7 %collective-permute-done.6 = bf16[16,80,256]{2,1,0:T(8,128)(2,1)S(1)} collective-permute-done((bf16[16,80,256]{2,1,0:T(8,128)(2,1)S(1)}, bf16[16,80,256]{2,1,0:T(8,128)(2,1)S(1)}, u32[]{:S(2)}, u32[]{:S(2)}) %collective-permute-start.6) | collective-permute-done | bytes 655392 | tf_op jit(solution)/shard_map/ppermute | solution.py:24
  127.2 0.1 select_bitcast_fusion.1
  127.3 1.1 pad_maximum_fusion
  128.4 0.1 reshape.59
  128.5 0.7 copy.21
  129.1 0.6 fusion
  (10 shorter events, 0.1 us)
Async XLA Ops:
  3.6 7.7 %copy-start.5 = (bf16[2,3,3,1152]{3,0,2,1:T(2,128)(2,1)S(1)}, bf16[2,3,3,1152]{3,0,2,1:T(2,128)(2,1)}, u32[]{:S(2)}) copy-start(bf16[2,3,3,1152]{3,0,2,1:T(2,128)(2,1)} %param.8) | copy-start | bytes 124420
  3.6 26.4 %copy-start = (bf16[2,1152,256]{2,1,0:T(8,128)(2,1)S(1)}, bf16[2,1152,256]{2,1,0:T(8,128)(2,1)}, u32[]{:S(2)}) copy-start(bf16[2,1152,256]{2,1,0:T(8,128)(2,1)} %pw_ref.1) | copy-start | bytes 3538948
  3.6 26.4 %copy-start.3 = (f32[2,256]{1,0:T(2,128)S(1)}, f32[2,256]{1,0:T(2,128)}, u32[]{:S(2)}) copy-start(f32[2,256]{1,0:T(2,128)} %pb_ref.1) | copy-start | bytes 6148
  3.6 26.4 %copy-start.4 = (s32[432]{0:T(512)S(1)}, s32[432]{0:T(512)}, u32[]{:S(2)}) copy-start(s32[432]{0:T(512)} %constant.25.clone.away_ref) | copy-start | bytes 5188
  3.6 26.4 %all-to-all-start = ((bf16[8,7,8,1664]{3,2,1,0:T(8,128)(2,1)}), bf16[8,7,8,1664]{3,2,1,0:T(8,128)(2,1)S(1)}, u32[]{:S(2)}, u32[]{:S(2)}) async-start(bf16[8,7,8,1664]{3,2,1,0:T(8,128)(2,1)} %bitcast.4), calls=%async_computation | async-start | bytes 2981888 | tf_op jit(solution)/shard_map/all_to_all | solution.py:28
  37.3 22.7 %copy-start.1 = (bf16[56,8,1152]{2,1,0:T(8,128)(2,1)}, bf16[56,8,1152]{2,1,0:T(8,128)(2,1)S(1)}, u32[]{:S(2)}) copy-start(bf16[56,8,1152]{2,1,0:T(8,128)(2,1)S(1)} %get-tuple-element.16) | copy-start | bytes 3096580
  37.4 7.8 %collective-permute-start = (bf16[1280,256]{1,0:T(8,128)(2,1)S(1)}, bf16[1280,256]{1,0:T(8,128)(2,1)S(1)}, u32[]{:S(2)}, u32[]{:S(2)}) collective-permute-start(bf16[1280,256]{1,0:T(8,128)(2,1)S(1)} %get-tuple-element.15), channel_id=1, source_target_pairs={{0,8},{8,0},{1,9},{9,1},{2,10},{10,2},{3,11},{11,3},{4,12},{12,4},... | collective-permute-start | bytes 1966088 | tf_op jit(solution)/shard_map/ppermute | solution.py:24
  60.0 40.2 %all-to-all-start.2 = ((bf16[8,7,8,1152]{3,2,1,0:T(8,128)(2,1)}), bf16[8,7,8,1152]{3,2,1,0:T(8,128)(2,1)S(1)}, u32[]{:S(2)}, u32[]{:S(2)}) async-start(bf16[8,7,8,1152]{3,2,1,0:T(8,128)(2,1)} %bitcast.25), calls=%async_computation.2 | async-start | bytes 2064384 | tf_op jit(solution)/shard_map/all_to_all | solution.py:28
  63.7 5.8 %collective-permute-start.1 = (f32[80,256]{1,0:T(8,128)S(1)}, f32[80,256]{1,0:T(8,128)S(1)}, u32[]{:S(2)}, u32[]{:S(2)}) collective-permute-start(f32[80,256]{1,0:T(8,128)S(1)} %convert_reduce_fusion), channel_id=1, source_target_pairs={{0,32},{32,0},{64,96},{96,64},{1,33},{33,1},{65,97},{97,65},{2,34}... | collective-permute-start | bytes 245768 | tf_op jit(solution)/shard_map/ppermute | solution.py:51
  69.5 38.4 %copy-start.2 = (s32[432]{0:T(512)S(1)}, s32[432]{0:T(512)}, u32[]{:S(2)}) copy-start(s32[432]{0:T(512)} %constant.24.clone.home_hbm.home_ref) | copy-start | bytes 5188
  69.5 7.0 %collective-permute-start.2 = (f32[80,256]{1,0:T(8,128)S(1)}, f32[80,256]{1,0:T(8,128)S(1)}, u32[]{:S(2)}, u32[]{:S(2)}) collective-permute-start(f32[80,256]{1,0:T(8,128)S(1)} %add.23), channel_id=1, source_target_pairs={{0,64},{32,96},{64,0},{96,32},{1,65},{33,97},{65,1},{97,33},{2,66}... | collective-permute-start | bytes 245768 | tf_op jit(solution)/shard_map/ppermute | solution.py:51
  76.5 14.4 %collective-permute-start.3 = (bf16[80,256]{1,0:T(8,128)(2,1)S(1)}, bf16[80,256]{1,0:T(8,128)(2,1)S(1)}, u32[]{:S(2)}, u32[]{:S(2)}) collective-permute-start(bf16[80,256]{1,0:T(8,128)(2,1)S(1)} %add_convert_fusion.1), channel_id=1, source_target_pairs={{128,0},{160,32},{192,64},{224,96},{256,128},{288,160},{320,192},{... | collective-permute-start | bytes 122888 | tf_op jit(solution)/shard_map/ppermute | solution.py:40
  89.0 9.3 %collective-permute-start.5 = (bf16[80,256]{1,0:T(8,128)(2,1)S(1)}, bf16[80,256]{1,0:T(8,128)(2,1)S(1)}, u32[]{:S(2)}, u32[]{:S(2)}) collective-permute-start(bf16[80,256]{1,0:T(8,128)(2,1)S(1)} %add_convert_fusion.1), channel_id=1, source_target_pairs={{384,0},{416,32},{448,64},{480,96},{0,128},{32,160},{64,192},{96,2... | collective-permute-start | bytes 122888 | tf_op jit(solution)/shard_map/ppermute | solution.py:40
  91.0 9.2 %collective-permute-start.4 = (bf16[80,256]{1,0:T(8,128)(2,1)S(1)}, bf16[80,256]{1,0:T(8,128)(2,1)S(1)}, u32[]{:S(2)}, u32[]{:S(2)}) collective-permute-start(bf16[80,256]{1,0:T(8,128)(2,1)S(1)} %collective-permute-done.3), channel_id=1, source_target_pairs={{128,0},{160,32},{192,64},{224,96},{256,128},{288,160},{320,192},{... | collective-permute-start | bytes 122888 | tf_op jit(solution)/shard_map/ppermute | solution.py:40
  101.1 15.8 %all-to-all-start.3 = ((bf16[16,80,256]{2,1,0:T(8,128)(2,1)}), bf16[16,80,256]{2,1,0:T(8,128)(2,1)S(1)}, u32[]{:S(2)}, u32[]{:S(2)}) async-start(bf16[16,80,256]{2,1,0:T(8,128)(2,1)} %broadcast_in_dim.10), calls=%async_computation.3 | async-start | bytes 1310720 | tf_op jit(solution)/shard_map/all_to_all | solution.py:28
  117.0 10.2 %collective-permute-start.6 = (bf16[16,80,256]{2,1,0:T(8,128)(2,1)S(1)}, bf16[16,80,256]{2,1,0:T(8,128)(2,1)S(1)}, u32[]{:S(2)}, u32[]{:S(2)}) collective-permute-start(bf16[16,80,256]{2,1,0:T(8,128)(2,1)S(1)} %all-to-all-done.3), channel_id=1, source_target_pairs={{0,8},{8,0},{1,9},{9,1},{2,10},{10,2},{3,11},{11,3},{4,12},{12,4},... | collective-permute-start | bytes 1966088 | tf_op jit(solution)/shard_map/ppermute | solution.py:24

commit v9 on v8

--- a/solution.py
+++ b/solution.py
@@ -48,7 +48,9 @@
 
 def sum_pair(own, apart):
     planes = lax.axis_size("zl")
-    return own + lax.ppermute(own, "zl", [(i, i ^ apart) for i in range(planes)])
+    own = own.astype(jnp.bfloat16)
+    other = lax.ppermute(own, "zl", [(i, i ^ apart) for i in range(planes)])
+    return own.astype(jnp.float32) + other.astype(jnp.float32)
 
 
 def deal_units(columns):
@@ -121,6 +123,34 @@
         return carry
 
     lax.fori_loop(0, columns, column, 0)
+
+
+def finish_body(core_ref, mine_ref, other_ref, point_ref, taps_ref, bias_ref):
+    shards, held, outputs = mine_ref.shape
+    channels = point_ref.shape[1]
+    main = channels // shards
+    per_tap = -(-channels // outputs)
+
+    def branch_out(branch, source):
+        for p in range(shards):
+            point_ref[branch, p * main : (p + 1) * main, :] = source[p, :main]
+
+        def extra(row):
+            return source[row // (held - main), main + row % (held - main)].astype(jnp.float32)
+
+        for n in range(9):
+            for c in range(per_tap):
+                width = min(outputs, channels - c * outputs)
+                row = extra(n * per_tap + c)[:width]
+                taps_ref[branch * 9 + n, c * outputs : c * outputs + width] = row.astype(taps_ref.dtype)
+        bias_ref[branch] = extra(9 * per_tap)
+
+    for first in (0, 1):
+
+        @pl.when(core_ref[0] == first)
+        def _():
+            branch_out(first, mine_ref)
+            branch_out(1 - first, other_ref)
 
 
 def on_chip(body, out_shape, scalars, arrays, scratch=(), name=None, space=pltpu.VMEM):
@@ -382,9 +412,9 @@
     terms = (kept + swap_cores(sent).astype(jnp.float32)).astype(jnp.bfloat16)
     shard = terms.shape[0] // plane
     terms = exchange(terms.reshape(plane, shard, outputs), PLANE)
+    terms = jnp.sum(terms.astype(jnp.float32), axis=0)
     fgrad, terms = lax.optimization_barrier((fgrad, terms))
     fgrad = exchange(fgrad.reshape(PEERS, SLOTS, HELD, channels), LON)
-    terms = jnp.sum(terms.astype(jnp.float32), axis=0)
     terms = sum_pair(sum_pair(terms, 1), 2)
     terms = sum_ring(terms.astype(jnp.bfloat16), lax.axis_size("zl"))
     fgrad, terms = lax.optimization_barrier((fgrad, terms))
@@ -399,14 +429,18 @@
     )[None]
     feature_grad, total = lax.optimization_barrier((feature_grad, total))
     other = swap_cores(total)
-    total = jnp.stack([jnp.where(core == 0, total, other), jnp.where(core == 0, other, total)])
-
-    main = channels // plane
-    point_grad = total[:, :, :main].reshape(point_w.shape)
-    small = total[:, :, main:].reshape(branches, -1, outputs)
-    per_tap = -(-channels // outputs)
-    depth_grad = small[:, : 9 * per_tap].reshape(branches, 9, -1)[:, :, :channels].reshape(depth_w.shape)
-    bias_grad = small[:, 9 * per_tap].astype(jnp.float32)
+    point_grad, depth_grad, bias_grad = on_chip(
+        finish_body,
+        (
+            jax.ShapeDtypeStruct(point_w.shape, act),
+            jax.ShapeDtypeStruct((branches * 9, channels), act),
+            jax.ShapeDtypeStruct(point_bias.shape, jnp.float32),
+        ),
+        (core.reshape(1),),
+        (total, other),
+        name="finish",
+    )
+    depth_grad = depth_grad.reshape(depth_w.shape)
     return (feature_grad, depth_grad, point_grad, bias_grad)
 
 

time: 130 us -> 128 us (0.985)
  Pallas kernels: 12.3 us -> 14.5 us
  other arithmetic: 2.08 us -> 0.32 us
  waiting for transfers between devices: 35.1 us -> 33.7 us
    pallas_call x3 -> x4, Pallas kernels: 12.3 us -> 14.5 us  [on_chip(): pl.pallas_call(body, out_shape=out_shape, in_specs=[smem] * len(scalars)...]
where the time goes in v9:
time: 128 us
  starting transfers between devices  61.9 us (48%)
  waiting for transfers between devices  33.7 us (26%)
  blocking collectives  14.7 us (11%)
  Pallas kernels  14.5 us (11%)
  local copies, waits for them, and re-layouts  1.67 us (1%)
    all_to_all x3, waiting for transfers between devices, exchange(): return lax.all_to_all(blocks, axes, 0, 0, tiled=True)  25.6 us
    ppermute x3, starting transfers between devices, fetch(): lax.ppermute(block, Z, [((i + ahead) % planes, i) for i in range(planes)])  20.5 us
    all_to_all x3, starting transfers between devices, exchange(): return lax.all_to_all(blocks, axes, 0, 0, tiled=True)  18.3 us
    all_to_all x1, blocking collectives, exchange(): return lax.all_to_all(blocks, axes, 0, 0, tiled=True)  14.7 us
    ppermute x2, starting transfers between devices, swap_cores(): return lax.ppermute(block, 'core', [(0, 1), (1, 0)])  14.5 us
    pallas_call x4, Pallas kernels, on_chip(): pl.pallas_call(body, out_shape=out_shape, in_specs=[smem] * len(scalars)...  14.5 us
    ppermute x2, starting transfers between devices, sum_pair(): other = lax.ppermute(own, 'zl', [(i, i ^ apart) for i in range(planes)])  8.56 us
    ppermute x2, waiting for transfers between devices, swap_cores(): return lax.ppermute(block, 'core', [(0, 1), (1, 0)])  3.4 us
  transfers between devices with their start and end apart: 10, of which 7 were waited for; matrix products, arithmetic and copies ran while one was open for 0% of the time, Pallas kernels for 2%

profile of v9, /device:TPU:1, one launch (start us, length us, event | category | flops | bytes accessed | tf_op | source)
XLA Modules:
  0.0 127.6 jit_solution(17744513318047585200)
XLA Ops:
  0.6 2.9 %pack.1 = bf16[56,8,1664]{2,1,0:T(8,128)(2,1)} custom-call(s32[1]{0:T(128)} %bitcast.who_ref, s32[432]{0:T(512)} %constant.22.clone.home_hbm.home_ref, bf16[9,48,1152]{2,1,0:T(8,128)(2,1)} %bitcast.13, bf16[9,48,512]{2,1,0:T(8,128)(2,1)} %bitcast.15), custom_call_target="tpu_custom_call" | custom-call | tf_op jit(solution)/shard_map/pack/pallas_call | solution.py:159
  3.6 0.0 copy-start.4
  3.6 0.0 copy-start
  3.6 0.0 copy-start.2
  3.6 0.0 copy-start.3
  3.6 7.6 %all-to-all-start = ((bf16[8,7,8,1664]{3,2,1,0:T(8,128)(2,1)}), bf16[8,7,8,1664]{3,2,1,0:T(8,128)(2,1)S(1)}, u32[]{:S(2)}, u32[]{:S(2)}) async-start(bf16[8,7,8,1664]{3,2,1,0:T(8,128)(2,1)} %bitcast.4), calls=%async_computation | async-start | bytes 2981888 | tf_op jit(solution)/shard_map/all_to_all | solution.py:28
  11.2 0.0 copy-done.4
  11.3 18.7 %all-to-all-done = bf16[8,7,8,1664]{3,2,1,0:T(8,128)(2,1)S(1)} async-done(((bf16[8,7,8,1664]{3,2,1,0:T(8,128)(2,1)}), bf16[8,7,8,1664]{3,2,1,0:T(8,128)(2,1)S(1)}, u32[]{:S(2)}, u32[]{:S(2)}) %all-to-all-start) | async-done | bytes 1490976 | tf_op jit(solution)/shard_map/all_to_all | solution.py:28
  30.0 0.0 copy-done
  30.0 0.0 copy-done.2
  30.0 0.0 copy-done.3
  30.0 8.3 %local_work.1 = (f32[1280,256]{1,0:T(8,128)S(1)}, bf16[1280,256]{1,0:T(8,128)(2,1)S(1)}, bf16[56,8,1152]{2,1,0:T(8,128)(2,1)}) custom-call(s32[1]{0:T(128)} %bitcast.who_ref, s32[1]{0:T(128)} %bitcast.1.core_ref, s32[432]{0:T(512)S(1)} %copy-done.3, bf16[56,8,1664]{2,1,0:T(8,128)(2,1)S(1)} %bitcast.10, f32[18,1152]{1,0:T(8,128)S(1)} %reshape.50.taps_ref, ...), custom_call_target="tpu_custom_call" | custom-call | tf_op jit(solution)/shard_map/local_work/pallas_call | solution.py:159
  38.3 6.0 %collective-permute-start = (bf16[1280,256]{1,0:T(8,128)(2,1)S(1)}, bf16[1280,256]{1,0:T(8,128)(2,1)S(1)}, u32[]{:S(2)}, u32[]{:S(2)}) collective-permute-start(bf16[1280,256]{1,0:T(8,128)(2,1)S(1)} %get-tuple-element.18), channel_id=1, source_target_pairs={{0,8},{8,0},{1,9},{9,1},{2,10},{10,2},{3,11},{11,3},{4,12},{12,4},... | collective-permute-start | bytes 1966088 | tf_op jit(solution)/shard_map/ppermute | solution.py:24
  44.4 1.7 %collective-permute-done = bf16[1280,256]{1,0:T(8,128)(2,1)S(1)} collective-permute-done((bf16[1280,256]{1,0:T(8,128)(2,1)S(1)}, bf16[1280,256]{1,0:T(8,128)(2,1)S(1)}, u32[]{:S(2)}, u32[]{:S(2)}) %collective-permute-start) | collective-permute-done | bytes 655392 | tf_op jit(solution)/shard_map/ppermute | solution.py:24
  46.1 0.2 add_convert_fusion
  46.2 14.7 %all_to_all.20 = bf16[16,80,256]{2,1,0:T(8,128)(2,1)S(1)} all-to-all(bf16[16,80,256]{2,1,0:T(8,128)(2,1)S(1)} %bitcast.12), channel_id=1, replica_groups=mesh['zh'=4,'zl'=4,'xl'=2,'core'=2,'y'=4,'xh'=2] {'xl','y','xh'}, dimensions={0} | all-to-all | bytes 1310720 | tf_op jit(solution)/shard_map/all_to_all | solution.py:28
  60.9 0.1 convert_reduce_fusion
  61.0 3.6 %all-to-all-start.2 = ((bf16[8,7,8,1152]{3,2,1,0:T(8,128)(2,1)}), bf16[8,7,8,1152]{3,2,1,0:T(8,128)(2,1)S(1)}, u32[]{:S(2)}, u32[]{:S(2)}) async-start(bf16[8,7,8,1152]{3,2,1,0:T(8,128)(2,1)} %bitcast.7), calls=%async_computation.2 | async-start | bytes 2064384 | tf_op jit(solution)/shard_map/all_to_all | solution.py:28
  64.6 0.0 copy-start.1
  64.6 3.7 %collective-permute-start.1 = (bf16[80,256]{1,0:T(8,128)(2,1)S(1)}, bf16[80,256]{1,0:T(8,128)(2,1)S(1)}, u32[]{:S(2)}, u32[]{:S(2)}) collective-permute-start(bf16[80,256]{1,0:T(8,128)(2,1)S(1)} %convert_reduce_fusion), channel_id=1, source_target_pairs={{0,32},{32,0},{64,96},{96,64},{1,33},{33,1},{65,97},{97,65},{2,34}... | collective-permute-start | bytes 122888 | tf_op jit(solution)/shard_map/ppermute | solution.py:52
  68.3 1.7 %collective-permute-done.1 = bf16[80,256]{1,0:T(8,128)(2,1)S(1)} collective-permute-done((bf16[80,256]{1,0:T(8,128)(2,1)S(1)}, bf16[80,256]{1,0:T(8,128)(2,1)S(1)}, u32[]{:S(2)}, u32[]{:S(2)}) %collective-permute-start.1) | collective-permute-done | bytes 40992 | tf_op jit(solution)/shard_map/ppermute | solution.py:52
  70.0 4.9 %collective-permute-start.2 = (bf16[80,256]{1,0:T(8,128)(2,1)S(1)}, bf16[80,256]{1,0:T(8,128)(2,1)S(1)}, u32[]{:S(2)}, u32[]{:S(2)}) collective-permute-start(bf16[80,256]{1,0:T(8,128)(2,1)S(1)} %add_convert_fusion.2), channel_id=1, source_target_pairs={{0,64},{32,96},{64,0},{96,32},{1,65},{33,97},{65,1},{97,33},{2,66}... | collective-permute-start | bytes 122888 | tf_op jit(solution)/shard_map/ppermute | solution.py:52
  74.9 1.7 %collective-permute-done.2 = bf16[80,256]{1,0:T(8,128)(2,1)S(1)} collective-permute-done((bf16[80,256]{1,0:T(8,128)(2,1)S(1)}, bf16[80,256]{1,0:T(8,128)(2,1)S(1)}, u32[]{:S(2)}, u32[]{:S(2)}) %collective-permute-start.2) | collective-permute-done | bytes 40992 | tf_op jit(solution)/shard_map/ppermute | solution.py:52
  76.6 11.3 %collective-permute-start.3 = (bf16[80,256]{1,0:T(8,128)(2,1)S(1)}, bf16[80,256]{1,0:T(8,128)(2,1)S(1)}, u32[]{:S(2)}, u32[]{:S(2)}) collective-permute-start(bf16[80,256]{1,0:T(8,128)(2,1)S(1)} %add_convert_fusion.1), channel_id=1, source_target_pairs={{128,0},{160,32},{192,64},{224,96},{256,128},{288,160},{320,192},{... | collective-permute-start | bytes 122888 | tf_op jit(solution)/shard_map/ppermute | solution.py:40
  87.9 1.9 %collective-permute-start.5 = (bf16[80,256]{1,0:T(8,128)(2,1)S(1)}, bf16[80,256]{1,0:T(8,128)(2,1)S(1)}, u32[]{:S(2)}, u32[]{:S(2)}) collective-permute-start(bf16[80,256]{1,0:T(8,128)(2,1)S(1)} %add_convert_fusion.1), channel_id=1, source_target_pairs={{384,0},{416,32},{448,64},{480,96},{0,128},{32,160},{64,192},{96,2... | collective-permute-start | bytes 122888 | tf_op jit(solution)/shard_map/ppermute | solution.py:40
  89.9 0.0 collective-permute-done.3
  89.9 7.3 %collective-permute-start.4 = (bf16[80,256]{1,0:T(8,128)(2,1)S(1)}, bf16[80,256]{1,0:T(8,128)(2,1)S(1)}, u32[]{:S(2)}, u32[]{:S(2)}) collective-permute-start(bf16[80,256]{1,0:T(8,128)(2,1)S(1)} %collective-permute-done.3), channel_id=1, source_target_pairs={{128,0},{160,32},{192,64},{224,96},{256,128},{288,160},{320,192},{... | collective-permute-start | bytes 122888 | tf_op jit(solution)/shard_map/ppermute | solution.py:40
  97.1 0.0 collective-permute-done.5
  97.2 1.4 %collective-permute-done.4 = bf16[80,256]{1,0:T(8,128)(2,1)S(1)} collective-permute-done((bf16[80,256]{1,0:T(8,128)(2,1)S(1)}, bf16[80,256]{1,0:T(8,128)(2,1)S(1)}, u32[]{:S(2)}, u32[]{:S(2)}) %collective-permute-start.4) | collective-permute-done | bytes 40992 | tf_op jit(solution)/shard_map/ppermute | solution.py:40
  98.5 0.0 all-to-all-done.2
  98.6 0.9 broadcast_in_dim.10
  99.4 7.1 %all-to-all-start.3 = ((bf16[16,80,256]{2,1,0:T(8,128)(2,1)}), bf16[16,80,256]{2,1,0:T(8,128)(2,1)S(1)}, u32[]{:S(2)}, u32[]{:S(2)}) async-start(bf16[16,80,256]{2,1,0:T(8,128)(2,1)} %broadcast_in_dim.10), calls=%async_computation.3 | async-start | bytes 1310720 | tf_op jit(solution)/shard_map/all_to_all | solution.py:28
  106.5 0.0 copy-done.1
  106.5 2.1 %unpack.1 = bf16[9,48,1152]{2,1,0:T(8,128)(2,1)} custom-call(s32[1]{0:T(128)} %bitcast.who_ref, s32[432]{0:T(512)S(1)} %copy-done.1, bf16[56,8,1152]{2,1,0:T(8,128)(2,1)S(1)} %bitcast.11), custom_call_target="tpu_custom_call" | custom-call | tf_op jit(solution)/shard_map/unpack/pallas_call | solution.py:159
  108.6 7.0 %all-to-all-done.3.mine_ref = bf16[16,80,256]{2,1,0:T(8,128)(2,1)S(1)} async-done(((bf16[16,80,256]{2,1,0:T(8,128)(2,1)}), bf16[16,80,256]{2,1,0:T(8,128)(2,1)S(1)}, u32[]{:S(2)}, u32[]{:S(2)}) %all-to-all-start.3) | async-done | bytes 655392 | tf_op jit(solution)/shard_map/all_to_all | solution.py:28
  115.6 8.5 %collective-permute-start.6 = (bf16[16,80,256]{2,1,0:T(8,128)(2,1)S(1)}, bf16[16,80,256]{2,1,0:T(8,128)(2,1)S(1)}, u32[]{:S(2)}, u32[]{:S(2)}) collective-permute-start(bf16[16,80,256]{2,1,0:T(8,128)(2,1)S(1)} %all-to-all-done.3.mine_ref), channel_id=1, source_target_pairs={{0,8},{8,0},{1,9},{9,1},{2,10},{10,2},{3,11},{11,3},{4,12},{12,4},... | collective-permute-start | bytes 1966088 | tf_op jit(solution)/shard_map/ppermute | solution.py:24
  124.1 1.7 %collective-permute-done.6.other_ref = bf16[16,80,256]{2,1,0:T(8,128)(2,1)S(1)} collective-permute-done((bf16[16,80,256]{2,1,0:T(8,128)(2,1)S(1)}, bf16[16,80,256]{2,1,0:T(8,128)(2,1)S(1)}, u32[]{:S(2)}, u32[]{:S(2)}) %collective-permute-start.6) | collective-permute-done | bytes 655392 | tf_op jit(solution)/shard_map/ppermute | solution.py:24
  125.8 1.1 finish.1
  127.0 0.7 copy.14
  (7 shorter events, 0.2 us)
Async XLA Ops:
  3.6 7.7 %copy-start.4 = (bf16[2,3,3,1152]{3,0,2,1:T(2,128)(2,1)S(1)}, bf16[2,3,3,1152]{3,0,2,1:T(2,128)(2,1)}, u32[]{:S(2)}) copy-start(bf16[2,3,3,1152]{3,0,2,1:T(2,128)(2,1)} %param.8) | copy-start | bytes 124420
  3.6 26.4 %copy-start = (bf16[2,1152,256]{2,1,0:T(8,128)(2,1)S(1)}, bf16[2,1152,256]{2,1,0:T(8,128)(2,1)}, u32[]{:S(2)}) copy-start(bf16[2,1152,256]{2,1,0:T(8,128)(2,1)} %pw_ref.1) | copy-start | bytes 3538948
  3.6 26.4 %copy-start.2 = (f32[2,256]{1,0:T(2,128)S(1)}, f32[2,256]{1,0:T(2,128)}, u32[]{:S(2)}) copy-start(f32[2,256]{1,0:T(2,128)} %pb_ref.1) | copy-start | bytes 6148
  3.6 26.4 %copy-start.3 = (s32[432]{0:T(512)S(1)}, s32[432]{0:T(512)}, u32[]{:S(2)}) copy-start(s32[432]{0:T(512)} %constant.23.clone.away_ref) | copy-start | bytes 5188
  3.6 26.4 %all-to-all-start = ((bf16[8,7,8,1664]{3,2,1,0:T(8,128)(2,1)}), bf16[8,7,8,1664]{3,2,1,0:T(8,128)(2,1)S(1)}, u32[]{:S(2)}, u32[]{:S(2)}) async-start(bf16[8,7,8,1664]{3,2,1,0:T(8,128)(2,1)} %bitcast.4), calls=%async_computation | async-start | bytes 2981888 | tf_op jit(solution)/shard_map/all_to_all | solution.py:28
  38.3 7.7 %collective-permute-start = (bf16[1280,256]{1,0:T(8,128)(2,1)S(1)}, bf16[1280,256]{1,0:T(8,128)(2,1)S(1)}, u32[]{:S(2)}, u32[]{:S(2)}) collective-permute-start(bf16[1280,256]{1,0:T(8,128)(2,1)S(1)} %get-tuple-element.18), channel_id=1, source_target_pairs={{0,8},{8,0},{1,9},{9,1},{2,10},{10,2},{3,11},{11,3},{4,12},{12,4},... | collective-permute-start | bytes 1966088 | tf_op jit(solution)/shard_map/ppermute | solution.py:24
  61.0 37.5 %all-to-all-start.2 = ((bf16[8,7,8,1152]{3,2,1,0:T(8,128)(2,1)}), bf16[8,7,8,1152]{3,2,1,0:T(8,128)(2,1)S(1)}, u32[]{:S(2)}, u32[]{:S(2)}) async-start(bf16[8,7,8,1152]{3,2,1,0:T(8,128)(2,1)} %bitcast.7), calls=%async_computation.2 | async-start | bytes 2064384 | tf_op jit(solution)/shard_map/all_to_all | solution.py:28
  64.6 41.9 %copy-start.1 = (s32[432]{0:T(512)S(1)}, s32[432]{0:T(512)}, u32[]{:S(2)}) copy-start(s32[432]{0:T(512)} %constant.22.clone.home_hbm.home_ref) | copy-start | bytes 5188
  64.6 5.3 %collective-permute-start.1 = (bf16[80,256]{1,0:T(8,128)(2,1)S(1)}, bf16[80,256]{1,0:T(8,128)(2,1)S(1)}, u32[]{:S(2)}, u32[]{:S(2)}) collective-permute-start(bf16[80,256]{1,0:T(8,128)(2,1)S(1)} %convert_reduce_fusion), channel_id=1, source_target_pairs={{0,32},{32,0},{64,96},{96,64},{1,33},{33,1},{65,97},{97,65},{2,34}... | collective-permute-start | bytes 122888 | tf_op jit(solution)/shard_map/ppermute | solution.py:52
  70.0 6.6 %collective-permute-start.2 = (bf16[80,256]{1,0:T(8,128)(2,1)S(1)}, bf16[80,256]{1,0:T(8,128)(2,1)S(1)}, u32[]{:S(2)}, u32[]{:S(2)}) collective-permute-start(bf16[80,256]{1,0:T(8,128)(2,1)S(1)} %add_convert_fusion.2), channel_id=1, source_target_pairs={{0,64},{32,96},{64,0},{96,32},{1,65},{33,97},{65,1},{97,33},{2,66}... | collective-permute-start | bytes 122888 | tf_op jit(solution)/shard_map/ppermute | solution.py:52
  76.6 13.3 %collective-permute-start.3 = (bf16[80,256]{1,0:T(8,128)(2,1)S(1)}, bf16[80,256]{1,0:T(8,128)(2,1)S(1)}, u32[]{:S(2)}, u32[]{:S(2)}) collective-permute-start(bf16[80,256]{1,0:T(8,128)(2,1)S(1)} %add_convert_fusion.1), channel_id=1, source_target_pairs={{128,0},{160,32},{192,64},{224,96},{256,128},{288,160},{320,192},{... | collective-permute-start | bytes 122888 | tf_op jit(solution)/shard_map/ppermute | solution.py:40
  87.9 9.2 %collective-permute-start.5 = (bf16[80,256]{1,0:T(8,128)(2,1)S(1)}, bf16[80,256]{1,0:T(8,128)(2,1)S(1)}, u32[]{:S(2)}, u32[]{:S(2)}) collective-permute-start(bf16[80,256]{1,0:T(8,128)(2,1)S(1)} %add_convert_fusion.1), channel_id=1, source_target_pairs={{384,0},{416,32},{448,64},{480,96},{0,128},{32,160},{64,192},{96,2... | collective-permute-start | bytes 122888 | tf_op jit(solution)/shard_map/ppermute | solution.py:40
  89.9 8.7 %collective-permute-start.4 = (bf16[80,256]{1,0:T(8,128)(2,1)S(1)}, bf16[80,256]{1,0:T(8,128)(2,1)S(1)}, u32[]{:S(2)}, u32[]{:S(2)}) collective-permute-start(bf16[80,256]{1,0:T(8,128)(2,1)S(1)} %collective-permute-done.3), channel_id=1, source_target_pairs={{128,0},{160,32},{192,64},{224,96},{256,128},{288,160},{320,192},{... | collective-permute-start | bytes 122888 | tf_op jit(solution)/shard_map/ppermute | solution.py:40
  99.4 16.1 %all-to-all-start.3 = ((bf16[16,80,256]{2,1,0:T(8,128)(2,1)}), bf16[16,80,256]{2,1,0:T(8,128)(2,1)S(1)}, u32[]{:S(2)}, u32[]{:S(2)}) async-start(bf16[16,80,256]{2,1,0:T(8,128)(2,1)} %broadcast_in_dim.10), calls=%async_computation.3 | async-start | bytes 1310720 | tf_op jit(solution)/shard_map/all_to_all | solution.py:28
  115.6 10.2 %collective-permute-start.6 = (bf16[16,80,256]{2,1,0:T(8,128)(2,1)S(1)}, bf16[16,80,256]{2,1,0:T(8,128)(2,1)S(1)}, u32[]{:S(2)}, u32[]{:S(2)}) collective-permute-start(bf16[16,80,256]{2,1,0:T(8,128)(2,1)S(1)} %all-to-all-done.3.mine_ref), channel_id=1, source_target_pairs={{0,8},{8,0},{1,9},{9,1},{2,10},{10,2},{3,11},{11,3},{4,12},{12,4},... | collective-permute-start | bytes 1966088 | tf_op jit(solution)/shard_map/ppermute | solution.py:24

commit v10 on v9

--- a/solution.py
+++ b/solution.py
@@ -142,7 +142,7 @@
             for c in range(per_tap):
                 width = min(outputs, channels - c * outputs)
                 row = extra(n * per_tap + c)[:width]
-                taps_ref[branch * 9 + n, c * outputs : c * outputs + width] = row.astype(taps_ref.dtype)
+                taps_ref[n, branch, c * outputs : c * outputs + width] = row.astype(taps_ref.dtype)
         bias_ref[branch] = extra(9 * per_tap)
 
     for first in (0, 1):
@@ -412,9 +412,9 @@
     terms = (kept + swap_cores(sent).astype(jnp.float32)).astype(jnp.bfloat16)
     shard = terms.shape[0] // plane
     terms = exchange(terms.reshape(plane, shard, outputs), PLANE)
-    terms = jnp.sum(terms.astype(jnp.float32), axis=0)
     fgrad, terms = lax.optimization_barrier((fgrad, terms))
     fgrad = exchange(fgrad.reshape(PEERS, SLOTS, HELD, channels), LON)
+    terms = jnp.sum(terms.astype(jnp.float32), axis=0)
     terms = sum_pair(sum_pair(terms, 1), 2)
     terms = sum_ring(terms.astype(jnp.bfloat16), lax.axis_size("zl"))
     fgrad, terms = lax.optimization_barrier((fgrad, terms))
@@ -433,14 +433,14 @@
         finish_body,
         (
             jax.ShapeDtypeStruct(point_w.shape, act),
-            jax.ShapeDtypeStruct((branches * 9, channels), act),
+            jax.ShapeDtypeStruct((9, branches, channels), act),
             jax.ShapeDtypeStruct(point_bias.shape, jnp.float32),
         ),
         (core.reshape(1),),
         (total, other),
         name="finish",
     )
-    depth_grad = depth_grad.reshape(depth_w.shape)
+    depth_grad = depth_grad.reshape(3, 3, branches, channels).transpose(2, 0, 1, 3)
     return (feature_grad, depth_grad, point_grad, bias_grad)
 
 

time: 128 us -> 127 us (level)
  no operation moved by 1% of the time
where the time goes in v10:
time: 127 us; the launch traced here: 126 us
  starting transfers between devices  61.8 us (49%)
  waiting for transfers between devices  33.7 us (27%)
  blocking collectives  14.7 us (12%)
  Pallas kernels  13.5 us (11%)
    all_to_all x3, waiting for transfers between devices, exchange(): return lax.all_to_all(blocks, axes, 0, 0, tiled=True)  25.6 us
    ppermute x3, starting transfers between devices, fetch(): lax.ppermute(block, Z, [((i + ahead) % planes, i) for i in range(planes)])  20.8 us
    all_to_all x3, starting transfers between devices, exchange(): return lax.all_to_all(blocks, axes, 0, 0, tiled=True)  17.9 us
    all_to_all x1, blocking collectives, exchange(): return lax.all_to_all(blocks, axes, 0, 0, tiled=True)  14.7 us
    ppermute x2, starting transfers between devices, swap_cores(): return lax.ppermute(block, 'core', [(0, 1), (1, 0)])  14.5 us
    pallas_call x4, Pallas kernels, on_chip(): pl.pallas_call(body, out_shape=out_shape, in_specs=[smem] * len(scalars)...  13.5 us
    ppermute x2, starting transfers between devices, sum_pair(): other = lax.ppermute(own, 'zl', [(i, i ^ apart) for i in range(planes)])  8.56 us
    ppermute x2, waiting for transfers between devices, swap_cores(): return lax.ppermute(block, 'core', [(0, 1), (1, 0)])  3.4 us
  transfers between devices with their start and end apart: 10, of which 7 were waited for; matrix products, arithmetic and copies ran while one was open for 0% of the time, Pallas kernels for 2%

profile of v10, /device:TPU:1, one launch (start us, length us, event | category | flops | bytes accessed | tf_op | source)
XLA Modules:
  0.0 125.9 jit_solution(3573414940990385959)
XLA Ops:
  0.6 2.9 %pack.1 = bf16[56,8,1664]{2,1,0:T(8,128)(2,1)} custom-call(s32[1]{0:T(128)} %bitcast.who_ref, s32[432]{0:T(512)} %constant.23.clone.home_hbm.home_ref, bf16[9,48,1152]{2,1,0:T(8,128)(2,1)} %bitcast.17, bf16[9,48,512]{2,1,0:T(8,128)(2,1)} %bitcast.19), custom_call_target="tpu_custom_call" | custom-call | tf_op jit(solution)/shard_map/pack/pallas_call | solution.py:159
  3.6 0.0 copy-start.5
  3.6 0.0 copy-start
  3.6 0.0 copy-start.3
  3.6 0.0 copy-start.4
  3.6 7.6 %all-to-all-start = ((bf16[8,7,8,1664]{3,2,1,0:T(8,128)(2,1)}), bf16[8,7,8,1664]{3,2,1,0:T(8,128)(2,1)S(1)}, u32[]{:S(2)}, u32[]{:S(2)}) async-start(bf16[8,7,8,1664]{3,2,1,0:T(8,128)(2,1)} %bitcast.4), calls=%async_computation | async-start | bytes 2981888 | tf_op jit(solution)/shard_map/all_to_all | solution.py:28
  11.2 0.0 copy-done.5
  11.3 18.7 %all-to-all-done = bf16[8,7,8,1664]{3,2,1,0:T(8,128)(2,1)S(1)} async-done(((bf16[8,7,8,1664]{3,2,1,0:T(8,128)(2,1)}), bf16[8,7,8,1664]{3,2,1,0:T(8,128)(2,1)S(1)}, u32[]{:S(2)}, u32[]{:S(2)}) %all-to-all-start) | async-done | bytes 1490976 | tf_op jit(solution)/shard_map/all_to_all | solution.py:28
  30.0 0.0 copy-done
  30.0 0.0 copy-done.3
  30.0 0.0 copy-done.4
  30.0 7.3 %local_work.1 = (f32[1280,256]{1,0:T(8,128)S(1)}, bf16[1280,256]{1,0:T(8,128)(2,1)S(1)}, bf16[56,8,1152]{2,1,0:T(8,128)(2,1)S(1)}) custom-call(s32[1]{0:T(128)} %bitcast.who_ref, s32[1]{0:T(128)} %bitcast.1.core_ref, s32[432]{0:T(512)S(1)} %copy-done.4, bf16[56,8,1664]{2,1,0:T(8,128)(2,1)S(1)} %bitcast.13, f32[18,1152]{1,0:T(8,128)S(1)} %reshape.50.taps_ref, ...), custom_call_target="tpu_custom_call" | custom-call | tf_op jit(solution)/shard_map/local_work/pallas_call | solution.py:159
  37.3 0.0 copy-start.1
  37.4 6.0 %collective-permute-start = (bf16[1280,256]{1,0:T(8,128)(2,1)S(1)}, bf16[1280,256]{1,0:T(8,128)(2,1)S(1)}, u32[]{:S(2)}, u32[]{:S(2)}) collective-permute-start(bf16[1280,256]{1,0:T(8,128)(2,1)S(1)} %get-tuple-element.18), channel_id=1, source_target_pairs={{0,8},{8,0},{1,9},{9,1},{2,10},{10,2},{3,11},{11,3},{4,12},{12,4},... | collective-permute-start | bytes 1966088 | tf_op jit(solution)/shard_map/ppermute | solution.py:24
  43.4 1.7 %collective-permute-done = bf16[1280,256]{1,0:T(8,128)(2,1)S(1)} collective-permute-done((bf16[1280,256]{1,0:T(8,128)(2,1)S(1)}, bf16[1280,256]{1,0:T(8,128)(2,1)S(1)}, u32[]{:S(2)}, u32[]{:S(2)}) %collective-permute-start) | collective-permute-done | bytes 655392 | tf_op jit(solution)/shard_map/ppermute | solution.py:24
  45.1 0.2 add_convert_fusion
  45.3 14.7 %all_to_all.20 = bf16[16,80,256]{2,1,0:T(8,128)(2,1)S(1)} all-to-all(bf16[16,80,256]{2,1,0:T(8,128)(2,1)S(1)} %bitcast.16), channel_id=1, replica_groups=mesh['zh'=4,'zl'=4,'xl'=2,'core'=2,'y'=4,'xh'=2] {'xl','y','xh'}, dimensions={0} | all-to-all | bytes 1310720 | tf_op jit(solution)/shard_map/all_to_all | solution.py:28
  60.0 0.0 copy-done.1
  60.0 3.6 %all-to-all-start.2 = ((bf16[8,7,8,1152]{3,2,1,0:T(8,128)(2,1)}), bf16[8,7,8,1152]{3,2,1,0:T(8,128)(2,1)S(1)}, u32[]{:S(2)}, u32[]{:S(2)}) async-start(bf16[8,7,8,1152]{3,2,1,0:T(8,128)(2,1)} %bitcast.15), calls=%async_computation.2 | async-start | bytes 2064384 | tf_op jit(solution)/shard_map/all_to_all | solution.py:28
  63.6 0.1 reduce_sum.12
  63.7 0.0 copy-start.2
  63.7 3.7 %collective-permute-start.1 = (bf16[80,256]{1,0:T(8,128)(2,1)S(1)}, bf16[80,256]{1,0:T(8,128)(2,1)S(1)}, u32[]{:S(2)}, u32[]{:S(2)}) collective-permute-start(bf16[80,256]{1,0:T(8,128)(2,1)S(1)} %reduce_sum.12), channel_id=1, source_target_pairs={{0,32},{32,0},{64,96},{96,64},{1,33},{33,1},{65,97},{97,65},{2,34}... | collective-permute-start | bytes 122888 | tf_op jit(solution)/shard_map/ppermute | solution.py:52
  67.4 1.7 %collective-permute-done.1 = bf16[80,256]{1,0:T(8,128)(2,1)S(1)} collective-permute-done((bf16[80,256]{1,0:T(8,128)(2,1)S(1)}, bf16[80,256]{1,0:T(8,128)(2,1)S(1)}, u32[]{:S(2)}, u32[]{:S(2)}) %collective-permute-start.1) | collective-permute-done | bytes 40992 | tf_op jit(solution)/shard_map/ppermute | solution.py:52
  69.0 4.9 %collective-permute-start.2 = (bf16[80,256]{1,0:T(8,128)(2,1)S(1)}, bf16[80,256]{1,0:T(8,128)(2,1)S(1)}, u32[]{:S(2)}, u32[]{:S(2)}) collective-permute-start(bf16[80,256]{1,0:T(8,128)(2,1)S(1)} %add_convert_fusion.2), channel_id=1, source_target_pairs={{0,64},{32,96},{64,0},{96,32},{1,65},{33,97},{65,1},{97,33},{2,66}... | collective-permute-start | bytes 122888 | tf_op jit(solution)/shard_map/ppermute | solution.py:52
  74.0 1.7 %collective-permute-done.2 = bf16[80,256]{1,0:T(8,128)(2,1)S(1)} collective-permute-done((bf16[80,256]{1,0:T(8,128)(2,1)S(1)}, bf16[80,256]{1,0:T(8,128)(2,1)S(1)}, u32[]{:S(2)}, u32[]{:S(2)}) %collective-permute-start.2) | collective-permute-done | bytes 40992 | tf_op jit(solution)/shard_map/ppermute | solution.py:52
  75.6 11.6 %collective-permute-start.3 = (bf16[80,256]{1,0:T(8,128)(2,1)S(1)}, bf16[80,256]{1,0:T(8,128)(2,1)S(1)}, u32[]{:S(2)}, u32[]{:S(2)}) collective-permute-start(bf16[80,256]{1,0:T(8,128)(2,1)S(1)} %add_convert_fusion.1), channel_id=1, source_target_pairs={{128,0},{160,32},{192,64},{224,96},{256,128},{288,160},{320,192},{... | collective-permute-start | bytes 122888 | tf_op jit(solution)/shard_map/ppermute | solution.py:40
  87.3 1.9 %collective-permute-start.5 = (bf16[80,256]{1,0:T(8,128)(2,1)S(1)}, bf16[80,256]{1,0:T(8,128)(2,1)S(1)}, u32[]{:S(2)}, u32[]{:S(2)}) collective-permute-start(bf16[80,256]{1,0:T(8,128)(2,1)S(1)} %add_convert_fusion.1), channel_id=1, source_target_pairs={{384,0},{416,32},{448,64},{480,96},{0,128},{32,160},{64,192},{96,2... | collective-permute-start | bytes 122888 | tf_op jit(solution)/shard_map/ppermute | solution.py:40
  89.2 0.0 collective-permute-done.3
  89.2 7.3 %collective-permute-start.4 = (bf16[80,256]{1,0:T(8,128)(2,1)S(1)}, bf16[80,256]{1,0:T(8,128)(2,1)S(1)}, u32[]{:S(2)}, u32[]{:S(2)}) collective-permute-start(bf16[80,256]{1,0:T(8,128)(2,1)S(1)} %collective-permute-done.3), channel_id=1, source_target_pairs={{128,0},{160,32},{192,64},{224,96},{256,128},{288,160},{320,192},{... | collective-permute-start | bytes 122888 | tf_op jit(solution)/shard_map/ppermute | solution.py:40
  96.5 0.0 collective-permute-done.5
  96.5 1.4 %collective-permute-done.4 = bf16[80,256]{1,0:T(8,128)(2,1)S(1)} collective-permute-done((bf16[80,256]{1,0:T(8,128)(2,1)S(1)}, bf16[80,256]{1,0:T(8,128)(2,1)S(1)}, u32[]{:S(2)}, u32[]{:S(2)}) %collective-permute-start.4) | collective-permute-done | bytes 40992 | tf_op jit(solution)/shard_map/ppermute | solution.py:40
  97.9 0.0 all-to-all-done.2
  97.9 0.9 broadcast_in_dim.10
  98.8 6.7 %all-to-all-start.3 = ((bf16[16,80,256]{2,1,0:T(8,128)(2,1)}), bf16[16,80,256]{2,1,0:T(8,128)(2,1)S(1)}, u32[]{:S(2)}, u32[]{:S(2)}) async-start(bf16[16,80,256]{2,1,0:T(8,128)(2,1)} %broadcast_in_dim.10), calls=%async_computation.3 | async-start | bytes 1310720 | tf_op jit(solution)/shard_map/all_to_all | solution.py:28
  105.5 0.0 copy-done.2
  105.5 2.1 %unpack.1 = bf16[9,48,1152]{2,1,0:T(8,128)(2,1)} custom-call(s32[1]{0:T(128)} %bitcast.who_ref, s32[432]{0:T(512)S(1)} %copy-done.2, bf16[56,8,1152]{2,1,0:T(8,128)(2,1)S(1)} %bitcast.14), custom_call_target="tpu_custom_call" | custom-call | tf_op jit(solution)/shard_map/unpack/pallas_call | solution.py:159
  107.6 7.0 %all-to-all-done.3.mine_ref = bf16[16,80,256]{2,1,0:T(8,128)(2,1)S(1)} async-done(((bf16[16,80,256]{2,1,0:T(8,128)(2,1)}), bf16[16,80,256]{2,1,0:T(8,128)(2,1)S(1)}, u32[]{:S(2)}, u32[]{:S(2)}) %all-to-all-start.3) | async-done | bytes 655392 | tf_op jit(solution)/shard_map/all_to_all | solution.py:28
  114.5 8.5 %collective-permute-start.6 = (bf16[16,80,256]{2,1,0:T(8,128)(2,1)S(1)}, bf16[16,80,256]{2,1,0:T(8,128)(2,1)S(1)}, u32[]{:S(2)}, u32[]{:S(2)}) collective-permute-start(bf16[16,80,256]{2,1,0:T(8,128)(2,1)S(1)} %all-to-all-done.3.mine_ref), channel_id=1, source_target_pairs={{0,8},{8,0},{1,9},{9,1},{2,10},{10,2},{3,11},{11,3},{4,12},{12,4},... | collective-permute-start | bytes 1966088 | tf_op jit(solution)/shard_map/ppermute | solution.py:24
  123.0 1.7 %collective-permute-done.6.other_ref = bf16[16,80,256]{2,1,0:T(8,128)(2,1)S(1)} collective-permute-done((bf16[16,80,256]{2,1,0:T(8,128)(2,1)S(1)}, bf16[16,80,256]{2,1,0:T(8,128)(2,1)S(1)}, u32[]{:S(2)}, u32[]{:S(2)}) %collective-permute-start.6) | collective-permute-done | bytes 655392 | tf_op jit(solution)/shard_map/ppermute | solution.py:24
  124.7 1.2 finish.1
  (6 shorter events, 0.1 us)
Async XLA Ops:
  3.6 7.7 %copy-start.5 = (bf16[2,3,3,1152]{3,0,2,1:T(2,128)(2,1)S(1)}, bf16[2,3,3,1152]{3,0,2,1:T(2,128)(2,1)}, u32[]{:S(2)}) copy-start(bf16[2,3,3,1152]{3,0,2,1:T(2,128)(2,1)} %param.8) | copy-start | bytes 124420
  3.6 26.4 %copy-start = (bf16[2,1152,256]{2,1,0:T(8,128)(2,1)S(1)}, bf16[2,1152,256]{2,1,0:T(8,128)(2,1)}, u32[]{:S(2)}) copy-start(bf16[2,1152,256]{2,1,0:T(8,128)(2,1)} %pw_ref.1) | copy-start | bytes 3538948
  3.6 26.4 %copy-start.3 = (f32[2,256]{1,0:T(2,128)S(1)}, f32[2,256]{1,0:T(2,128)}, u32[]{:S(2)}) copy-start(f32[2,256]{1,0:T(2,128)} %pb_ref.1) | copy-start | bytes 6148
  3.6 26.4 %copy-start.4 = (s32[432]{0:T(512)S(1)}, s32[432]{0:T(512)}, u32[]{:S(2)}) copy-start(s32[432]{0:T(512)} %constant.24.clone.away_ref) | copy-start | bytes 5188
  3.6 26.4 %all-to-all-start = ((bf16[8,7,8,1664]{3,2,1,0:T(8,128)(2,1)}), bf16[8,7,8,1664]{3,2,1,0:T(8,128)(2,1)S(1)}, u32[]{:S(2)}, u32[]{:S(2)}) async-start(bf16[8,7,8,1664]{3,2,1,0:T(8,128)(2,1)} %bitcast.4), calls=%async_computation | async-start | bytes 2981888 | tf_op jit(solution)/shard_map/all_to_all | solution.py:28
  37.3 22.7 %copy-start.1 = (bf16[56,8,1152]{2,1,0:T(8,128)(2,1)}, bf16[56,8,1152]{2,1,0:T(8,128)(2,1)S(1)}, u32[]{:S(2)}) copy-start(bf16[56,8,1152]{2,1,0:T(8,128)(2,1)S(1)} %get-tuple-element.19) | copy-start | bytes 3096580
  37.4 7.8 %collective-permute-start = (bf16[1280,256]{1,0:T(8,128)(2,1)S(1)}, bf16[1280,256]{1,0:T(8,128)(2,1)S(1)}, u32[]{:S(2)}, u32[]{:S(2)}) collective-permute-start(bf16[1280,256]{1,0:T(8,128)(2,1)S(1)} %get-tuple-element.18), channel_id=1, source_target_pairs={{0,8},{8,0},{1,9},{9,1},{2,10},{10,2},{3,11},{11,3},{4,12},{12,4},... | collective-permute-start | bytes 1966088 | tf_op jit(solution)/shard_map/ppermute | solution.py:24
  60.0 37.9 %all-to-all-start.2 = ((bf16[8,7,8,1152]{3,2,1,0:T(8,128)(2,1)}), bf16[8,7,8,1152]{3,2,1,0:T(8,128)(2,1)S(1)}, u32[]{:S(2)}, u32[]{:S(2)}) async-start(bf16[8,7,8,1152]{3,2,1,0:T(8,128)(2,1)} %bitcast.15), calls=%async_computation.2 | async-start | bytes 2064384 | tf_op jit(solution)/shard_map/all_to_all | solution.py:28
  63.7 41.8 %copy-start.2 = (s32[432]{0:T(512)S(1)}, s32[432]{0:T(512)}, u32[]{:S(2)}) copy-start(s32[432]{0:T(512)} %constant.23.clone.home_hbm.home_ref) | copy-start | bytes 5188
  63.7 5.3 %collective-permute-start.1 = (bf16[80,256]{1,0:T(8,128)(2,1)S(1)}, bf16[80,256]{1,0:T(8,128)(2,1)S(1)}, u32[]{:S(2)}, u32[]{:S(2)}) collective-permute-start(bf16[80,256]{1,0:T(8,128)(2,1)S(1)} %reduce_sum.12), channel_id=1, source_target_pairs={{0,32},{32,0},{64,96},{96,64},{1,33},{33,1},{65,97},{97,65},{2,34}... | collective-permute-start | bytes 122888 | tf_op jit(solution)/shard_map/ppermute | solution.py:52
  69.0 6.6 %collective-permute-start.2 = (bf16[80,256]{1,0:T(8,128)(2,1)S(1)}, bf16[80,256]{1,0:T(8,128)(2,1)S(1)}, u32[]{:S(2)}, u32[]{:S(2)}) collective-permute-start(bf16[80,256]{1,0:T(8,128)(2,1)S(1)} %add_convert_fusion.2), channel_id=1, source_target_pairs={{0,64},{32,96},{64,0},{96,32},{1,65},{33,97},{65,1},{97,33},{2,66}... | collective-permute-start | bytes 122888 | tf_op jit(solution)/shard_map/ppermute | solution.py:52
  75.6 13.6 %collective-permute-start.3 = (bf16[80,256]{1,0:T(8,128)(2,1)S(1)}, bf16[80,256]{1,0:T(8,128)(2,1)S(1)}, u32[]{:S(2)}, u32[]{:S(2)}) collective-permute-start(bf16[80,256]{1,0:T(8,128)(2,1)S(1)} %add_convert_fusion.1), channel_id=1, source_target_pairs={{128,0},{160,32},{192,64},{224,96},{256,128},{288,160},{320,192},{... | collective-permute-start | bytes 122888 | tf_op jit(solution)/shard_map/ppermute | solution.py:40
  87.3 9.2 %collective-permute-start.5 = (bf16[80,256]{1,0:T(8,128)(2,1)S(1)}, bf16[80,256]{1,0:T(8,128)(2,1)S(1)}, u32[]{:S(2)}, u32[]{:S(2)}) collective-permute-start(bf16[80,256]{1,0:T(8,128)(2,1)S(1)} %add_convert_fusion.1), channel_id=1, source_target_pairs={{384,0},{416,32},{448,64},{480,96},{0,128},{32,160},{64,192},{96,2... | collective-permute-start | bytes 122888 | tf_op jit(solution)/shard_map/ppermute | solution.py:40
  89.2 8.7 %collective-permute-start.4 = (bf16[80,256]{1,0:T(8,128)(2,1)S(1)}, bf16[80,256]{1,0:T(8,128)(2,1)S(1)}, u32[]{:S(2)}, u32[]{:S(2)}) collective-permute-start(bf16[80,256]{1,0:T(8,128)(2,1)S(1)} %collective-permute-done.3), channel_id=1, source_target_pairs={{128,0},{160,32},{192,64},{224,96},{256,128},{288,160},{320,192},{... | collective-permute-start | bytes 122888 | tf_op jit(solution)/shard_map/ppermute | solution.py:40
  98.8 15.7 %all-to-all-start.3 = ((bf16[16,80,256]{2,1,0:T(8,128)(2,1)}), bf16[16,80,256]{2,1,0:T(8,128)(2,1)S(1)}, u32[]{:S(2)}, u32[]{:S(2)}) async-start(bf16[16,80,256]{2,1,0:T(8,128)(2,1)} %broadcast_in_dim.10), calls=%async_computation.3 | async-start | bytes 1310720 | tf_op jit(solution)/shard_map/all_to_all | solution.py:28
  114.5 10.2 %collective-permute-start.6 = (bf16[16,80,256]{2,1,0:T(8,128)(2,1)S(1)}, bf16[16,80,256]{2,1,0:T(8,128)(2,1)S(1)}, u32[]{:S(2)}, u32[]{:S(2)}) collective-permute-start(bf16[16,80,256]{2,1,0:T(8,128)(2,1)S(1)} %all-to-all-done.3.mine_ref), channel_id=1, source_target_pairs={{0,8},{8,0},{1,9},{9,1},{2,10},{10,2},{3,11},{11,3},{4,12},{12,4},... | collective-permute-start | bytes 1966088 | tf_op jit(solution)/shard_map/ppermute | solution.py:24

commit v11 on v10

--- a/solution.py
+++ b/solution.py
@@ -412,10 +412,10 @@
     terms = (kept + swap_cores(sent).astype(jnp.float32)).astype(jnp.bfloat16)
     shard = terms.shape[0] // plane
     terms = exchange(terms.reshape(plane, shard, outputs), PLANE)
+    terms = sum_pair(jnp.sum(terms.astype(jnp.float32), axis=0), 1)
     fgrad, terms = lax.optimization_barrier((fgrad, terms))
     fgrad = exchange(fgrad.reshape(PEERS, SLOTS, HELD, channels), LON)
-    terms = jnp.sum(terms.astype(jnp.float32), axis=0)
-    terms = sum_pair(sum_pair(terms, 1), 2)
+    terms = sum_pair(terms, 2)
     terms = sum_ring(terms.astype(jnp.bfloat16), lax.axis_size("zl"))
     fgrad, terms = lax.optimization_barrier((fgrad, terms))
     total = (terms / images).astype(jnp.bfloat16)

time: 127 us -> 128 us (level)
  no operation moved by 1% of the time
where the time goes in v11:
time: 128 us; the launch traced here: 127 us
  starting transfers between devices  62.5 us (49%)
  waiting for transfers between devices  33.2 us (26%)
  blocking collectives  14.7 us (11%)
  Pallas kernels  14.5 us (11%)
    all_to_all x3, waiting for transfers between devices, exchange(): return lax.all_to_all(blocks, axes, 0, 0, tiled=True)  25.6 us
    ppermute x3, starting transfers between devices, fetch(): lax.ppermute(block, Z, [((i + ahead) % planes, i) for i in range(planes)])  20.8 us
    all_to_all x3, starting transfers between devices, exchange(): return lax.all_to_all(blocks, axes, 0, 0, tiled=True)  18.3 us
    ppermute x2, starting transfers between devices, swap_cores(): return lax.ppermute(block, 'core', [(0, 1), (1, 0)])  14.8 us
    all_to_all x1, blocking collectives, exchange(): return lax.all_to_all(blocks, axes, 0, 0, tiled=True)  14.7 us
    pallas_call x4, Pallas kernels, on_chip(): pl.pallas_call(body, out_shape=out_shape, in_specs=[smem] * len(scalars)...  14.5 us
    ppermute x2, starting transfers between devices, sum_pair(): other = lax.ppermute(own, 'zl', [(i, i ^ apart) for i in range(planes)])  8.56 us
    ppermute x2, waiting for transfers between devices, swap_cores(): return lax.ppermute(block, 'core', [(0, 1), (1, 0)])  3.4 us
  transfers between devices with their start and end apart: 10, of which 7 were waited for; matrix products, arithmetic and copies ran while one was open for 0% of the time, Pallas kernels for 2%

profile of v11, /device:TPU:1, one launch (start us, length us, event | category | flops | bytes accessed | tf_op | source)
XLA Modules:
  0.0 127.0 jit_solution(8518599138786765450)
XLA Ops:
  0.6 2.9 %pack.1 = bf16[56,8,1664]{2,1,0:T(8,128)(2,1)} custom-call(s32[1]{0:T(128)} %bitcast.who_ref, s32[432]{0:T(512)} %constant.23.clone.home_hbm.home_ref, bf16[9,48,1152]{2,1,0:T(8,128)(2,1)} %bitcast.16, bf16[9,48,512]{2,1,0:T(8,128)(2,1)} %bitcast.18), custom_call_target="tpu_custom_call" | custom-call | tf_op jit(solution)/shard_map/pack/pallas_call | solution.py:159
  3.6 0.0 copy-start.4
  3.6 0.0 copy-start
  3.6 0.0 copy-start.2
  3.6 0.0 copy-start.3
  3.6 7.6 %all-to-all-start = ((bf16[8,7,8,1664]{3,2,1,0:T(8,128)(2,1)}), bf16[8,7,8,1664]{3,2,1,0:T(8,128)(2,1)S(1)}, u32[]{:S(2)}, u32[]{:S(2)}) async-start(bf16[8,7,8,1664]{3,2,1,0:T(8,128)(2,1)} %bitcast.4), calls=%async_computation | async-start | bytes 2981888 | tf_op jit(solution)/shard_map/all_to_all | solution.py:28
  11.2 0.0 copy-done.4
  11.3 18.7 %all-to-all-done = bf16[8,7,8,1664]{3,2,1,0:T(8,128)(2,1)S(1)} async-done(((bf16[8,7,8,1664]{3,2,1,0:T(8,128)(2,1)}), bf16[8,7,8,1664]{3,2,1,0:T(8,128)(2,1)S(1)}, u32[]{:S(2)}, u32[]{:S(2)}) %all-to-all-start) | async-done | bytes 1490976 | tf_op jit(solution)/shard_map/all_to_all | solution.py:28
  30.0 0.0 copy-done
  30.0 0.0 copy-done.2
  30.0 0.0 copy-done.3
  30.0 8.3 %local_work.1 = (f32[1280,256]{1,0:T(8,128)S(1)}, bf16[1280,256]{1,0:T(8,128)(2,1)S(1)}, bf16[56,8,1152]{2,1,0:T(8,128)(2,1)}) custom-call(s32[1]{0:T(128)} %bitcast.who_ref, s32[1]{0:T(128)} %bitcast.1.core_ref, s32[432]{0:T(512)S(1)} %copy-done.3, bf16[56,8,1664]{2,1,0:T(8,128)(2,1)S(1)} %bitcast.13, f32[18,1152]{1,0:T(8,128)S(1)} %reshape.50.taps_ref, ...), custom_call_target="tpu_custom_call" | custom-call | tf_op jit(solution)/shard_map/local_work/pallas_call | solution.py:159
  38.3 6.0 %collective-permute-start = (bf16[1280,256]{1,0:T(8,128)(2,1)S(1)}, bf16[1280,256]{1,0:T(8,128)(2,1)S(1)}, u32[]{:S(2)}, u32[]{:S(2)}) collective-permute-start(bf16[1280,256]{1,0:T(8,128)(2,1)S(1)} %get-tuple-element.18), channel_id=1, source_target_pairs={{0,8},{8,0},{1,9},{9,1},{2,10},{10,2},{3,11},{11,3},{4,12},{12,4},... | collective-permute-start | bytes 1966088 | tf_op jit(solution)/shard_map/ppermute | solution.py:24
  44.4 1.7 %collective-permute-done = bf16[1280,256]{1,0:T(8,128)(2,1)S(1)} collective-permute-done((bf16[1280,256]{1,0:T(8,128)(2,1)S(1)}, bf16[1280,256]{1,0:T(8,128)(2,1)S(1)}, u32[]{:S(2)}, u32[]{:S(2)}) %collective-permute-start) | collective-permute-done | bytes 655392 | tf_op jit(solution)/shard_map/ppermute | solution.py:24
  46.1 0.2 add_convert_fusion
  46.2 14.7 %all_to_all.20 = bf16[16,80,256]{2,1,0:T(8,128)(2,1)S(1)} all-to-all(bf16[16,80,256]{2,1,0:T(8,128)(2,1)S(1)} %bitcast.15), channel_id=1, replica_groups=mesh['zh'=4,'zl'=4,'xl'=2,'core'=2,'y'=4,'xh'=2] {'xl','y','xh'}, dimensions={0} | all-to-all | bytes 1310720 | tf_op jit(solution)/shard_map/all_to_all | solution.py:28
  60.9 0.1 reduce_sum.12
  61.0 3.7 %collective-permute-start.1 = (bf16[80,256]{1,0:T(8,128)(2,1)S(1)}, bf16[80,256]{1,0:T(8,128)(2,1)S(1)}, u32[]{:S(2)}, u32[]{:S(2)}) collective-permute-start(bf16[80,256]{1,0:T(8,128)(2,1)S(1)} %reduce_sum.12), channel_id=1, source_target_pairs={{0,32},{32,0},{64,96},{96,64},{1,33},{33,1},{65,97},{97,65},{2,34}... | collective-permute-start | bytes 122888 | tf_op jit(solution)/shard_map/ppermute | solution.py:52
  64.7 1.4 %collective-permute-done.1 = bf16[80,256]{1,0:T(8,128)(2,1)S(1)} collective-permute-done((bf16[80,256]{1,0:T(8,128)(2,1)S(1)}, bf16[80,256]{1,0:T(8,128)(2,1)S(1)}, u32[]{:S(2)}, u32[]{:S(2)}) %collective-permute-start.1) | collective-permute-done | bytes 40992 | tf_op jit(solution)/shard_map/ppermute | solution.py:52
  66.1 3.6 %all-to-all-start.2 = ((bf16[8,7,8,1152]{3,2,1,0:T(8,128)(2,1)}), bf16[8,7,8,1152]{3,2,1,0:T(8,128)(2,1)S(1)}, u32[]{:S(2)}, u32[]{:S(2)}) async-start(bf16[8,7,8,1152]{3,2,1,0:T(8,128)(2,1)} %bitcast.7), calls=%async_computation.2 | async-start | bytes 2064384 | tf_op jit(solution)/shard_map/all_to_all | solution.py:28
  69.7 0.0 copy-start.1
  69.7 4.9 %collective-permute-start.2 = (bf16[80,256]{1,0:T(8,128)(2,1)S(1)}, bf16[80,256]{1,0:T(8,128)(2,1)S(1)}, u32[]{:S(2)}, u32[]{:S(2)}) collective-permute-start(bf16[80,256]{1,0:T(8,128)(2,1)S(1)} %convert_add_fusion), channel_id=1, source_target_pairs={{0,64},{32,96},{64,0},{96,32},{1,65},{33,97},{65,1},{97,33},{2,66}... | collective-permute-start | bytes 122888 | tf_op jit(solution)/shard_map/ppermute | solution.py:52
  74.6 1.4 %collective-permute-done.2 = bf16[80,256]{1,0:T(8,128)(2,1)S(1)} collective-permute-done((bf16[80,256]{1,0:T(8,128)(2,1)S(1)}, bf16[80,256]{1,0:T(8,128)(2,1)S(1)}, u32[]{:S(2)}, u32[]{:S(2)}) %collective-permute-start.2) | collective-permute-done | bytes 40992 | tf_op jit(solution)/shard_map/ppermute | solution.py:52
  76.0 11.6 %collective-permute-start.3 = (bf16[80,256]{1,0:T(8,128)(2,1)S(1)}, bf16[80,256]{1,0:T(8,128)(2,1)S(1)}, u32[]{:S(2)}, u32[]{:S(2)}) collective-permute-start(bf16[80,256]{1,0:T(8,128)(2,1)S(1)} %add_convert_fusion.1), channel_id=1, source_target_pairs={{128,0},{160,32},{192,64},{224,96},{256,128},{288,160},{320,192},{... | collective-permute-start | bytes 122888 | tf_op jit(solution)/shard_map/ppermute | solution.py:40
  87.6 1.9 %collective-permute-start.5 = (bf16[80,256]{1,0:T(8,128)(2,1)S(1)}, bf16[80,256]{1,0:T(8,128)(2,1)S(1)}, u32[]{:S(2)}, u32[]{:S(2)}) collective-permute-start(bf16[80,256]{1,0:T(8,128)(2,1)S(1)} %add_convert_fusion.1), channel_id=1, source_target_pairs={{384,0},{416,32},{448,64},{480,96},{0,128},{32,160},{64,192},{96,2... | collective-permute-start | bytes 122888 | tf_op jit(solution)/shard_map/ppermute | solution.py:40
  89.6 0.0 collective-permute-done.3
  89.6 7.3 %collective-permute-start.4 = (bf16[80,256]{1,0:T(8,128)(2,1)S(1)}, bf16[80,256]{1,0:T(8,128)(2,1)S(1)}, u32[]{:S(2)}, u32[]{:S(2)}) collective-permute-start(bf16[80,256]{1,0:T(8,128)(2,1)S(1)} %collective-permute-done.3), channel_id=1, source_target_pairs={{128,0},{160,32},{192,64},{224,96},{256,128},{288,160},{320,192},{... | collective-permute-start | bytes 122888 | tf_op jit(solution)/shard_map/ppermute | solution.py:40
  96.8 0.0 collective-permute-done.5
  96.9 1.4 %collective-permute-done.4 = bf16[80,256]{1,0:T(8,128)(2,1)S(1)} collective-permute-done((bf16[80,256]{1,0:T(8,128)(2,1)S(1)}, bf16[80,256]{1,0:T(8,128)(2,1)S(1)}, u32[]{:S(2)}, u32[]{:S(2)}) %collective-permute-start.4) | collective-permute-done | bytes 40992 | tf_op jit(solution)/shard_map/ppermute | solution.py:40
  98.3 0.0 all-to-all-done.2
  98.3 0.9 broadcast_in_dim.10
  99.2 7.1 %all-to-all-start.3 = ((bf16[16,80,256]{2,1,0:T(8,128)(2,1)}), bf16[16,80,256]{2,1,0:T(8,128)(2,1)S(1)}, u32[]{:S(2)}, u32[]{:S(2)}) async-start(bf16[16,80,256]{2,1,0:T(8,128)(2,1)} %broadcast_in_dim.10), calls=%async_computation.3 | async-start | bytes 1310720 | tf_op jit(solution)/shard_map/all_to_all | solution.py:28
  106.2 0.0 copy-done.1
  106.3 2.1 %unpack.1 = bf16[9,48,1152]{2,1,0:T(8,128)(2,1)} custom-call(s32[1]{0:T(128)} %bitcast.who_ref, s32[432]{0:T(512)S(1)} %copy-done.1, bf16[56,8,1152]{2,1,0:T(8,128)(2,1)S(1)} %bitcast.14), custom_call_target="tpu_custom_call" | custom-call | tf_op jit(solution)/shard_map/unpack/pallas_call | solution.py:159
  108.3 7.0 %all-to-all-done.3.mine_ref = bf16[16,80,256]{2,1,0:T(8,128)(2,1)S(1)} async-done(((bf16[16,80,256]{2,1,0:T(8,128)(2,1)}), bf16[16,80,256]{2,1,0:T(8,128)(2,1)S(1)}, u32[]{:S(2)}, u32[]{:S(2)}) %all-to-all-start.3) | async-done | bytes 655392 | tf_op jit(solution)/shard_map/all_to_all | solution.py:28
  115.3 8.8 %collective-permute-start.6 = (bf16[16,80,256]{2,1,0:T(8,128)(2,1)S(1)}, bf16[16,80,256]{2,1,0:T(8,128)(2,1)S(1)}, u32[]{:S(2)}, u32[]{:S(2)}) collective-permute-start(bf16[16,80,256]{2,1,0:T(8,128)(2,1)S(1)} %all-to-all-done.3.mine_ref), channel_id=1, source_target_pairs={{0,8},{8,0},{1,9},{9,1},{2,10},{10,2},{3,11},{11,3},{4,12},{12,4},... | collective-permute-start | bytes 1966088 | tf_op jit(solution)/shard_map/ppermute | solution.py:24
  124.1 1.7 %collective-permute-done.6.other_ref = bf16[16,80,256]{2,1,0:T(8,128)(2,1)S(1)} collective-permute-done((bf16[16,80,256]{2,1,0:T(8,128)(2,1)S(1)}, bf16[16,80,256]{2,1,0:T(8,128)(2,1)S(1)}, u32[]{:S(2)}, u32[]{:S(2)}) %collective-permute-start.6) | collective-permute-done | bytes 655392 | tf_op jit(solution)/shard_map/ppermute | solution.py:24
  125.8 1.2 finish.1
  (6 shorter events, 0.1 us)
Async XLA Ops:
  3.6 7.7 %copy-start.4 = (bf16[2,3,3,1152]{3,0,2,1:T(2,128)(2,1)S(1)}, bf16[2,3,3,1152]{3,0,2,1:T(2,128)(2,1)}, u32[]{:S(2)}) copy-start(bf16[2,3,3,1152]{3,0,2,1:T(2,128)(2,1)} %param.8) | copy-start | bytes 124420
  3.6 26.4 %copy-start = (bf16[2,1152,256]{2,1,0:T(8,128)(2,1)S(1)}, bf16[2,1152,256]{2,1,0:T(8,128)(2,1)}, u32[]{:S(2)}) copy-start(bf16[2,1152,256]{2,1,0:T(8,128)(2,1)} %pw_ref.1) | copy-start | bytes 3538948
  3.6 26.4 %copy-start.2 = (f32[2,256]{1,0:T(2,128)S(1)}, f32[2,256]{1,0:T(2,128)}, u32[]{:S(2)}) copy-start(f32[2,256]{1,0:T(2,128)} %pb_ref.1) | copy-start | bytes 6148
  3.6 26.4 %copy-start.3 = (s32[432]{0:T(512)S(1)}, s32[432]{0:T(512)}, u32[]{:S(2)}) copy-start(s32[432]{0:T(512)} %constant.24.clone.away_ref) | copy-start | bytes 5188
  3.6 26.4 %all-to-all-start = ((bf16[8,7,8,1664]{3,2,1,0:T(8,128)(2,1)}), bf16[8,7,8,1664]{3,2,1,0:T(8,128)(2,1)S(1)}, u32[]{:S(2)}, u32[]{:S(2)}) async-start(bf16[8,7,8,1664]{3,2,1,0:T(8,128)(2,1)} %bitcast.4), calls=%async_computation | async-start | bytes 2981888 | tf_op jit(solution)/shard_map/all_to_all | solution.py:28
  38.3 7.7 %collective-permute-start = (bf16[1280,256]{1,0:T(8,128)(2,1)S(1)}, bf16[1280,256]{1,0:T(8,128)(2,1)S(1)}, u32[]{:S(2)}, u32[]{:S(2)}) collective-permute-start(bf16[1280,256]{1,0:T(8,128)(2,1)S(1)} %get-tuple-element.18), channel_id=1, source_target_pairs={{0,8},{8,0},{1,9},{9,1},{2,10},{10,2},{3,11},{11,3},{4,12},{12,4},... | collective-permute-start | bytes 1966088 | tf_op jit(solution)/shard_map/ppermute | solution.py:24
  61.0 5.0 %collective-permute-start.1 = (bf16[80,256]{1,0:T(8,128)(2,1)S(1)}, bf16[80,256]{1,0:T(8,128)(2,1)S(1)}, u32[]{:S(2)}, u32[]{:S(2)}) collective-permute-start(bf16[80,256]{1,0:T(8,128)(2,1)S(1)} %reduce_sum.12), channel_id=1, source_target_pairs={{0,32},{32,0},{64,96},{96,64},{1,33},{33,1},{65,97},{97,65},{2,34}... | collective-permute-start | bytes 122888 | tf_op jit(solution)/shard_map/ppermute | solution.py:52
  66.1 32.2 %all-to-all-start.2 = ((bf16[8,7,8,1152]{3,2,1,0:T(8,128)(2,1)}), bf16[8,7,8,1152]{3,2,1,0:T(8,128)(2,1)S(1)}, u32[]{:S(2)}, u32[]{:S(2)}) async-start(bf16[8,7,8,1152]{3,2,1,0:T(8,128)(2,1)} %bitcast.7), calls=%async_computation.2 | async-start | bytes 2064384 | tf_op jit(solution)/shard_map/all_to_all | solution.py:28
  69.7 36.6 %copy-start.1 = (s32[432]{0:T(512)S(1)}, s32[432]{0:T(512)}, u32[]{:S(2)}) copy-start(s32[432]{0:T(512)} %constant.23.clone.home_hbm.home_ref) | copy-start | bytes 5188
  69.7 6.3 %collective-permute-start.2 = (bf16[80,256]{1,0:T(8,128)(2,1)S(1)}, bf16[80,256]{1,0:T(8,128)(2,1)S(1)}, u32[]{:S(2)}, u32[]{:S(2)}) collective-permute-start(bf16[80,256]{1,0:T(8,128)(2,1)S(1)} %convert_add_fusion), channel_id=1, source_target_pairs={{0,64},{32,96},{64,0},{96,32},{1,65},{33,97},{65,1},{97,33},{2,66}... | collective-permute-start | bytes 122888 | tf_op jit(solution)/shard_map/ppermute | solution.py:52
  76.0 13.6 %collective-permute-start.3 = (bf16[80,256]{1,0:T(8,128)(2,1)S(1)}, bf16[80,256]{1,0:T(8,128)(2,1)S(1)}, u32[]{:S(2)}, u32[]{:S(2)}) collective-permute-start(bf16[80,256]{1,0:T(8,128)(2,1)S(1)} %add_convert_fusion.1), channel_id=1, source_target_pairs={{128,0},{160,32},{192,64},{224,96},{256,128},{288,160},{320,192},{... | collective-permute-start | bytes 122888 | tf_op jit(solution)/shard_map/ppermute | solution.py:40
  87.6 9.2 %collective-permute-start.5 = (bf16[80,256]{1,0:T(8,128)(2,1)S(1)}, bf16[80,256]{1,0:T(8,128)(2,1)S(1)}, u32[]{:S(2)}, u32[]{:S(2)}) collective-permute-start(bf16[80,256]{1,0:T(8,128)(2,1)S(1)} %add_convert_fusion.1), channel_id=1, source_target_pairs={{384,0},{416,32},{448,64},{480,96},{0,128},{32,160},{64,192},{96,2... | collective-permute-start | bytes 122888 | tf_op jit(solution)/shard_map/ppermute | solution.py:40
  89.6 8.7 %collective-permute-start.4 = (bf16[80,256]{1,0:T(8,128)(2,1)S(1)}, bf16[80,256]{1,0:T(8,128)(2,1)S(1)}, u32[]{:S(2)}, u32[]{:S(2)}) collective-permute-start(bf16[80,256]{1,0:T(8,128)(2,1)S(1)} %collective-permute-done.3), channel_id=1, source_target_pairs={{128,0},{160,32},{192,64},{224,96},{256,128},{288,160},{320,192},{... | collective-permute-start | bytes 122888 | tf_op jit(solution)/shard_map/ppermute | solution.py:40
  99.2 16.1 %all-to-all-start.3 = ((bf16[16,80,256]{2,1,0:T(8,128)(2,1)}), bf16[16,80,256]{2,1,0:T(8,128)(2,1)S(1)}, u32[]{:S(2)}, u32[]{:S(2)}) async-start(bf16[16,80,256]{2,1,0:T(8,128)(2,1)} %broadcast_in_dim.10), calls=%async_computation.3 | async-start | bytes 1310720 | tf_op jit(solution)/shard_map/all_to_all | solution.py:28
  115.3 10.5 %collective-permute-start.6 = (bf16[16,80,256]{2,1,0:T(8,128)(2,1)S(1)}, bf16[16,80,256]{2,1,0:T(8,128)(2,1)S(1)}, u32[]{:S(2)}, u32[]{:S(2)}) collective-permute-start(bf16[16,80,256]{2,1,0:T(8,128)(2,1)S(1)} %all-to-all-done.3.mine_ref), channel_id=1, source_target_pairs={{0,8},{8,0},{1,9},{9,1},{2,10},{10,2},{3,11},{11,3},{4,12},{12,4},... | collective-permute-start | bytes 1966088 | tf_op jit(solution)/shard_map/ppermute | solution.py:24

commit v12 on v10

--- a/solution.py
+++ b/solution.py
@@ -415,8 +415,8 @@
     fgrad, terms = lax.optimization_barrier((fgrad, terms))
     fgrad = exchange(fgrad.reshape(PEERS, SLOTS, HELD, channels), LON)
     terms = jnp.sum(terms.astype(jnp.float32), axis=0)
-    terms = sum_pair(sum_pair(terms, 1), 2)
     terms = sum_ring(terms.astype(jnp.bfloat16), lax.axis_size("zl"))
+    terms = sum_pair(sum_pair(terms, 2), 1)
     fgrad, terms = lax.optimization_barrier((fgrad, terms))
     total = (terms / images).astype(jnp.bfloat16)
     total = gather_copies(total, PLANE)

time: 127 us -> 127 us (level)
  starting transfers between devices: 61.8 us -> 60.5 us
  waiting for transfers between devices: 33.7 us -> 35 us
    ppermute x2, starting transfers between devices: 8.56 us -> 5.75 us  [sum_pair(): other = lax.ppermute(own, 'zl', [(i, i ^ apart) for i in range(planes)])]
    ppermute x2, waiting for transfers between devices: 3.34 us -> 4.63 us  [sum_pair(): other = lax.ppermute(own, 'zl', [(i, i ^ apart) for i in range(planes)])]
where the time goes in v12:
time: 127 us; the launch traced here: 126 us
  starting transfers between devices  60.5 us (48%)
  waiting for transfers between devices  35 us (28%)
  blocking collectives  14.7 us (12%)
  Pallas kernels  13.5 us (11%)
    all_to_all x3, waiting for transfers between devices, exchange(): return lax.all_to_all(blocks, axes, 0, 0, tiled=True)  25.6 us
    ppermute x3, starting transfers between devices, fetch(): lax.ppermute(block, Z, [((i + ahead) % planes, i) for i in range(planes)])  21.8 us
    all_to_all x3, starting transfers between devices, exchange(): return lax.all_to_all(blocks, axes, 0, 0, tiled=True)  17.9 us
    ppermute x2, starting transfers between devices, swap_cores(): return lax.ppermute(block, 'core', [(0, 1), (1, 0)])  15.1 us
    all_to_all x1, blocking collectives, exchange(): return lax.all_to_all(blocks, axes, 0, 0, tiled=True)  14.7 us
    pallas_call x4, Pallas kernels, on_chip(): pl.pallas_call(body, out_shape=out_shape, in_specs=[smem] * len(scalars)...  13.5 us
    ppermute x2, starting transfers between devices, sum_pair(): other = lax.ppermute(own, 'zl', [(i, i ^ apart) for i in range(planes)])  5.75 us
    ppermute x2, waiting for transfers between devices, sum_pair(): other = lax.ppermute(own, 'zl', [(i, i ^ apart) for i in range(planes)])  4.63 us
  transfers between devices with their start and end apart: 10, of which 7 were waited for; matrix products, arithmetic and copies ran while one was open for 0% of the time, Pallas kernels for 2%

profile of v12, /device:TPU:1, one launch (start us, length us, event | category | flops | bytes accessed | tf_op | source)
XLA Modules:
  0.0 125.9 jit_solution(6673225143315220125)
XLA Ops:
  0.6 2.9 %pack.1 = bf16[56,8,1664]{2,1,0:T(8,128)(2,1)} custom-call(s32[1]{0:T(128)} %bitcast.who_ref, s32[432]{0:T(512)} %constant.23.clone.home_hbm.home_ref, bf16[9,48,1152]{2,1,0:T(8,128)(2,1)} %bitcast.17, bf16[9,48,512]{2,1,0:T(8,128)(2,1)} %bitcast.19), custom_call_target="tpu_custom_call" | custom-call | tf_op jit(solution)/shard_map/pack/pallas_call | solution.py:159
  3.6 0.0 copy-start.5
  3.6 0.0 copy-start
  3.6 0.0 copy-start.3
  3.6 0.0 copy-start.4
  3.6 7.6 %all-to-all-start = ((bf16[8,7,8,1664]{3,2,1,0:T(8,128)(2,1)}), bf16[8,7,8,1664]{3,2,1,0:T(8,128)(2,1)S(1)}, u32[]{:S(2)}, u32[]{:S(2)}) async-start(bf16[8,7,8,1664]{3,2,1,0:T(8,128)(2,1)} %bitcast.4), calls=%async_computation | async-start | bytes 2981888 | tf_op jit(solution)/shard_map/all_to_all | solution.py:28
  11.2 0.0 copy-done.5
  11.3 18.7 %all-to-all-done = bf16[8,7,8,1664]{3,2,1,0:T(8,128)(2,1)S(1)} async-done(((bf16[8,7,8,1664]{3,2,1,0:T(8,128)(2,1)}), bf16[8,7,8,1664]{3,2,1,0:T(8,128)(2,1)S(1)}, u32[]{:S(2)}, u32[]{:S(2)}) %all-to-all-start) | async-done | bytes 1490976 | tf_op jit(solution)/shard_map/all_to_all | solution.py:28
  30.0 0.0 copy-done
  30.0 0.0 copy-done.3
  30.0 0.0 copy-done.4
  30.0 7.3 %local_work.1 = (f32[1280,256]{1,0:T(8,128)S(1)}, bf16[1280,256]{1,0:T(8,128)(2,1)S(1)}, bf16[56,8,1152]{2,1,0:T(8,128)(2,1)S(1)}) custom-call(s32[1]{0:T(128)} %bitcast.who_ref, s32[1]{0:T(128)} %bitcast.1.core_ref, s32[432]{0:T(512)S(1)} %copy-done.4, bf16[56,8,1664]{2,1,0:T(8,128)(2,1)S(1)} %bitcast.13, f32[18,1152]{1,0:T(8,128)S(1)} %reshape.50.taps_ref, ...), custom_call_target="tpu_custom_call" | custom-call | tf_op jit(solution)/shard_map/local_work/pallas_call | solution.py:159
  37.3 0.0 copy-start.1
  37.4 6.0 %collective-permute-start = (bf16[1280,256]{1,0:T(8,128)(2,1)S(1)}, bf16[1280,256]{1,0:T(8,128)(2,1)S(1)}, u32[]{:S(2)}, u32[]{:S(2)}) collective-permute-start(bf16[1280,256]{1,0:T(8,128)(2,1)S(1)} %get-tuple-element.18), channel_id=1, source_target_pairs={{0,8},{8,0},{1,9},{9,1},{2,10},{10,2},{3,11},{11,3},{4,12},{12,4},... | collective-permute-start | bytes 1966088 | tf_op jit(solution)/shard_map/ppermute | solution.py:24
  43.4 1.7 %collective-permute-done = bf16[1280,256]{1,0:T(8,128)(2,1)S(1)} collective-permute-done((bf16[1280,256]{1,0:T(8,128)(2,1)S(1)}, bf16[1280,256]{1,0:T(8,128)(2,1)S(1)}, u32[]{:S(2)}, u32[]{:S(2)}) %collective-permute-start) | collective-permute-done | bytes 655392 | tf_op jit(solution)/shard_map/ppermute | solution.py:24
  45.1 0.2 add_convert_fusion
  45.3 14.7 %all_to_all.20 = bf16[16,80,256]{2,1,0:T(8,128)(2,1)S(1)} all-to-all(bf16[16,80,256]{2,1,0:T(8,128)(2,1)S(1)} %bitcast.16), channel_id=1, replica_groups=mesh['zh'=4,'zl'=4,'xl'=2,'core'=2,'y'=4,'xh'=2] {'xl','y','xh'}, dimensions={0} | all-to-all | bytes 1310720 | tf_op jit(solution)/shard_map/all_to_all | solution.py:28
  60.0 0.0 copy-done.1
  60.0 3.6 %all-to-all-start.2 = ((bf16[8,7,8,1152]{3,2,1,0:T(8,128)(2,1)}), bf16[8,7,8,1152]{3,2,1,0:T(8,128)(2,1)S(1)}, u32[]{:S(2)}, u32[]{:S(2)}) async-start(bf16[8,7,8,1152]{3,2,1,0:T(8,128)(2,1)} %bitcast.15), calls=%async_computation.2 | async-start | bytes 2064384 | tf_op jit(solution)/shard_map/all_to_all | solution.py:28
  63.6 0.1 reduce_sum.12
  63.7 0.0 copy-start.2
  63.7 12.6 %collective-permute-start.1 = (bf16[80,256]{1,0:T(8,128)(2,1)S(1)}, bf16[80,256]{1,0:T(8,128)(2,1)S(1)}, u32[]{:S(2)}, u32[]{:S(2)}) collective-permute-start(bf16[80,256]{1,0:T(8,128)(2,1)S(1)} %reduce_sum.12), channel_id=1, source_target_pairs={{128,0},{160,32},{192,64},{224,96},{256,128},{288,160},{320,192},{... | collective-permute-start | bytes 122888 | tf_op jit(solution)/shard_map/ppermute | solution.py:40
  76.3 1.9 %collective-permute-start.3 = (bf16[80,256]{1,0:T(8,128)(2,1)S(1)}, bf16[80,256]{1,0:T(8,128)(2,1)S(1)}, u32[]{:S(2)}, u32[]{:S(2)}) collective-permute-start(bf16[80,256]{1,0:T(8,128)(2,1)S(1)} %reduce_sum.12), channel_id=1, source_target_pairs={{384,0},{416,32},{448,64},{480,96},{0,128},{32,160},{64,192},{96,2... | collective-permute-start | bytes 122888 | tf_op jit(solution)/shard_map/ppermute | solution.py:40
  78.2 0.0 collective-permute-done.1
  78.2 7.3 %collective-permute-start.2 = (bf16[80,256]{1,0:T(8,128)(2,1)S(1)}, bf16[80,256]{1,0:T(8,128)(2,1)S(1)}, u32[]{:S(2)}, u32[]{:S(2)}) collective-permute-start(bf16[80,256]{1,0:T(8,128)(2,1)S(1)} %collective-permute-done.1), channel_id=1, source_target_pairs={{128,0},{160,32},{192,64},{224,96},{256,128},{288,160},{320,192},{... | collective-permute-start | bytes 122888 | tf_op jit(solution)/shard_map/ppermute | solution.py:40
  85.5 0.0 collective-permute-done.3
  85.5 1.4 %collective-permute-done.2 = bf16[80,256]{1,0:T(8,128)(2,1)S(1)} collective-permute-done((bf16[80,256]{1,0:T(8,128)(2,1)S(1)}, bf16[80,256]{1,0:T(8,128)(2,1)S(1)}, u32[]{:S(2)}, u32[]{:S(2)}) %collective-permute-start.2) | collective-permute-done | bytes 40992 | tf_op jit(solution)/shard_map/ppermute | solution.py:40
  86.9 3.1 %collective-permute-start.4 = (bf16[80,256]{1,0:T(8,128)(2,1)S(1)}, bf16[80,256]{1,0:T(8,128)(2,1)S(1)}, u32[]{:S(2)}, u32[]{:S(2)}) collective-permute-start(bf16[80,256]{1,0:T(8,128)(2,1)S(1)} %add_convert_fusion.2), channel_id=1, source_target_pairs={{0,64},{32,96},{64,0},{96,32},{1,65},{33,97},{65,1},{97,33},{2,66}... | collective-permute-start | bytes 122888 | tf_op jit(solution)/shard_map/ppermute | solution.py:52
  90.0 2.5 %collective-permute-done.4 = bf16[80,256]{1,0:T(8,128)(2,1)S(1)} collective-permute-done((bf16[80,256]{1,0:T(8,128)(2,1)S(1)}, bf16[80,256]{1,0:T(8,128)(2,1)S(1)}, u32[]{:S(2)}, u32[]{:S(2)}) %collective-permute-start.4) | collective-permute-done | bytes 40992 | tf_op jit(solution)/shard_map/ppermute | solution.py:52
  92.6 2.6 %collective-permute-start.5 = (bf16[80,256]{1,0:T(8,128)(2,1)S(1)}, bf16[80,256]{1,0:T(8,128)(2,1)S(1)}, u32[]{:S(2)}, u32[]{:S(2)}) collective-permute-start(bf16[80,256]{1,0:T(8,128)(2,1)S(1)} %add_convert_fusion.1), channel_id=1, source_target_pairs={{0,32},{32,0},{64,96},{96,64},{1,33},{33,1},{65,97},{97,65},{2,34}... | collective-permute-start | bytes 122888 | tf_op jit(solution)/shard_map/ppermute | solution.py:52
  95.2 2.1 %collective-permute-done.5 = bf16[80,256]{1,0:T(8,128)(2,1)S(1)} collective-permute-done((bf16[80,256]{1,0:T(8,128)(2,1)S(1)}, bf16[80,256]{1,0:T(8,128)(2,1)S(1)}, u32[]{:S(2)}, u32[]{:S(2)}) %collective-permute-start.5) | collective-permute-done | bytes 40992 | tf_op jit(solution)/shard_map/ppermute | solution.py:52
  97.3 0.0 all-to-all-done.2
  97.3 0.9 broadcast_in_dim.10
  98.2 6.7 %all-to-all-start.3 = ((bf16[16,80,256]{2,1,0:T(8,128)(2,1)}), bf16[16,80,256]{2,1,0:T(8,128)(2,1)S(1)}, u32[]{:S(2)}, u32[]{:S(2)}) async-start(bf16[16,80,256]{2,1,0:T(8,128)(2,1)} %broadcast_in_dim.10), calls=%async_computation.3 | async-start | bytes 1310720 | tf_op jit(solution)/shard_map/all_to_all | solution.py:28
  104.9 0.0 copy-done.2
  104.9 2.1 %unpack.1 = bf16[9,48,1152]{2,1,0:T(8,128)(2,1)} custom-call(s32[1]{0:T(128)} %bitcast.who_ref, s32[432]{0:T(512)S(1)} %copy-done.2, bf16[56,8,1152]{2,1,0:T(8,128)(2,1)S(1)} %bitcast.14), custom_call_target="tpu_custom_call" | custom-call | tf_op jit(solution)/shard_map/unpack/pallas_call | solution.py:159
  107.0 7.0 %all-to-all-done.3.mine_ref = bf16[16,80,256]{2,1,0:T(8,128)(2,1)S(1)} async-done(((bf16[16,80,256]{2,1,0:T(8,128)(2,1)}), bf16[16,80,256]{2,1,0:T(8,128)(2,1)S(1)}, u32[]{:S(2)}, u32[]{:S(2)}) %all-to-all-start.3) | async-done | bytes 655392 | tf_op jit(solution)/shard_map/all_to_all | solution.py:28
  114.0 9.1 %collective-permute-start.6 = (bf16[16,80,256]{2,1,0:T(8,128)(2,1)S(1)}, bf16[16,80,256]{2,1,0:T(8,128)(2,1)S(1)}, u32[]{:S(2)}, u32[]{:S(2)}) collective-permute-start(bf16[16,80,256]{2,1,0:T(8,128)(2,1)S(1)} %all-to-all-done.3.mine_ref), channel_id=1, source_target_pairs={{0,8},{8,0},{1,9},{9,1},{2,10},{10,2},{3,11},{11,3},{4,12},{12,4},... | collective-permute-start | bytes 1966088 | tf_op jit(solution)/shard_map/ppermute | solution.py:24
  123.0 1.7 %collective-permute-done.6.other_ref = bf16[16,80,256]{2,1,0:T(8,128)(2,1)S(1)} collective-permute-done((bf16[16,80,256]{2,1,0:T(8,128)(2,1)S(1)}, bf16[16,80,256]{2,1,0:T(8,128)(2,1)S(1)}, u32[]{:S(2)}, u32[]{:S(2)}) %collective-permute-start.6) | collective-permute-done | bytes 655392 | tf_op jit(solution)/shard_map/ppermute | solution.py:24
  124.7 1.2 finish.1
  (6 shorter events, 0.1 us)
Async XLA Ops:
  3.6 7.7 %copy-start.5 = (bf16[2,3,3,1152]{3,0,2,1:T(2,128)(2,1)S(1)}, bf16[2,3,3,1152]{3,0,2,1:T(2,128)(2,1)}, u32[]{:S(2)}) copy-start(bf16[2,3,3,1152]{3,0,2,1:T(2,128)(2,1)} %param.8) | copy-start | bytes 124420
  3.6 26.4 %copy-start = (bf16[2,1152,256]{2,1,0:T(8,128)(2,1)S(1)}, bf16[2,1152,256]{2,1,0:T(8,128)(2,1)}, u32[]{:S(2)}) copy-start(bf16[2,1152,256]{2,1,0:T(8,128)(2,1)} %pw_ref.1) | copy-start | bytes 3538948
  3.6 26.4 %copy-start.3 = (f32[2,256]{1,0:T(2,128)S(1)}, f32[2,256]{1,0:T(2,128)}, u32[]{:S(2)}) copy-start(f32[2,256]{1,0:T(2,128)} %pb_ref.1) | copy-start | bytes 6148
  3.6 26.4 %copy-start.4 = (s32[432]{0:T(512)S(1)}, s32[432]{0:T(512)}, u32[]{:S(2)}) copy-start(s32[432]{0:T(512)} %constant.24.clone.away_ref) | copy-start | bytes 5188
  3.6 26.4 %all-to-all-start = ((bf16[8,7,8,1664]{3,2,1,0:T(8,128)(2,1)}), bf16[8,7,8,1664]{3,2,1,0:T(8,128)(2,1)S(1)}, u32[]{:S(2)}, u32[]{:S(2)}) async-start(bf16[8,7,8,1664]{3,2,1,0:T(8,128)(2,1)} %bitcast.4), calls=%async_computation | async-start | bytes 2981888 | tf_op jit(solution)/shard_map/all_to_all | solution.py:28
  37.3 22.7 %copy-start.1 = (bf16[56,8,1152]{2,1,0:T(8,128)(2,1)}, bf16[56,8,1152]{2,1,0:T(8,128)(2,1)S(1)}, u32[]{:S(2)}) copy-start(bf16[56,8,1152]{2,1,0:T(8,128)(2,1)S(1)} %get-tuple-element.19) | copy-start | bytes 3096580
  37.4 7.8 %collective-permute-start = (bf16[1280,256]{1,0:T(8,128)(2,1)S(1)}, bf16[1280,256]{1,0:T(8,128)(2,1)S(1)}, u32[]{:S(2)}, u32[]{:S(2)}) collective-permute-start(bf16[1280,256]{1,0:T(8,128)(2,1)S(1)} %get-tuple-element.18), channel_id=1, source_target_pairs={{0,8},{8,0},{1,9},{9,1},{2,10},{10,2},{3,11},{11,3},{4,12},{12,4},... | collective-permute-start | bytes 1966088 | tf_op jit(solution)/shard_map/ppermute | solution.py:24
  60.0 37.3 %all-to-all-start.2 = ((bf16[8,7,8,1152]{3,2,1,0:T(8,128)(2,1)}), bf16[8,7,8,1152]{3,2,1,0:T(8,128)(2,1)S(1)}, u32[]{:S(2)}, u32[]{:S(2)}) async-start(bf16[8,7,8,1152]{3,2,1,0:T(8,128)(2,1)} %bitcast.15), calls=%async_computation.2 | async-start | bytes 2064384 | tf_op jit(solution)/shard_map/all_to_all | solution.py:28
  63.7 41.2 %copy-start.2 = (s32[432]{0:T(512)S(1)}, s32[432]{0:T(512)}, u32[]{:S(2)}) copy-start(s32[432]{0:T(512)} %constant.23.clone.home_hbm.home_ref) | copy-start | bytes 5188
  63.7 14.5 %collective-permute-start.1 = (bf16[80,256]{1,0:T(8,128)(2,1)S(1)}, bf16[80,256]{1,0:T(8,128)(2,1)S(1)}, u32[]{:S(2)}, u32[]{:S(2)}) collective-permute-start(bf16[80,256]{1,0:T(8,128)(2,1)S(1)} %reduce_sum.12), channel_id=1, source_target_pairs={{128,0},{160,32},{192,64},{224,96},{256,128},{288,160},{320,192},{... | collective-permute-start | bytes 122888 | tf_op jit(solution)/shard_map/ppermute | solution.py:40
  76.3 9.2 %collective-permute-start.3 = (bf16[80,256]{1,0:T(8,128)(2,1)S(1)}, bf16[80,256]{1,0:T(8,128)(2,1)S(1)}, u32[]{:S(2)}, u32[]{:S(2)}) collective-permute-start(bf16[80,256]{1,0:T(8,128)(2,1)S(1)} %reduce_sum.12), channel_id=1, source_target_pairs={{384,0},{416,32},{448,64},{480,96},{0,128},{32,160},{64,192},{96,2... | collective-permute-start | bytes 122888 | tf_op jit(solution)/shard_map/ppermute | solution.py:40
  78.2 8.7 %collective-permute-start.2 = (bf16[80,256]{1,0:T(8,128)(2,1)S(1)}, bf16[80,256]{1,0:T(8,128)(2,1)S(1)}, u32[]{:S(2)}, u32[]{:S(2)}) collective-permute-start(bf16[80,256]{1,0:T(8,128)(2,1)S(1)} %collective-permute-done.1), channel_id=1, source_target_pairs={{128,0},{160,32},{192,64},{224,96},{256,128},{288,160},{320,192},{... | collective-permute-start | bytes 122888 | tf_op jit(solution)/shard_map/ppermute | solution.py:40
  86.9 5.6 %collective-permute-start.4 = (bf16[80,256]{1,0:T(8,128)(2,1)S(1)}, bf16[80,256]{1,0:T(8,128)(2,1)S(1)}, u32[]{:S(2)}, u32[]{:S(2)}) collective-permute-start(bf16[80,256]{1,0:T(8,128)(2,1)S(1)} %add_convert_fusion.2), channel_id=1, source_target_pairs={{0,64},{32,96},{64,0},{96,32},{1,65},{33,97},{65,1},{97,33},{2,66}... | collective-permute-start | bytes 122888 | tf_op jit(solution)/shard_map/ppermute | solution.py:52
  92.6 4.7 %collective-permute-start.5 = (bf16[80,256]{1,0:T(8,128)(2,1)S(1)}, bf16[80,256]{1,0:T(8,128)(2,1)S(1)}, u32[]{:S(2)}, u32[]{:S(2)}) collective-permute-start(bf16[80,256]{1,0:T(8,128)(2,1)S(1)} %add_convert_fusion.1), channel_id=1, source_target_pairs={{0,32},{32,0},{64,96},{96,64},{1,33},{33,1},{65,97},{97,65},{2,34}... | collective-permute-start | bytes 122888 | tf_op jit(solution)/shard_map/ppermute | solution.py:52
  98.2 15.7 %all-to-all-start.3 = ((bf16[16,80,256]{2,1,0:T(8,128)(2,1)}), bf16[16,80,256]{2,1,0:T(8,128)(2,1)S(1)}, u32[]{:S(2)}, u32[]{:S(2)}) async-start(bf16[16,80,256]{2,1,0:T(8,128)(2,1)} %broadcast_in_dim.10), calls=%async_computation.3 | async-start | bytes 1310720 | tf_op jit(solution)/shard_map/all_to_all | solution.py:28
  114.0 10.8 %collective-permute-start.6 = (bf16[16,80,256]{2,1,0:T(8,128)(2,1)S(1)}, bf16[16,80,256]{2,1,0:T(8,128)(2,1)S(1)}, u32[]{:S(2)}, u32[]{:S(2)}) collective-permute-start(bf16[16,80,256]{2,1,0:T(8,128)(2,1)S(1)} %all-to-all-done.3.mine_ref), channel_id=1, source_target_pairs={{0,8},{8,0},{1,9},{9,1},{2,10},{10,2},{3,11},{11,3},{4,12},{12,4},... | collective-permute-start | bytes 1966088 | tf_op jit(solution)/shard_map/ppermute | solution.py:24
